TPU v7x, 32 devices: a whole 2x2x4 slice. The times are simulated.
32 devices in a mesh: groups: 2 (over x), context: 16 (over z, y, core).
Axes of the slice: x: 2, y: 2, z: 4, core: 2. Of those that a mesh axis runs over, the one named last changes fastest.
Arguments:
- encoded: bfloat16 [24576, 1536], P(('groups', 'context')), parts along dimension 0, may hold values from -64 to 64, as said below
- query_weight: bfloat16 [1536, 768], P('context'), may hold values from -0.104613624 to 0.104613624
- key_weight: bfloat16 [1536, 768], P('context'), may hold values from -4 to 4
- value_weight: bfloat16 [1536, 768], P('context'), may hold values from -0.15625 to 0.15625
- out_weight: bfloat16 [1536, 768], P('context'), may hold values from -0.875 to 0.875
- cotangent: bfloat16 [24576, 1536], P(('groups', 'context')), parts along dimension 0, may hold values from -6 to 6
- valid_frames: int32 [2], P('groups'), parts along dimension 0, may hold values from 11536 to 12288
Outputs:
- layer_out: bfloat16 [24576, 1536], P(('groups', 'context')), parts along dimension 0
- encoded_grad: bfloat16 [24576, 1536], P(('groups', 'context')), parts along dimension 0
- query_weight_grad: float32 [3072, 768], P(('groups', 'context')), parts along dimension 0
- key_weight_grad: float32 [3072, 768], P(('groups', 'context')), parts along dimension 0
- value_weight_grad: float32 [3072, 768], P(('groups', 'context')), parts along dimension 0
- out_weight_grad: float32 [3072, 768], P(('groups', 'context')), parts along dimension 0
There are 2 independent parts, one for each index of `groups`. A program takes and returns all parts, laid end to end along the dimension named above; an argument that names none is the same for every part. Nothing has to cross between parts.
Inputs may be any that keep to these rules, and one draw needn't show every extreme that they name: Frames at position valid_frames and later are padding. `encoded`: drawn afresh for each recording.
All inputs are finite; a program needn't handle non-finite values.
Results may differ from a plain program's by a relative error of at most 0.014.
The roundings to bfloat16 on the way count: a program that leaves them out, or rounds other values in their place, can miss the bound.
Values may be sent and summed in bfloat16 or wider, within the bound.
No kernel may reach another device: no remote copies, remote signals or barrier semaphores. Data moves between devices by JAX's collectives and lax.ppermute only.
A program may use at most 192 MiB of HBM per device.

v0:
```python
import jax
import jax.numpy as jnp
from jax import lax
from jax.experimental import pallas as pl
from jax.experimental.pallas import tpu as pltpu
from jax.sharding import PartitionSpec as P

HEADS = 12
HD = 64
BLOCK = 16
LEFT = 16
E = 768
SPAN = LEFT * BLOCK
HALF = SPAN // 2
PAIR = 2 * HD
SIZES = (4, 4, 4)
GROUPS = len(SIZES)
WIDTHS = tuple(HD * size for size in SIZES)
STARTS = tuple(sum(WIDTHS[:i]) for i in range(GROUPS))

epsilon = 1e-05

F32 = jnp.float32
BF16 = jnp.bfloat16

SCALE = 0.3


def hint(us):
    return pl.CostEstimate(flops=int(SCALE * us * 1.15e9), transcendentals=0, bytes_accessed=1 << 10)


def passed_along(value, axis, by):
    count = lax.axis_size(axis)
    pairs = [(i, i + by) for i in range(count) if 0 <= i + by < count]
    return lax.ppermute(value, axis, pairs)


def swapped(value, mask):
    count = lax.axis_size("context")
    return lax.ppermute(value, "context", [(i, i ^ mask) for i in range(count)])


def after(value, *others):
    return lax.optimization_barrier((value, *others))[0]


def normalize_values(values):
    centered = values - jnp.mean(values, axis=1, keepdims=True)
    inverse = lax.rsqrt(jnp.mean(centered * centered, axis=1, keepdims=True) + epsilon)
    return (centered * inverse, inverse)


def dot_nt(a, b):
    return lax.dot_general(a, b, (((1,), (1,)), ((), ())), preferred_element_type=F32)


def dot_nn(a, b):
    return lax.dot_general(a, b, (((1,), (0,)), ((), ())), preferred_element_type=F32)


def attention_body(
    pos_ref,
    q_ref,
    k_ref,
    v_ref,
    g_ref,
    o_ref,
    dq_ref,
    main_ref,
    tail_ref,
    halo_ref,
    bias_ref,
    kt_ref,
    vt_ref,
    ot_ref,
    dqt_ref,
    p_ref,
    ds_ref,
    acc_ref,
):
    rows = g_ref.shape[0]
    tiles = rows // SPAN
    first = pos_ref[0]
    count = pos_ref[1]

    @pl.when(pl.program_id(0) == 0)
    def _():
        for t in range(tiles):
            for c in range(2):
                key = lax.broadcasted_iota(jnp.int32, (SPAN + HALF, HALF), 0) + c * HALF
                query = lax.broadcasted_iota(jnp.int32, (SPAN + HALF, HALF), 1) + c * HALF
                key_block = key // BLOCK
                query_block = query // BLOCK
                pos = key + (first + (t - 1) * SPAN)
                allowed = (
                    (key_block >= query_block)
                    & (key_block <= query_block + LEFT)
                    & (pos >= 0)
                    & (pos < count)
                )
                bias_ref[t, c] = jnp.where(allowed, 0.0, -1e30)
        p_ref[...] = jnp.zeros_like(p_ref)
        ds_ref[...] = jnp.zeros_like(ds_ref)

    kt_ref[...] = k_ref[...].T
    vt_ref[...] = v_ref[...].T
    lane = lax.broadcasted_iota(jnp.int32, (SPAN, PAIR), 1)
    acc_ref[...] = jnp.zeros_like(acc_ref)

    def one_tile(t, carry):
        start = pl.multiple_of(t * SPAN, SPAN)
        qs = pl.ds(start, SPAN)
        ks = pl.ds(start, 2 * SPAN)
        q = q_ref[pl.ds(start + SPAN, SPAN), :] * BF16(HD ** (-0.5))
        g = g_ref[qs, :]
        k = k_ref[ks, :]
        v = v_ref[ks, :]
        q_heads = []
        g_heads = []
        for h in range(2):
            mine = (lane >= HD) if h else (lane < HD)
            q_heads.append(jnp.where(mine, q, jnp.zeros_like(q)))
            g_heads.append(jnp.where(mine, g, jnp.zeros_like(g)))
            s = dot_nt(k, q_heads[h])
            d = dot_nt(v, g_heads[h])
            for c in range(2):
                kr = slice(c * HALF, c * HALF + SPAN + HALF)
                qc = slice(c * HALF, (c + 1) * HALF)
                out = slice(h * SPAN + c * HALF, h * SPAN + (c + 1) * HALF)
                scores = s[kr, qc] + bias_ref[t, c]
                shifted = jnp.exp(scores - jnp.max(scores, axis=0, keepdims=True))
                probs = shifted * (1.0 / jnp.sum(shifted, axis=0, keepdims=True))
                weighted = probs * d[kr, qc]
                delta = jnp.sum(weighted, axis=0, keepdims=True)
                p_ref[kr, out] = probs.astype(BF16)
                ds_ref[kr, out] = (weighted - probs * delta).astype(BF16)
            hs = slice(h * HD, (h + 1) * HD)
            cols = slice(h * SPAN, (h + 1) * SPAN)
            ot_ref[hs, qs] = dot_nn(vt_ref[hs, ks], p_ref[:, cols])
            dqt_ref[hs, qs] = dot_nn(kt_ref[hs, ks], ds_ref[:, cols]) * HD ** (-0.5)
        acc_ref[0, ks, :] += dot_nn(ds_ref[...], jnp.concatenate(q_heads, axis=0))
        acc_ref[1, ks, :] += dot_nn(p_ref[...], jnp.concatenate(g_heads, axis=0))
        return carry

    lax.fori_loop(0, tiles, one_tile, 0, unroll=True)
    row = lax.broadcasted_iota(jnp.int32, (rows, PAIR), 0) + first
    o_ref[...] = jnp.where(row < count, ot_ref[...].T, 0.0).astype(BF16)
    dq_ref[...] = dqt_ref[...].T.astype(BF16)
    halo_ref[...] = acc_ref[:, :SPAN, :].astype(BF16)
    main_ref[...] = acc_ref[:, SPAN:rows, :].astype(BF16)
    tail_ref[...] = acc_ref[:, rows:, :]


def attention(pos, projected, grad_attn):
    rows, cols = grad_attn.shape
    ext = rows + SPAN
    steps = cols // PAIR
    sd = jax.ShapeDtypeStruct
    column = lambda part: pl.BlockSpec((ext, PAIR), lambda j: (0, part * steps + j))
    flat = pl.BlockSpec((rows, PAIR), lambda j: (0, j))
    both = lambda r: pl.BlockSpec((2, r, PAIR), lambda j: (0, 0, j))
    return pl.pallas_call(
        attention_body,
        grid=(steps,),
        in_specs=[pl.BlockSpec(memory_space=pltpu.SMEM), column(0), column(1), column(2), flat],
        out_specs=[flat, flat, both(rows - SPAN), both(SPAN), both(SPAN)],
        out_shape=[
            sd((rows, cols), BF16),
            sd((rows, cols), BF16),
            sd((2, rows - SPAN, cols), BF16),
            sd((2, SPAN, cols), F32),
            sd((2, SPAN, cols), BF16),
        ],
        scratch_shapes=[
            pltpu.VMEM((rows // SPAN, 2, SPAN + HALF, HALF), F32),
            pltpu.VMEM((PAIR, ext), BF16),
            pltpu.VMEM((PAIR, ext), BF16),
            pltpu.VMEM((PAIR, rows), F32),
            pltpu.VMEM((PAIR, rows), F32),
            pltpu.VMEM((2 * SPAN, 2 * SPAN), BF16),
            pltpu.VMEM((2 * SPAN, 2 * SPAN), BF16),
            pltpu.VMEM((2, ext, PAIR), F32),
        ],
        compiler_params=pltpu.CompilerParams(
            dimension_semantics=("arbitrary",), vmem_limit_bytes=24 << 20
        ),
        cost_estimate=hint(9.4),
    )(pos, projected, projected, projected, grad_attn)


def order_of(count):
    if count < 4 or count & (count - 1):
        raise ValueError("context size")
    far = count // 4
    return [4 * k + 2 * y + c for c in range(2) for y in range(2) for k in range(far)]


def stacked(parts):
    rows = [p.shape[0] for p in parts]

    def body(*refs):
        out_ref, sem = refs[-2:]
        copies = [
            pltpu.make_async_copy(
                ref, out_ref.at[sum(rows[:i]) : sum(rows[: i + 1]), :], sem.at[i]
            )
            for i, ref in enumerate(refs[:-2])
        ]
        for copy in copies:
            copy.start()
        for copy in copies:
            copy.wait()

    anywhere = pl.BlockSpec(memory_space=pl.ANY)
    return pl.pallas_call(
        body,
        in_specs=[anywhere] * len(parts),
        out_specs=pl.BlockSpec(memory_space=pltpu.VMEM),
        out_shape=jax.ShapeDtypeStruct((sum(rows), parts[0].shape[1]), parts[0].dtype),
        scratch_shapes=[pltpu.SemaphoreType.DMA((len(parts),))],
        compiler_params=pltpu.CompilerParams(vmem_limit_bytes=12 << 20),
        cost_estimate=hint(1.5),
    )(*parts)


def put_in_order(out_ref, flat_ref, turned_ref, value, here, order):
    rows = turned_ref.shape[0] // len(order)
    turned_ref[...] = value.T
    for j, offset in enumerate(order):
        source = pl.multiple_of((here ^ offset) * rows, rows)
        out_ref[j * rows : (j + 1) * rows, :] = turned_ref[pl.ds(source, rows), :]
    flat_ref[...] = out_ref[...].T


def prepare(me, encoded, cotangent, order):
    frames, width = encoded.shape

    def body(me_ref, own_ref, cot_ref, x_ref, c_ref, xt_ref, ct_ref, turned_ref):
        here = me_ref[0]
        normed = normalize_values(own_ref[...].astype(F32))[0].astype(BF16)
        put_in_order(xt_ref, x_ref, turned_ref, normed, here, order)
        put_in_order(ct_ref, c_ref, turned_ref, cot_ref[...], here, order)

    sd = jax.ShapeDtypeStruct
    flat = pl.BlockSpec((SPAN, width), lambda i: (i, 0))
    turned = pl.BlockSpec((width, SPAN), lambda i: (0, i))
    return pl.pallas_call(
        body,
        grid=(frames // SPAN,),
        in_specs=[pl.BlockSpec(memory_space=pltpu.SMEM), flat, flat],
        out_specs=[pl.BlockSpec((SPAN, width), lambda i: (i + 1, 0)), flat, turned, turned],
        out_shape=[
            sd((frames + SPAN, width), BF16),
            sd((frames, width), BF16),
            sd((width, frames), BF16),
            sd((width, frames), BF16),
        ],
        scratch_shapes=[pltpu.VMEM((width, SPAN), BF16)],
        compiler_params=pltpu.CompilerParams(
            dimension_semantics=("arbitrary",), vmem_limit_bytes=24 << 20
        ),
        cost_estimate=hint(6.4),
    )(me, encoded, cotangent)


def prepare_left(me, left, x, order):
    width = left.shape[1]

    def body(me_ref, left_ref, x_ref, out_ref, ordered_ref, turned_ref):
        normed = normalize_values(left_ref[...].astype(F32))[0].astype(BF16)
        put_in_order(ordered_ref, out_ref, turned_ref, normed, me_ref[0], order)

    return pl.pallas_call(
        body,
        grid=(1,),
        in_specs=[
            pl.BlockSpec(memory_space=pltpu.SMEM),
            pl.BlockSpec((SPAN, width), lambda i: (0, 0)),
            pl.BlockSpec(memory_space=pl.ANY),
        ],
        out_specs=pl.BlockSpec((SPAN, width), lambda i: (0, 0)),
        out_shape=jax.ShapeDtypeStruct(x.shape, x.dtype),
        input_output_aliases={2: 0},
        scratch_shapes=[pltpu.VMEM((width, SPAN), BF16), pltpu.VMEM((width, SPAN), BF16)],
        compiler_params=pltpu.CompilerParams(vmem_limit_bytes=12 << 20),
        cost_estimate=hint(2.0),
    )(me, left, x)


def gradients_body(
    xt_ref, ct_ref, query_ref, main_ref, tail_ref, returned_ref, mixed_ref, keep_ref, send_ref, back_ref
):
    step = pl.program_id(0)
    half = pl.num_programs(0) // 2
    rows, cols = query_ref.shape

    @pl.when(step == 0)
    def _():
        back_ref[:, :cols] = query_ref[...]
        for i in range(2):
            part = slice((i + 1) * cols, (i + 2) * cols)
            back_ref[: rows - SPAN, part] = main_ref[i]
            back_ref[rows - SPAN :, part] = (tail_ref[i] + returned_ref[i].astype(F32)).astype(BF16)

    inner = dot_nn(xt_ref[...], back_ref[...]).astype(BF16)
    outer = dot_nn(ct_ref[...], mixed_ref[...]).astype(BF16)

    @pl.when(step < half)
    def _():
        keep_ref[:, : 3 * cols] = inner
        keep_ref[:, 3 * cols :] = outer

    @pl.when(step >= half)
    def _():
        send_ref[:, : 3 * cols] = inner
        send_ref[:, 3 * cols :] = outer


def gradients(xt, ct, query_back, main, tail, returned, mixed):
    width = xt.shape[0]
    rows, cols = mixed.shape
    tile = 256
    steps = width // tile
    whole = lambda a: pl.BlockSpec(a.shape, lambda i: (0,) * a.ndim)
    sd = jax.ShapeDtypeStruct
    return pl.pallas_call(
        gradients_body,
        grid=(steps,),
        in_specs=[
            pl.BlockSpec((tile, rows), lambda i: (i, 0)),
            pl.BlockSpec((tile, rows), lambda i: (i, 0)),
            *(whole(a) for a in (query_back, main, tail, returned, mixed)),
        ],
        out_specs=[
            pl.BlockSpec((tile, 4 * cols), lambda i: (jnp.minimum(i, steps // 2 - 1), 0)),
            pl.BlockSpec((tile, 4 * cols), lambda i: (jnp.maximum(i - steps // 2, 0), 0)),
            pl.BlockSpec((rows, 3 * cols), lambda i: (0, 0)),
        ],
        out_shape=[
            sd((width // 2, 4 * cols), BF16),
            sd((width // 2, 4 * cols), BF16),
            sd((rows, 3 * cols), BF16),
        ],
        compiler_params=pltpu.CompilerParams(
            dimension_semantics=("arbitrary",), vmem_limit_bytes=24 << 20
        ),
        cost_estimate=hint(4.0),
    )(xt, ct, query_back, main, tail, returned, mixed)


def fetch(me_ref, weight_refs, held_ref, sem, parts, count):
    here = me_ref[0]
    rows = held_ref.shape[0] // count
    copies = []
    for d in range(count):
        apart = here ^ d
        j = apart % 2 * (count // 2) + apart // 2 % 2 * (count // 4) + apart // 4
        source = pl.multiple_of(j * rows, rows)
        for g, (weight_ref, (first, cols, to)) in enumerate(zip(weight_refs, parts)):
            copies.append(
                pltpu.make_async_copy(
                    weight_ref.at[pl.ds(source, rows), first : first + cols],
                    held_ref.at[d * rows : (d + 1) * rows, to : to + cols],
                    sem.at[g, d],
                )
            )
    for copy in copies:
        copy.start()
    return copies


def finish_out(me, encoded, attended, weights, count):
    frames, width = encoded.shape
    groups = len(weights)
    parts = [(3 * w, w, first) for w, first in zip(WIDTHS, STARTS)]
    tile = 256

    def body(me_ref, enc_ref, *refs):
        mixed_refs = refs[:groups]
        weight_refs = refs[groups : 2 * groups]
        out_ref, held_ref, sem = refs[2 * groups :]
        for copy in fetch(me_ref, weight_refs, held_ref, sem, parts, count):
            copy.wait()

        def one_tile(t, carry):
            part = pl.ds(pl.multiple_of(t * tile, tile), tile)
            projected = enc_ref[:, part].astype(F32)
            for mixed_ref, (_, w, first) in zip(mixed_refs, parts):
                projected = projected + dot_nt(mixed_ref[...], held_ref[part, first : first + w])
            out_ref[:, part] = projected.astype(BF16)
            return carry

        lax.fori_loop(0, width // tile, one_tile, 0)

    vmem = pl.BlockSpec(memory_space=pltpu.VMEM)
    return pl.pallas_call(
        body,
        in_specs=[
            pl.BlockSpec(memory_space=pltpu.SMEM),
            *(vmem for _ in range(1 + groups)),
            *(pl.BlockSpec(memory_space=pl.ANY) for _ in range(groups)),
        ],
        out_specs=vmem,
        out_shape=jax.ShapeDtypeStruct((frames, width), BF16),
        scratch_shapes=[
            pltpu.VMEM((width, E), BF16),
            pltpu.SemaphoreType.DMA((groups, count)),
        ],
        compiler_params=pltpu.CompilerParams(vmem_limit_bytes=24 << 20),
        cost_estimate=hint(7.0),
    )(me, encoded, *attended, *weights)


def finish_grad(me, encoded, cotangent, backs, weights, count):
    frames, width = encoded.shape
    groups = len(weights)
    parts = [(0, 3 * w, 3 * first) for w, first in zip(WIDTHS, STARTS)]
    tile = 256

    def body(me_ref, enc_ref, cot_ref, *refs):
        back_refs = refs[:groups]
        weight_refs = refs[groups : 2 * groups]
        grad_ref, held_ref, feature_ref, sem = refs[2 * groups :]
        for copy in fetch(me_ref, weight_refs, held_ref, sem, parts, count):
            copy.wait()

        def one_tile(t, carry):
            part = pl.ds(pl.multiple_of(t * tile, tile), tile)
            feature_ref[:, part] = sum(
                dot_nt(back_ref[...], held_ref[part, first : first + w])
                for back_ref, (_, w, first) in zip(back_refs, parts)
            )
            return carry

        lax.fori_loop(0, width // tile, one_tile, 0)

        def some_rows(r, carry):
            part = pl.ds(pl.multiple_of(r * 64, 64), 64)
            unit_rows, inverse = normalize_values(enc_ref[part, :].astype(F32))
            feature = feature_ref[part, :]
            centered_grad = (
                feature
                - jnp.mean(feature, axis=1, keepdims=True)
                - unit_rows * jnp.mean(feature * unit_rows, axis=1, keepdims=True)
            )
            grad_ref[part, :] = (cot_ref[part, :].astype(F32) + inverse * centered_grad).astype(BF16)
            return carry

        lax.fori_loop(0, frames // 64, some_rows, 0)

    vmem = pl.BlockSpec(memory_space=pltpu.VMEM)
    return pl.pallas_call(
        body,
        in_specs=[
            pl.BlockSpec(memory_space=pltpu.SMEM),
            *(vmem for _ in range(2 + groups)),
            *(pl.BlockSpec(memory_space=pl.ANY) for _ in range(groups)),
        ],
        out_specs=vmem,
        out_shape=jax.ShapeDtypeStruct((frames, width), BF16),
        scratch_shapes=[
            pltpu.VMEM((width, 3 * E), BF16),
            pltpu.VMEM((frames, width), F32),
            pltpu.SemaphoreType.DMA((groups, count)),
        ],
        compiler_params=pltpu.CompilerParams(vmem_limit_bytes=36 << 20),
        cost_estimate=hint(14.0),
    )(me, encoded, cotangent, *backs, *weights)


def collect(sums):
    rows = sums[0][0].shape[0]

    def body(*refs):
        outs = refs[-4:]
        at = 0
        for (_, parts), cols, first in zip(sums, WIDTHS, STARTS):
            total = refs[at][...]
            for part_ref in refs[at + 1 : at + 1 + len(parts)]:
                total = total + part_ref[...].astype(F32)
            at += 1 + len(parts)
            for k in range(4):
                outs[k][:, first : first + cols] = total[:, k * cols : (k + 1) * cols]

    flat = [a for own, parts in sums for a in (own, *parts)]
    vmem = pl.BlockSpec(memory_space=pltpu.VMEM)
    return pl.pallas_call(
        body,
        in_specs=[vmem] * len(flat),
        out_specs=[vmem] * 4,
        out_shape=[jax.ShapeDtypeStruct((rows, E), F32)] * 4,
        compiler_params=pltpu.CompilerParams(vmem_limit_bytes=16 << 20),
        cost_estimate=hint(1.2),
    )(*flat)


def shards(encoded, query_weight, key_weight, value_weight, out_weight, cotangent, valid_frames):
    valid_count = valid_frames[0]
    frames_dev = encoded.shape[0]
    count = lax.axis_size("context")
    far = count // 4
    order = order_of(count)
    index = lax.axis_index("context").astype(jnp.int32)
    first_row = index * frames_dev
    me = index[None]
    pos = jnp.stack([first_row, valid_count])
    row_mask = (first_row + jnp.arange(frames_dev, dtype=jnp.int32) < valid_count).astype(F32)[
        :, None
    ]
    left = passed_along(encoded[frames_dev - SPAN :], "context", 1)
    sources = (query_weight, key_weight, value_weight, out_weight)

    def block_of(i, sources):
        part = slice(STARTS[i], STARTS[i] + WIDTHS[i])
        return jnp.concatenate([w[:, part] for w in sources], axis=1)

    raw, near, other, weights = ([None] * GROUPS for _ in range(4))

    def gather_far(i, *gate):
        block = block_of(i, lax.optimization_barrier((*sources, *gate))[:4] if gate else sources)
        raw[i] = (block, *(swapped(block, 4 * k) for k in range(1, far)))

    def join_far(i, *gate):
        parts = after(raw[i], *gate) if gate else raw[i]
        near[i] = stacked(parts)

    def gather_next(i, *gate):
        if gate:
            near[i] = after(near[i], *gate)
        other[i] = swapped(near[i], 2)

    def gather_chip(i, *gate):
        if gate:
            other[i] = after(other[i], *gate)
        mine = stacked([near[i], other[i]])
        weights[i] = stacked([mine, swapped(mine, 1)])

    own_x, c, xt, ct = prepare(me, encoded, cotangent, order)
    gather_far(0)
    join_far(0, own_x)
    gather_next(0)
    near_sibling = swapped(near[0], 1)
    gather_far(1, near[0])
    join_far(1)
    other[0] = after(other[0], near[1], left)
    weights[0] = stacked([near[0], other[0], near_sibling, swapped(other[0], 1)])
    x = prepare_left(me, left, own_x, order)
    gather_next(1, other[0])
    gather_far(2, near[1], other[0])

    def project(i, *gate):
        whole = after(weights[i], *gate) if gate else weights[i]
        cols = WIDTHS[i]
        projected = jnp.dot(x, whole[:, : 3 * cols], preferred_element_type=F32).astype(BF16)
        grad_attn = jnp.dot(c, whole[:, 3 * cols :], preferred_element_type=F32)
        return projected, (grad_attn * row_mask).astype(BF16)

    attended, backs, keeps, sends, sums = [], [], [], [], []

    def sum_chip(i):
        total = keeps[i].astype(F32) + swapped(sends[i], 1).astype(F32)
        half = total.shape[0] // 2
        return total[:half], total[half:].astype(BF16)

    def split_far(held, got):
        total = held + got.astype(F32)
        rows = total.shape[0] // far
        return total[:rows], [total[k * rows : (k + 1) * rows].astype(BF16) for k in range(1, far)]

    held = got = own = parts = None
    for i in range(GROUPS):
        projected, grad_attn = project(i, *((keeps[i - 1], *other[i + 1 : i + 2]) if i else ()))
        if i:
            held, send = sum_chip(i - 1)
            held, send, projected = lax.optimization_barrier((held, send, projected))
            got = swapped(send, 2)
        if i > 1:
            parts, projected = lax.optimization_barrier((parts, projected))
            sums.append((own, parts))
        mixed, query_back, main, tail, halo = attention(pos, projected, grad_attn)
        attended.append(mixed)
        returned = passed_along(halo, "context", -1)
        if i + 1 < GROUPS:
            if i + 2 < GROUPS:
                join_far(i + 2, mixed)
            gather_chip(i + 1, mixed, *(near[i + 2 : i + 3]))
        if i + 2 < GROUPS:
            gather_next(i + 2, mixed, other[i + 1])
        if i:
            held, got, mixed = lax.optimization_barrier((held, got, mixed))
            own, away = split_far(held, got)
            parts = [swapped(part, 4 * k) for k, part in enumerate(away, 1)]
        keep, send, back = gradients(xt, ct, query_back, main, tail, returned, mixed)
        keeps.append(keep)
        sends.append(send)
        backs.append(back)
    held, send = sum_chip(GROUPS - 1)
    held, send, ready = lax.optimization_barrier((held, send, me))
    got = swapped(send, 2)
    layer_out = finish_out(ready, encoded, attended, weights, count)
    got, parts, layer_out = lax.optimization_barrier((got, parts, layer_out))
    sums.append((own, parts))
    own, away = split_far(held, got)
    *away, ready = lax.optimization_barrier((*away, me))
    parts = [swapped(part, 4 * k) for k, part in enumerate(away, 1)]
    encoded_grad = finish_grad(ready, encoded, cotangent, backs, weights, count)
    parts, encoded_grad = lax.optimization_barrier((parts, encoded_grad))
    sums.append((own, parts))
    return (layer_out, encoded_grad, *collect(sums))


def solution(mesh):
    placed = (
        P(("groups", "context"), None),
        P("context", None),
        P("context", None),
        P("context", None),
        P("context", None),
        P(("groups", "context"), None),
        P("groups"),
    )
    return jax.shard_map(
        shards,
        mesh=mesh,
        in_specs=placed,
        out_specs=(P(("groups", "context"), None),) * 6,
        check_vma=False,
    )
```

profile of v0, /device:TPU:0, one launch (start us, length us, event | category | flops | bytes accessed | tf_op | source)
XLA Modules:
  0.0 227.9 jit_solution(9946135511808179965)
XLA Ops:
  0.6 0.8 slice.124
  1.4 0.8 slice.125
  2.2 0.8 slice.126
  3.0 0.8 slice.127
  3.9 5.1 %collective-permute-start.3 = (bf16[96,1024]{1,0:T(8,128)(2,1)S(1)}, bf16[96,1024]{1,0:T(8,128)(2,1)S(1)}, u32[]{:S(2)}, u32[]{:S(2)}) collective-permute-start(bf16[96,1024]{1,0:T(8,128)(2,1)S(1)} %pad_maximum_fusion.refs_0_), channel_id=1, source_target_pairs={{0,12},{1,13},{2,14},{3,15},{4,8},{5,9},{6,10},{7,11},{8,4},{9,5},... | collective-permute-start | bytes 589832 | tf_op jit(solution)/shard_map/ppermute | solution.py:41
  9.6 2.1 slice.123
  11.7 2.2 collective-permute-start
  13.9 1.7 copy-done.2
  15.5 1.7 copy-done.8
  17.2 4.7 %shard_map.118 = (bf16[1024,1536]{1,0:T(8,128)(2,1)S(1)}, bf16[768,1536]{1,0:T(8,128)(2,1)S(1)}, bf16[1536,768]{1,0:T(8,128)(2,1)S(1)}, bf16[1536,768]{1,0:T(8,128)(2,1)S(1)}) custom-call(s32[1]{0:T(128)} %bitcast.me_ref, bf16[768,1536]{1,0:T(8,128)(2,1)S(1)} %copy-done.2, bf16[768,1536]{1,0:T(8,128)(2,1)S(1)} %copy-done.8), custom_call_target="tpu_custom_call" | custom-call | flops 2208000000 | bytes 1024 | tf_op jit(solution)/shard_map/pallas_call | solution.py:248
  21.9 1.4 copy-done
  23.3 1.6 copy-done.4
  24.9 1.4 copy-done.16
  27.7 0.9 copy-done.13
  28.6 0.9 copy-done.15
  29.5 1.0 shard_map.120.refs_0_
  30.6 1.5 collective-permute-start.4
  32.1 3.7 %collective-permute-start.7 = (bf16[96,1024]{1,0:T(8,128)(2,1)S(1)}, bf16[96,1024]{1,0:T(8,128)(2,1)S(1)}, u32[]{:S(2)}, u32[]{:S(2)}) collective-permute-start(bf16[96,1024]{1,0:T(8,128)(2,1)S(1)} %pad_maximum_fusion.1.refs_0_), channel_id=1, source_target_pairs={{0,12},{1,13},{2,14},{3,15},{4,8},{5,9},{6,10},{7,11},{8,4},{9,5},... | collective-permute-start | bytes 589832 | tf_op jit(solution)/shard_map/ppermute | solution.py:41
  36.5 5.3 %collective-permute-done.7.refs_3_ = bf16[96,1024]{1,0:T(8,128)(2,1)S(1)} collective-permute-done((bf16[96,1024]{1,0:T(8,128)(2,1)S(1)}, bf16[96,1024]{1,0:T(8,128)(2,1)S(1)}, u32[]{:S(2)}, u32[]{:S(2)}) %collective-permute-start.7) | collective-permute-done | bytes 196640 | tf_op jit(solution)/shard_map/ppermute | solution.py:41
  41.9 10.9 %collective-permute-done.6.refs_2_ = bf16[96,1024]{1,0:T(8,128)(2,1)S(1)} collective-permute-done((bf16[96,1024]{1,0:T(8,128)(2,1)S(1)}, bf16[96,1024]{1,0:T(8,128)(2,1)S(1)}, u32[]{:S(2)}, u32[]{:S(2)}) %collective-permute-start.6) | collective-permute-done | bytes 196640 | tf_op jit(solution)/shard_map/ppermute | solution.py:41
  52.8 1.0 shard_map.121.refs_0_
  53.8 0.9 copy-done.10
  55.8 1.9 copy-done.5
  57.7 2.1 shard_map.119
  59.8 1.6 copy-done.6
  61.5 2.4 %collective-permute-start.15 = (bf16[96,1024]{1,0:T(8,128)(2,1)S(1)}, bf16[96,1024]{1,0:T(8,128)(2,1)S(1)}, u32[]{:S(2)}, u32[]{:S(2)}) collective-permute-start(bf16[96,1024]{1,0:T(8,128)(2,1)S(1)} %pad_maximum_fusion.2.refs_0_), channel_id=1, source_target_pairs={{0,12},{1,13},{2,14},{3,15},{4,8},{5,9},{6,10},{7,11},{8,4},{9,5},... | collective-permute-start | bytes 589832 | tf_op jit(solution)/shard_map/ppermute | solution.py:41
  63.9 2.0 collective-permute-start.13
  66.5 1.7 shard_map.122.refs_3_
  68.2 2.6 %fusion.12.q_ref.k_ref.v_ref = bf16[1024,768]{1,0:T(8,128)(2,1)S(1)} fusion(bf16[1024,1536]{1,0:T(8,128)(2,1)S(1)} %copy-done.7, bf16[1536,1024]{1,0:T(8,128)(2,1)S(1)} %shard_map.122.refs_3_), kind=kOutput, calls=%fused_computation.11 | convolution fusion | flops 2416705536 | bytes 7077888 | tf_op jit(solution)/shard_map/dot_general | solution.py:555
  71.7 9.4 %shard_map.123 = (bf16[768,256]{1,0:T(8,128)(2,1)S(1)}, bf16[768,256]{1,0:T(8,128)(2,1)S(1)}, bf16[2,512,256]{2,1,0:T(8,128)(2,1)S(1)}, f32[2,256,256]{2,1,0:T(8,128)S(1)}, bf16[2,256,256]{2,1,0:T(8,128)(2,1)S(1)}) custom-call(s32[2]{0:T(128)S(1)} %pad_add_fusion.pos_ref, bf16[1024,768]{1,0:T(8,128)(2,1)S(1)} %fusion.12.q_ref.k_ref.v_ref, ...), custom_call_target="tpu_custom_call" | custom-call | flops 3243000064 | bytes 1024 | tf_op jit(solution)/shard_map/pallas_call | solution.py:163
  81.1 1.1 shard_map.125.refs_0_
  82.2 2.6 %collective-permute-done.12.refs_1_ = bf16[384,1024]{1,0:T(8,128)(2,1)S(1)} collective-permute-done((bf16[384,1024]{1,0:T(8,128)(2,1)S(1)}, bf16[384,1024]{1,0:T(8,128)(2,1)S(1)}, u32[]{:S(2)}, u32[]{:S(2)}) %collective-permute-start.12) | collective-permute-done | bytes 786464 | tf_op jit(solution)/shard_map/ppermute | solution.py:41
  85.0 1.5 collective-permute-start.10
  86.4 2.8 %collective-permute-start.17 = (bf16[384,1024]{1,0:T(8,128)(2,1)S(1)}, bf16[384,1024]{1,0:T(8,128)(2,1)S(1)}, u32[]{:S(2)}, u32[]{:S(2)}) collective-permute-start(bf16[384,1024]{1,0:T(8,128)(2,1)S(1)} %shard_map.125.refs_0_), channel_id=1, source_target_pairs={{0,2},{1,3},{2,0},{3,1},{4,6},{5,7},{6,4},{7,5},{8,10},{9,11},{10,... | collective-permute-start | bytes 2359304 | tf_op jit(solution)/shard_map/ppermute | solution.py:41
  89.2 4.0 %shard_map.124 = (bf16[768,1024]{1,0:T(8,128)(2,1)S(1)}, bf16[768,1024]{1,0:T(8,128)(2,1)S(1)}, bf16[768,768]{1,0:T(8,128)(2,1)S(1)}) custom-call(bf16[1536,768]{1,0:T(8,128)(2,1)S(1)} %get-tuple-element.93.xt_ref, bf16[1536,768]{1,0:T(8,128)(2,1)S(1)} %copy-done.1, bf16[768,256]{1,0:T(8,128)(2,1)S(1)} %get-tuple-element.106.query_ref, ...), custom_call_target="tpu_custom_call" | custom-call | flops 1380000000 | bytes 1024 | tf_op jit(solution)/shard_map/pallas_call | solution.py:327
  93.2 6.8 %collective-permute-start.11 = (bf16[768,1024]{1,0:T(8,128)(2,1)S(1)}, bf16[768,1024]{1,0:T(8,128)(2,1)S(1)}, u32[]{:S(2)}, u32[]{:S(2)}) collective-permute-start(bf16[768,1024]{1,0:T(8,128)(2,1)S(1)} %get-tuple-element.112), channel_id=1, source_target_pairs={{0,1},{1,0},{2,3},{3,2},{4,5},{5,4},{6,7},{7,6},{8,9},{9,8},{10,11... | collective-permute-start | bytes 4718600 | tf_op jit(solution)/shard_map/ppermute | solution.py:41
  100.2 9.7 %collective-permute-done.17.refs_1_ = bf16[384,1024]{1,0:T(8,128)(2,1)S(1)} collective-permute-done((bf16[384,1024]{1,0:T(8,128)(2,1)S(1)}, bf16[384,1024]{1,0:T(8,128)(2,1)S(1)}, u32[]{:S(2)}, u32[]{:S(2)}) %collective-permute-start.17) | collective-permute-done | bytes 786464 | tf_op jit(solution)/shard_map/ppermute | solution.py:41
  110.7 2.6 %fusion.6.q_ref.k_ref.v_ref = bf16[1024,768]{1,0:T(8,128)(2,1)S(1)} fusion(bf16[1024,1536]{1,0:T(8,128)(2,1)S(1)} %copy-done.7, bf16[1536,1024]{1,0:T(8,128)(2,1)S(1)} %shard_map.127.refs_4_), kind=kOutput, calls=%fused_computation.9 | convolution fusion | flops 2416705536 | bytes 7077888 | tf_op jit(solution)/shard_map/dot_general | solution.py:555
  114.1 1.5 copy-done.18
  116.3 9.4 %shard_map.128 = (bf16[768,256]{1,0:T(8,128)(2,1)S(1)}, bf16[768,256]{1,0:T(8,128)(2,1)S(1)}, bf16[2,512,256]{2,1,0:T(8,128)(2,1)S(1)}, f32[2,256,256]{2,1,0:T(8,128)S(1)}, bf16[2,256,256]{2,1,0:T(8,128)(2,1)S(1)}) custom-call(s32[2]{0:T(128)S(1)} %pad_add_fusion.pos_ref, bf16[1024,768]{1,0:T(8,128)(2,1)S(1)} %fusion.6.q_ref.k_ref.v_ref, ...), custom_call_target="tpu_custom_call" | custom-call | flops 3243000064 | bytes 1024 | tf_op jit(solution)/shard_map/pallas_call | solution.py:163
  125.9 1.5 collective-permute-start.22
  127.4 7.4 %collective-permute-done.18 = bf16[384,1024]{1,0:T(8,128)(2,1)S(1)} collective-permute-done((bf16[384,1024]{1,0:T(8,128)(2,1)S(1)}, bf16[384,1024]{1,0:T(8,128)(2,1)S(1)}, u32[]{:S(2)}, u32[]{:S(2)}) %collective-permute-start.18) | collective-permute-done | bytes 786464 | tf_op jit(solution)/shard_map/ppermute | solution.py:41
  134.8 4.0 %shard_map.129 = (bf16[768,1024]{1,0:T(8,128)(2,1)S(1)}, bf16[768,1024]{1,0:T(8,128)(2,1)S(1)}, bf16[768,768]{1,0:T(8,128)(2,1)S(1)}) custom-call(bf16[1536,768]{1,0:T(8,128)(2,1)S(1)} %get-tuple-element.93.xt_ref, bf16[1536,768]{1,0:T(8,128)(2,1)S(1)} %copy-done.1, bf16[768,256]{1,0:T(8,128)(2,1)S(1)} %get-tuple-element.131.query_ref, ...), custom_call_target="tpu_custom_call" | custom-call | flops 1380000000 | bytes 1024 | tf_op jit(solution)/shard_map/pallas_call | solution.py:327
  139.9 1.5 collective-permute-start.21
  141.8 2.6 %collective-permute-start.19 = (bf16[96,1024]{1,0:T(8,128)(2,1)S(1)}, bf16[96,1024]{1,0:T(8,128)(2,1)S(1)}, u32[]{:S(2)}, u32[]{:S(2)}) collective-permute-start(bf16[96,1024]{1,0:T(8,128)(2,1)S(1)} %get-tuple-element.194), channel_id=1, source_target_pairs={{0,4},{1,5},{2,6},{3,7},{4,0},{5,1},{6,2},{7,3},{8,12},{9,13},{10,... | collective-permute-start | bytes 589832 | tf_op jit(solution)/shard_map/ppermute | solution.py:41
  144.6 2.6 %fusion.9.q_ref.k_ref.v_ref = bf16[1024,768]{1,0:T(8,128)(2,1)S(1)} fusion(bf16[1024,1536]{1,0:T(8,128)(2,1)S(1)} %copy-done.7, bf16[1536,1024]{1,0:T(8,128)(2,1)S(1)} %shard_map.131.refs_5_), kind=kOutput, calls=%fused_computation.10 | convolution fusion | flops 2416705536 | bytes 7077888 | tf_op jit(solution)/shard_map/dot_general | solution.py:555
  148.0 1.5 copy-done.19
  149.5 1.9 collective-permute-start.26
  152.2 7.0 %collective-permute-done.20.refs_2_ = bf16[96,1024]{1,0:T(8,128)(2,1)S(1)} collective-permute-done((bf16[96,1024]{1,0:T(8,128)(2,1)S(1)}, bf16[96,1024]{1,0:T(8,128)(2,1)S(1)}, u32[]{:S(2)}, u32[]{:S(2)}) %collective-permute-start.20) | collective-permute-done | bytes 196640 | tf_op jit(solution)/shard_map/ppermute | solution.py:41
  159.2 9.4 %shard_map.132 = (bf16[768,256]{1,0:T(8,128)(2,1)S(1)}, bf16[768,256]{1,0:T(8,128)(2,1)S(1)}, bf16[2,512,256]{2,1,0:T(8,128)(2,1)S(1)}, f32[2,256,256]{2,1,0:T(8,128)S(1)}, bf16[2,256,256]{2,1,0:T(8,128)(2,1)S(1)}) custom-call(s32[2]{0:T(128)S(1)} %pad_add_fusion.pos_ref, bf16[1024,768]{1,0:T(8,128)(2,1)S(1)} %fusion.9.q_ref.k_ref.v_ref, ...), custom_call_target="tpu_custom_call" | custom-call | flops 3243000064 | bytes 1024 | tf_op jit(solution)/shard_map/pallas_call | solution.py:163
  168.6 1.6 collective-permute-start.25
  170.2 1.9 collective-permute-done.25.returned_ref
  172.0 4.0 %shard_map.133 = (bf16[768,1024]{1,0:T(8,128)(2,1)S(1)}, bf16[768,1024]{1,0:T(8,128)(2,1)S(1)}, bf16[768,768]{1,0:T(8,128)(2,1)S(1)}) custom-call(bf16[1536,768]{1,0:T(8,128)(2,1)S(1)} %get-tuple-element.93.xt_ref, bf16[1536,768]{1,0:T(8,128)(2,1)S(1)} %copy-done.1, bf16[768,256]{1,0:T(8,128)(2,1)S(1)} %get-tuple-element.142.query_ref, ...), custom_call_target="tpu_custom_call" | custom-call | flops 1380000000 | bytes 1024 | tf_op jit(solution)/shard_map/pallas_call | solution.py:327
  176.0 5.1 %collective-permute-start.27 = (bf16[768,1024]{1,0:T(8,128)(2,1)S(1)}, bf16[768,1024]{1,0:T(8,128)(2,1)S(1)}, u32[]{:S(2)}, u32[]{:S(2)}) collective-permute-start(bf16[768,1024]{1,0:T(8,128)(2,1)S(1)} %get-tuple-element.151), channel_id=1, source_target_pairs={{0,1},{1,0},{2,3},{3,2},{4,5},{5,4},{6,7},{7,6},{8,9},{9,8},{10,11... | collective-permute-start | bytes 4718600 | tf_op jit(solution)/shard_map/ppermute | solution.py:41
  181.1 3.0 %collective-permute-done.27 = bf16[768,1024]{1,0:T(8,128)(2,1)S(1)} collective-permute-done((bf16[768,1024]{1,0:T(8,128)(2,1)S(1)}, bf16[768,1024]{1,0:T(8,128)(2,1)S(1)}, u32[]{:S(2)}, u32[]{:S(2)}) %collective-permute-start.27) | collective-permute-done | bytes 1572896 | tf_op jit(solution)/shard_map/ppermute | solution.py:41
  184.9 1.5 copy-done.20
  186.4 2.2 collective-permute-start.28
  190.2 3.4 %collective-permute-start.29 = (bf16[96,1024]{1,0:T(8,128)(2,1)S(1)}, bf16[96,1024]{1,0:T(8,128)(2,1)S(1)}, u32[]{:S(2)}, u32[]{:S(2)}) collective-permute-start(bf16[96,1024]{1,0:T(8,128)(2,1)S(1)} %get-tuple-element.191), channel_id=1, source_target_pairs={{0,4},{1,5},{2,6},{3,7},{4,0},{5,1},{6,2},{7,3},{8,12},{9,13},{10,... | collective-permute-start | bytes 589832 | tf_op jit(solution)/shard_map/ppermute | solution.py:41
  193.6 5.6 %shard_map.134 = bf16[768,1536]{1,0:T(8,128)(2,1)} custom-call(s32[1]{0:T(128)} %bitcast.me_ref, bf16[768,1536]{1,0:T(8,128)(2,1)S(1)} %copy-done.3, bf16[768,256]{1,0:T(8,128)(2,1)S(1)} %get-tuple-element.110.mixed_ref.refs_0_, bf16[768,256]{1,0:T(8,128)(2,1)S(1)} %get-tuple-element.135.mixed_ref.refs_1_, ...), custom_call_target="tpu_custom_call" | custom-call | flops 2415000064 | bytes 1024 | tf_op jit(solution)/shard_map/pallas_call | solution.py:397
  199.3 8.4 %collective-permute-done.30.refs_6_ = bf16[96,1024]{1,0:T(8,128)(2,1)S(1)} collective-permute-done((bf16[96,1024]{1,0:T(8,128)(2,1)S(1)}, bf16[96,1024]{1,0:T(8,128)(2,1)S(1)}, u32[]{:S(2)}, u32[]{:S(2)}) %collective-permute-start.30) | collective-permute-done | bytes 196640 | tf_op jit(solution)/shard_map/ppermute | solution.py:41
  208.3 2.0 collective-permute-start.33
  210.3 2.4 %collective-permute-start.34 = (bf16[96,1024]{1,0:T(8,128)(2,1)S(1)}, bf16[96,1024]{1,0:T(8,128)(2,1)S(1)}, u32[]{:S(2)}, u32[]{:S(2)}) collective-permute-start(bf16[96,1024]{1,0:T(8,128)(2,1)S(1)} %get-tuple-element.161), channel_id=1, source_target_pairs={{0,12},{1,13},{2,14},{3,15},{4,8},{5,9},{6,10},{7,11},{8,4},{9,5},... | collective-permute-start | bytes 589832 | tf_op jit(solution)/shard_map/ppermute | solution.py:41
  212.6 14.0 %shard_map.135 = bf16[768,1536]{1,0:T(8,128)(2,1)} custom-call(s32[1]{0:T(128)} %bitcast.me_ref, bf16[768,1536]{1,0:T(8,128)(2,1)S(1)} %copy-done.3, bf16[768,1536]{1,0:T(8,128)(2,1)S(1)} %copy-done.9, bf16[768,768]{1,0:T(8,128)(2,1)S(1)} %get-tuple-element.163.refs_0_, bf16[768,768]{1,0:T(8,128)(2,1)S(1)} %get-tuple-element.164.refs_1_, ...), custom_call_target="tpu_custom_call" | custom-call | flops 4830000128 | bytes 1024 | tf_op jit(solution)/shard_map/pallas_call | solution.py:453
  226.7 1.2 shard_map.136
  (120 shorter events, 13.5 us)
Async XLA Ops:
  3.9 22.5 %collective-permute-start.3 = (bf16[96,1024]{1,0:T(8,128)(2,1)S(1)}, bf16[96,1024]{1,0:T(8,128)(2,1)S(1)}, u32[]{:S(2)}, u32[]{:S(2)}) collective-permute-start(bf16[96,1024]{1,0:T(8,128)(2,1)S(1)} %pad_maximum_fusion.refs_0_), channel_id=1, source_target_pairs={{0,12},{1,13},{2,14},{3,15},{4,8},{5,9},{6,10},{7,11},{8,4},{9,5},... | collective-permute-start | bytes 589832 | tf_op jit(solution)/shard_map/ppermute | solution.py:41
  9.0 17.4 %collective-permute-start.2 = (bf16[96,1024]{1,0:T(8,128)(2,1)S(1)}, bf16[96,1024]{1,0:T(8,128)(2,1)S(1)}, u32[]{:S(2)}, u32[]{:S(2)}) collective-permute-start(bf16[96,1024]{1,0:T(8,128)(2,1)S(1)} %pad_maximum_fusion.refs_0_), channel_id=1, source_target_pairs={{0,8},{1,9},{2,10},{3,11},{4,12},{5,13},{6,14},{7,15},{8,0},{9,1},... | collective-permute-start | bytes 589832 | tf_op jit(solution)/shard_map/ppermute | solution.py:41
  9.0 18.0 %collective-permute-start.1 = (bf16[96,1024]{1,0:T(8,128)(2,1)S(1)}, bf16[96,1024]{1,0:T(8,128)(2,1)S(1)}, u32[]{:S(2)}, u32[]{:S(2)}) collective-permute-start(bf16[96,1024]{1,0:T(8,128)(2,1)S(1)} %pad_maximum_fusion.refs_0_), channel_id=1, source_target_pairs={{0,4},{1,5},{2,6},{3,7},{4,0},{5,1},{6,2},{7,3},{8,12},{9,13},{10,... | collective-permute-start | bytes 589832 | tf_op jit(solution)/shard_map/ppermute | solution.py:41
  11.7 43.1 %collective-permute-start = (bf16[256,1536]{1,0:T(8,128)(2,1)}, bf16[256,1536]{1,0:T(8,128)(2,1)}, u32[]{:S(2)}, u32[]{:S(2)}) collective-permute-start(bf16[256,1536]{1,0:T(8,128)(2,1)} %slice.123), channel_id=1, source_target_pairs={{0,1},{1,2},{2,3},{3,4},{4,5},{5,6},{6,7},{7,8},{8,9},{9,10},{10,1... | collective-permute-start | bytes 2359304 | tf_op jit(solution)/shard_map/ppermute | solution.py:36
  13.9 1.7 copy-start.2
  15.5 1.7 copy-start.8
  17.2 14.8 %slice-start.3 = ((bf16[96,768]{1,0:T(8,128)(2,1)}), bf16[96,256]{1,0:T(8,128)(2,1)S(1)}, s32[]{:S(2)}) async-start(bf16[96,768]{1,0:T(8,128)(2,1)} %param.8), calls=%async_computation.3 | async-start | bytes 98304 | tf_op jit(solution)/shard_map/slice | solution.py:516
  17.2 14.8 %slice-start.5 = ((bf16[96,768]{1,0:T(8,128)(2,1)}), bf16[96,256]{1,0:T(8,128)(2,1)S(1)}, s32[]{:S(2)}) async-start(bf16[96,768]{1,0:T(8,128)(2,1)} %param.9), calls=%async_computation.5 | async-start | bytes 98304 | tf_op jit(solution)/shard_map/slice | solution.py:516
  17.2 14.8 %slice-start.7 = ((bf16[96,768]{1,0:T(8,128)(2,1)}), bf16[96,256]{1,0:T(8,128)(2,1)S(1)}, s32[]{:S(2)}) async-start(bf16[96,768]{1,0:T(8,128)(2,1)} %param.10), calls=%async_computation.7 | async-start | bytes 98304 | tf_op jit(solution)/shard_map/slice | solution.py:516
  17.2 14.8 %slice-start.9 = ((bf16[96,768]{1,0:T(8,128)(2,1)}), bf16[96,256]{1,0:T(8,128)(2,1)S(1)}, s32[]{:S(2)}) async-start(bf16[96,768]{1,0:T(8,128)(2,1)} %param.11), calls=%async_computation.9 | async-start | bytes 98304 | tf_op jit(solution)/shard_map/slice | solution.py:516
  21.9 1.4 copy-start
  23.3 1.6 copy-start.4
  24.9 1.4 copy-start.16
  27.7 0.9 copy-start.13
  30.6 24.2 %collective-permute-start.4 = (bf16[384,1024]{1,0:T(8,128)(2,1)S(1)}, bf16[384,1024]{1,0:T(8,128)(2,1)}, u32[]{:S(2)}, u32[]{:S(2)}) collective-permute-start(bf16[384,1024]{1,0:T(8,128)(2,1)S(1)} %shard_map.120.refs_0_), channel_id=1, source_target_pairs={{0,2},{1,3},{2,0},{3,1},{4,6},{5,7},{6,4},{7,5},{8,10},{9,11},{10,... | collective-permute-start | bytes 2359304 | tf_op jit(solution)/shard_map/ppermute | solution.py:41
  32.1 9.8 %collective-permute-start.7 = (bf16[96,1024]{1,0:T(8,128)(2,1)S(1)}, bf16[96,1024]{1,0:T(8,128)(2,1)S(1)}, u32[]{:S(2)}, u32[]{:S(2)}) collective-permute-start(bf16[96,1024]{1,0:T(8,128)(2,1)S(1)} %pad_maximum_fusion.1.refs_0_), channel_id=1, source_target_pairs={{0,12},{1,13},{2,14},{3,15},{4,8},{5,9},{6,10},{7,11},{8,4},{9,5},... | collective-permute-start | bytes 589832 | tf_op jit(solution)/shard_map/ppermute | solution.py:41
  35.8 17.0 %collective-permute-start.6 = (bf16[96,1024]{1,0:T(8,128)(2,1)S(1)}, bf16[96,1024]{1,0:T(8,128)(2,1)S(1)}, u32[]{:S(2)}, u32[]{:S(2)}) collective-permute-start(bf16[96,1024]{1,0:T(8,128)(2,1)S(1)} %pad_maximum_fusion.1.refs_0_), channel_id=1, source_target_pairs={{0,8},{1,9},{2,10},{3,11},{4,12},{5,13},{6,14},{7,15},{8,0},{9,1},... | collective-permute-start | bytes 589832 | tf_op jit(solution)/shard_map/ppermute | solution.py:41
  35.8 17.0 %collective-permute-start.5 = (bf16[96,1024]{1,0:T(8,128)(2,1)S(1)}, bf16[96,1024]{1,0:T(8,128)(2,1)S(1)}, u32[]{:S(2)}, u32[]{:S(2)}) collective-permute-start(bf16[96,1024]{1,0:T(8,128)(2,1)S(1)} %pad_maximum_fusion.1.refs_0_), channel_id=1, source_target_pairs={{0,4},{1,5},{2,6},{3,7},{4,0},{5,1},{6,2},{7,3},{8,12},{9,13},{10,... | collective-permute-start | bytes 589832 | tf_op jit(solution)/shard_map/ppermute | solution.py:41
  41.9 24.1 %collective-permute-start.8 = (bf16[384,1024]{1,0:T(8,128)(2,1)S(1)}, bf16[384,1024]{1,0:T(8,128)(2,1)}, u32[]{:S(2)}, u32[]{:S(2)}) collective-permute-start(bf16[384,1024]{1,0:T(8,128)(2,1)S(1)} %shard_map.120.refs_0_), channel_id=1, source_target_pairs={{0,1},{1,0},{2,3},{3,2},{4,5},{5,4},{6,7},{7,6},{8,9},{9,8},{10,11... | collective-permute-start | bytes 2359304 | tf_op jit(solution)/shard_map/ppermute | solution.py:41
  53.8 0.9 copy-start.10
  54.8 11.7 %collective-permute-start.9 = (bf16[384,1024]{1,0:T(8,128)(2,1)}, bf16[384,1024]{1,0:T(8,128)(2,1)}, u32[]{:S(2)}, u32[]{:S(2)}) collective-permute-start(bf16[384,1024]{1,0:T(8,128)(2,1)} %collective-permute-done.4.refs_1_), channel_id=1, source_target_pairs={{0,1},{1,0},{2,3},{3,2},{4,5},{5,4},{6,7},{7,6},{8,9},{9,8},{10,11... | collective-permute-start | bytes 2359304 | tf_op jit(solution)/shard_map/ppermute | solution.py:41
  55.8 1.9 copy-start.5
  57.7 3.8 %slice-start.4 = ((bf16[96,768]{1,0:T(8,128)(2,1)}), bf16[96,256]{1,0:T(8,128)(2,1)S(1)}, s32[]{:S(2)}) async-start(bf16[96,768]{1,0:T(8,128)(2,1)} %param.8), calls=%async_computation.4 | async-start | bytes 98304 | tf_op jit(solution)/shard_map/slice | solution.py:516
  57.7 3.8 %slice-start.6 = ((bf16[96,768]{1,0:T(8,128)(2,1)}), bf16[96,256]{1,0:T(8,128)(2,1)S(1)}, s32[]{:S(2)}) async-start(bf16[96,768]{1,0:T(8,128)(2,1)} %param.9), calls=%async_computation.6 | async-start | bytes 98304 | tf_op jit(solution)/shard_map/slice | solution.py:516
  57.7 3.8 %slice-start.8 = ((bf16[96,768]{1,0:T(8,128)(2,1)}), bf16[96,256]{1,0:T(8,128)(2,1)S(1)}, s32[]{:S(2)}) async-start(bf16[96,768]{1,0:T(8,128)(2,1)} %param.10), calls=%async_computation.8 | async-start | bytes 98304 | tf_op jit(solution)/shard_map/slice | solution.py:516
  57.7 3.8 %slice-start.10 = ((bf16[96,768]{1,0:T(8,128)(2,1)}), bf16[96,256]{1,0:T(8,128)(2,1)S(1)}, s32[]{:S(2)}) async-start(bf16[96,768]{1,0:T(8,128)(2,1)} %param.11), calls=%async_computation.10 | async-start | bytes 98304 | tf_op jit(solution)/shard_map/slice | solution.py:516
  57.7 8.2 %copy-start.11 = (bf16[384,1024]{1,0:T(8,128)(2,1)S(1)}, bf16[384,1024]{1,0:T(8,128)(2,1)}, u32[]{:S(2)}) copy-start(bf16[384,1024]{1,0:T(8,128)(2,1)} %copy-done.10) | copy-start | bytes 2359300
  59.8 1.6 copy-start.6
  61.5 6.7 %copy-start.7 = (bf16[1024,1536]{1,0:T(8,128)(2,1)S(1)}, bf16[1024,1536]{1,0:T(8,128)(2,1)}, u32[]{:S(2)}) copy-start(bf16[1024,1536]{1,0:T(8,128)(2,1)} %copy-done.6) | copy-start | bytes 9437188
  61.5 19.6 %collective-permute-start.15 = (bf16[96,1024]{1,0:T(8,128)(2,1)S(1)}, bf16[96,1024]{1,0:T(8,128)(2,1)S(1)}, u32[]{:S(2)}, u32[]{:S(2)}) collective-permute-start(bf16[96,1024]{1,0:T(8,128)(2,1)S(1)} %pad_maximum_fusion.2.refs_0_), channel_id=1, source_target_pairs={{0,12},{1,13},{2,14},{3,15},{4,8},{5,9},{6,10},{7,11},{8,4},{9,5},... | collective-permute-start | bytes 589832 | tf_op jit(solution)/shard_map/ppermute | solution.py:41
  63.9 17.2 %collective-permute-start.14 = (bf16[96,1024]{1,0:T(8,128)(2,1)S(1)}, bf16[96,1024]{1,0:T(8,128)(2,1)S(1)}, u32[]{:S(2)}, u32[]{:S(2)}) collective-permute-start(bf16[96,1024]{1,0:T(8,128)(2,1)S(1)} %pad_maximum_fusion.2.refs_0_), channel_id=1, source_target_pairs={{0,8},{1,9},{2,10},{3,11},{4,12},{5,13},{6,14},{7,15},{8,0},{9,1},... | collective-permute-start | bytes 589832 | tf_op jit(solution)/shard_map/ppermute | solution.py:41
  63.9 17.2 %collective-permute-start.13 = (bf16[96,1024]{1,0:T(8,128)(2,1)S(1)}, bf16[96,1024]{1,0:T(8,128)(2,1)S(1)}, u32[]{:S(2)}, u32[]{:S(2)}) collective-permute-start(bf16[96,1024]{1,0:T(8,128)(2,1)S(1)} %pad_maximum_fusion.2.refs_0_), channel_id=1, source_target_pairs={{0,4},{1,5},{2,6},{3,7},{4,0},{5,1},{6,2},{7,3},{8,12},{9,13},{10,... | collective-permute-start | bytes 589832 | tf_op jit(solution)/shard_map/ppermute | solution.py:41
  65.9 18.8 %collective-permute-start.12 = (bf16[384,1024]{1,0:T(8,128)(2,1)S(1)}, bf16[384,1024]{1,0:T(8,128)(2,1)S(1)}, u32[]{:S(2)}, u32[]{:S(2)}) collective-permute-start(bf16[384,1024]{1,0:T(8,128)(2,1)S(1)} %copy-done.11), channel_id=1, source_target_pairs={{0,2},{1,3},{2,0},{3,1},{4,6},{5,7},{6,4},{7,5},{8,10},{9,11},{10,... | collective-permute-start | bytes 2359304 | tf_op jit(solution)/shard_map/ppermute | solution.py:41
  68.2 2.7 %copy-start.17 = (bf16[768,1536]{1,0:T(8,128)(2,1)S(1)}, bf16[768,1536]{1,0:T(8,128)(2,1)}, u32[]{:S(2)}) copy-start(bf16[768,1536]{1,0:T(8,128)(2,1)} %copy-done.16) | copy-start | bytes 7077892
  81.1 8.1 %copy-start.1 = (bf16[1536,768]{1,0:T(8,128)(2,1)S(1)}, bf16[1536,768]{1,0:T(8,128)(2,1)}, u32[]{:S(2)}) copy-start(bf16[1536,768]{1,0:T(8,128)(2,1)} %copy-done) | copy-start | bytes 7077892
  84.9 15.1 %collective-permute-start.16 = (bf16[768,1024]{1,0:T(8,128)(2,1)S(1)}, bf16[768,1024]{1,0:T(8,128)(2,1)S(1)}, u32[]{:S(2)}, u32[]{:S(2)}) collective-permute-start(bf16[768,1024]{1,0:T(8,128)(2,1)S(1)} %shard_map.126.refs_0_), channel_id=1, source_target_pairs={{0,1},{1,0},{2,3},{3,2},{4,5},{5,4},{6,7},{7,6},{8,9},{9,8},{10,11... | collective-permute-start | bytes 4718600 | tf_op jit(solution)/shard_map/ppermute | solution.py:41
  85.0 4.3 %collective-permute-start.10 = (bf16[2,256,256]{2,1,0:T(8,128)(2,1)S(1)}, bf16[2,256,256]{2,1,0:T(8,128)(2,1)S(1)}, u32[]{:S(2)}, u32[]{:S(2)}) collective-permute-start(bf16[2,256,256]{2,1,0:T(8,128)(2,1)S(1)} %get-tuple-element.109), channel_id=1, source_target_pairs={{1,0},{2,1},{3,2},{4,3},{5,4},{6,5},{7,6},{8,7},{9,8},{10,9},{11,1... | collective-permute-start | bytes 786440 | tf_op jit(solution)/shard_map/ppermute | solution.py:36
  86.4 23.4 %collective-permute-start.17 = (bf16[384,1024]{1,0:T(8,128)(2,1)S(1)}, bf16[384,1024]{1,0:T(8,128)(2,1)S(1)}, u32[]{:S(2)}, u32[]{:S(2)}) collective-permute-start(bf16[384,1024]{1,0:T(8,128)(2,1)S(1)} %shard_map.125.refs_0_), channel_id=1, source_target_pairs={{0,2},{1,3},{2,0},{3,1},{4,6},{5,7},{6,4},{7,5},{8,10},{9,11},{10,... | collective-permute-start | bytes 2359304 | tf_op jit(solution)/shard_map/ppermute | solution.py:41
  93.2 20.1 %collective-permute-start.11 = (bf16[768,1024]{1,0:T(8,128)(2,1)S(1)}, bf16[768,1024]{1,0:T(8,128)(2,1)S(1)}, u32[]{:S(2)}, u32[]{:S(2)}) collective-permute-start(bf16[768,1024]{1,0:T(8,128)(2,1)S(1)} %get-tuple-element.112), channel_id=1, source_target_pairs={{0,1},{1,0},{2,3},{3,2},{4,5},{5,4},{6,7},{7,6},{8,9},{9,8},{10,11... | collective-permute-start | bytes 4718600 | tf_op jit(solution)/shard_map/ppermute | solution.py:41
  114.0 1.6 copy-start.18
  115.6 19.2 %collective-permute-start.18 = (bf16[384,1024]{1,0:T(8,128)(2,1)S(1)}, bf16[384,1024]{1,0:T(8,128)(2,1)S(1)}, u32[]{:S(2)}, u32[]{:S(2)}) collective-permute-start(bf16[384,1024]{1,0:T(8,128)(2,1)S(1)} %slice.203), channel_id=1, source_target_pairs={{0,2},{1,3},{2,0},{3,1},{4,6},{5,7},{6,4},{7,5},{8,10},{9,11},{10,... | collective-permute-start | bytes 2359304 | tf_op jit(solution)/shard_map/ppermute | solution.py:41
  125.8 18.5 %collective-permute-start.24 = (bf16[768,1024]{1,0:T(8,128)(2,1)S(1)}, bf16[768,1024]{1,0:T(8,128)(2,1)S(1)}, u32[]{:S(2)}, u32[]{:S(2)}) collective-permute-start(bf16[768,1024]{1,0:T(8,128)(2,1)S(1)} %shard_map.130.refs_0_), channel_id=1, source_target_pairs={{0,1},{1,0},{2,3},{3,2},{4,5},{5,4},{6,7},{7,6},{8,9},{9,8},{10,11... | collective-permute-start | bytes 4718600 | tf_op jit(solution)/shard_map/ppermute | solution.py:41
  125.9 8.9 %collective-permute-start.22 = (bf16[2,256,256]{2,1,0:T(8,128)(2,1)S(1)}, bf16[2,256,256]{2,1,0:T(8,128)(2,1)S(1)}, u32[]{:S(2)}, u32[]{:S(2)}) collective-permute-start(bf16[2,256,256]{2,1,0:T(8,128)(2,1)S(1)} %get-tuple-element.134), channel_id=1, source_target_pairs={{1,0},{2,1},{3,2},{4,3},{5,4},{6,5},{7,6},{8,7},{9,8},{10,9},{11,1... | collective-permute-start | bytes 786440 | tf_op jit(solution)/shard_map/ppermute | solution.py:36
  134.8 4.6 %slice-start = ((f32[768,1024]{1,0:T(8,128)}), f32[384,1024]{1,0:T(8,128)S(1)}, s32[]{:S(2)}) async-start(f32[768,1024]{1,0:T(8,128)} %copy-done.18), calls=%async_computation | async-start | bytes 3145728 | tf_op jit(solution)/shard_map/slice | solution.py:564
  138.8 8.4 %collective-permute-start.23 = (bf16[768,1024]{1,0:T(8,128)(2,1)S(1)}, bf16[768,1024]{1,0:T(8,128)(2,1)S(1)}, u32[]{:S(2)}, u32[]{:S(2)}) collective-permute-start(bf16[768,1024]{1,0:T(8,128)(2,1)S(1)} %get-tuple-element.137), channel_id=1, source_target_pairs={{0,1},{1,0},{2,3},{3,2},{4,5},{5,4},{6,7},{7,6},{8,9},{9,8},{10,11... | collective-permute-start | bytes 4718600 | tf_op jit(solution)/shard_map/ppermute | solution.py:41
  139.9 12.3 %collective-permute-start.21 = (bf16[96,1024]{1,0:T(8,128)(2,1)S(1)}, bf16[96,1024]{1,0:T(8,128)(2,1)S(1)}, u32[]{:S(2)}, u32[]{:S(2)}) collective-permute-start(bf16[96,1024]{1,0:T(8,128)(2,1)S(1)} %get-tuple-element.192), channel_id=1, source_target_pairs={{0,12},{1,13},{2,14},{3,15},{4,8},{5,9},{6,10},{7,11},{8,4},{9,5},... | collective-permute-start | bytes 589832 | tf_op jit(solution)/shard_map/ppermute | solution.py:41
  141.4 17.8 %collective-permute-start.20 = (bf16[96,1024]{1,0:T(8,128)(2,1)S(1)}, bf16[96,1024]{1,0:T(8,128)(2,1)S(1)}, u32[]{:S(2)}, u32[]{:S(2)}) collective-permute-start(bf16[96,1024]{1,0:T(8,128)(2,1)S(1)} %get-tuple-element.193), channel_id=1, source_target_pairs={{0,8},{1,9},{2,10},{3,11},{4,12},{5,13},{6,14},{7,15},{8,0},{9,1},... | collective-permute-start | bytes 589832 | tf_op jit(solution)/shard_map/ppermute | solution.py:41
  141.8 17.4 %collective-permute-start.19 = (bf16[96,1024]{1,0:T(8,128)(2,1)S(1)}, bf16[96,1024]{1,0:T(8,128)(2,1)S(1)}, u32[]{:S(2)}, u32[]{:S(2)}) collective-permute-start(bf16[96,1024]{1,0:T(8,128)(2,1)S(1)} %get-tuple-element.194), channel_id=1, source_target_pairs={{0,4},{1,5},{2,6},{3,7},{4,0},{5,1},{6,2},{7,3},{8,12},{9,13},{10,... | collective-permute-start | bytes 589832 | tf_op jit(solution)/shard_map/ppermute | solution.py:41
  147.9 1.6 copy-start.19
  149.5 20.7 %collective-permute-start.26 = (bf16[384,1024]{1,0:T(8,128)(2,1)S(1)}, bf16[384,1024]{1,0:T(8,128)(2,1)S(1)}, u32[]{:S(2)}, u32[]{:S(2)}) collective-permute-start(bf16[384,1024]{1,0:T(8,128)(2,1)S(1)} %slice.202), channel_id=1, source_target_pairs={{0,2},{1,3},{2,0},{3,1},{4,6},{5,7},{6,4},{7,5},{8,10},{9,11},{10,... | collective-permute-start | bytes 2359304 | tf_op jit(solution)/shard_map/ppermute | solution.py:41
  168.6 3.4 %collective-permute-start.25 = (bf16[2,256,256]{2,1,0:T(8,128)(2,1)S(1)}, bf16[2,256,256]{2,1,0:T(8,128)(2,1)S(1)}, u32[]{:S(2)}, u32[]{:S(2)}) collective-permute-start(bf16[2,256,256]{2,1,0:T(8,128)(2,1)S(1)} %get-tuple-element.145), channel_id=1, source_target_pairs={{1,0},{2,1},{3,2},{4,3},{5,4},{6,5},{7,6},{8,7},{9,8},{10,9},{11,1... | collective-permute-start | bytes 786440 | tf_op jit(solution)/shard_map/ppermute | solution.py:36
  176.0 8.2 %collective-permute-start.27 = (bf16[768,1024]{1,0:T(8,128)(2,1)S(1)}, bf16[768,1024]{1,0:T(8,128)(2,1)S(1)}, u32[]{:S(2)}, u32[]{:S(2)}) collective-permute-start(bf16[768,1024]{1,0:T(8,128)(2,1)S(1)} %get-tuple-element.151), channel_id=1, source_target_pairs={{0,1},{1,0},{2,3},{3,2},{4,5},{5,4},{6,7},{7,6},{8,9},{9,8},{10,11... | collective-permute-start | bytes 4718600 | tf_op jit(solution)/shard_map/ppermute | solution.py:41
  184.8 1.7 copy-start.20
  184.8 3.9 %slice-start.1 = ((f32[768,1024]{1,0:T(8,128)}), f32[384,1024]{1,0:T(8,128)S(1)}, s32[]{:S(2)}) async-start(f32[768,1024]{1,0:T(8,128)} %copy-done.19), calls=%async_computation.1 | async-start | bytes 3145728 | tf_op jit(solution)/shard_map/slice | solution.py:564
  186.4 7.2 %copy-start.3 = (bf16[768,1536]{1,0:T(8,128)(2,1)S(1)}, bf16[768,1536]{1,0:T(8,128)(2,1)}, u32[]{:S(2)}) copy-start(bf16[768,1536]{1,0:T(8,128)(2,1)} %enc_ref.3) | copy-start | bytes 7077892
  186.4 21.3 %collective-permute-start.28 = (bf16[384,1024]{1,0:T(8,128)(2,1)S(1)}, bf16[384,1024]{1,0:T(8,128)(2,1)S(1)}, u32[]{:S(2)}, u32[]{:S(2)}) collective-permute-start(bf16[384,1024]{1,0:T(8,128)(2,1)S(1)} %slice.201), channel_id=1, source_target_pairs={{0,2},{1,3},{2,0},{3,1},{4,6},{5,7},{6,4},{7,5},{8,10},{9,11},{10,... | collective-permute-start | bytes 2359304 | tf_op jit(solution)/shard_map/ppermute | solution.py:41
  189.1 10.1 %collective-permute-start.31 = (bf16[96,1024]{1,0:T(8,128)(2,1)S(1)}, bf16[96,1024]{1,0:T(8,128)(2,1)S(1)}, u32[]{:S(2)}, u32[]{:S(2)}) collective-permute-start(bf16[96,1024]{1,0:T(8,128)(2,1)S(1)} %get-tuple-element.189), channel_id=1, source_target_pairs={{0,12},{1,13},{2,14},{3,15},{4,8},{5,9},{6,10},{7,11},{8,4},{9,5},... | collective-permute-start | bytes 589832 | tf_op jit(solution)/shard_map/ppermute | solution.py:41
  189.9 17.8 %collective-permute-start.30 = (bf16[96,1024]{1,0:T(8,128)(2,1)S(1)}, bf16[96,1024]{1,0:T(8,128)(2,1)S(1)}, u32[]{:S(2)}, u32[]{:S(2)}) collective-permute-start(bf16[96,1024]{1,0:T(8,128)(2,1)S(1)} %get-tuple-element.190), channel_id=1, source_target_pairs={{0,8},{1,9},{2,10},{3,11},{4,12},{5,13},{6,14},{7,15},{8,0},{9,1},... | collective-permute-start | bytes 589832 | tf_op jit(solution)/shard_map/ppermute | solution.py:41
  190.2 17.6 %collective-permute-start.29 = (bf16[96,1024]{1,0:T(8,128)(2,1)S(1)}, bf16[96,1024]{1,0:T(8,128)(2,1)S(1)}, u32[]{:S(2)}, u32[]{:S(2)}) collective-permute-start(bf16[96,1024]{1,0:T(8,128)(2,1)S(1)} %get-tuple-element.191), channel_id=1, source_target_pairs={{0,4},{1,5},{2,6},{3,7},{4,0},{5,1},{6,2},{7,3},{8,12},{9,13},{10,... | collective-permute-start | bytes 589832 | tf_op jit(solution)/shard_map/ppermute | solution.py:41
  193.6 14.1 %slice-start.2 = ((f32[768,1024]{1,0:T(8,128)}), f32[384,1024]{1,0:T(8,128)S(1)}, s32[]{:S(2)}) async-start(f32[768,1024]{1,0:T(8,128)} %copy-done.20), calls=%async_computation.2 | async-start | bytes 3145728 | tf_op jit(solution)/shard_map/slice | solution.py:564
  199.3 13.4 %copy-start.9 = (bf16[768,1536]{1,0:T(8,128)(2,1)S(1)}, bf16[768,1536]{1,0:T(8,128)(2,1)}, u32[]{:S(2)}) copy-start(bf16[768,1536]{1,0:T(8,128)(2,1)} %cot_ref.3) | copy-start | bytes 7077892
  208.2 18.5 %collective-permute-start.32 = (bf16[96,1024]{1,0:T(8,128)(2,1)S(1)}, bf16[96,1024]{1,0:T(8,128)(2,1)S(1)}, u32[]{:S(2)}, u32[]{:S(2)}) collective-permute-start(bf16[96,1024]{1,0:T(8,128)(2,1)S(1)} %get-tuple-element.159), channel_id=1, source_target_pairs={{0,4},{1,5},{2,6},{3,7},{4,0},{5,1},{6,2},{7,3},{8,12},{9,13},{10,... | collective-permute-start | bytes 589832 | tf_op jit(solution)/shard_map/ppermute | solution.py:41
  208.3 18.4 %collective-permute-start.33 = (bf16[96,1024]{1,0:T(8,128)(2,1)S(1)}, bf16[96,1024]{1,0:T(8,128)(2,1)S(1)}, u32[]{:S(2)}, u32[]{:S(2)}) collective-permute-start(bf16[96,1024]{1,0:T(8,128)(2,1)S(1)} %get-tuple-element.160), channel_id=1, source_target_pairs={{0,8},{1,9},{2,10},{3,11},{4,12},{5,13},{6,14},{7,15},{8,0},{9,1},... | collective-permute-start | bytes 589832 | tf_op jit(solution)/shard_map/ppermute | solution.py:41
  210.3 16.5 %collective-permute-start.34 = (bf16[96,1024]{1,0:T(8,128)(2,1)S(1)}, bf16[96,1024]{1,0:T(8,128)(2,1)S(1)}, u32[]{:S(2)}, u32[]{:S(2)}) collective-permute-start(bf16[96,1024]{1,0:T(8,128)(2,1)S(1)} %get-tuple-element.161), channel_id=1, source_target_pairs={{0,12},{1,13},{2,14},{3,15},{4,8},{5,9},{6,10},{7,11},{8,4},{9,5},... | collective-permute-start | bytes 589832 | tf_op jit(solution)/shard_map/ppermute | solution.py:41
  (3 other events, 2.3 us)
where the time goes:
time: 229 us; the launch traced here: 228 us
  Pallas kernels  73.2 us (32%)
  starting transfers between devices  57.4 us (25%)
  waiting for transfers between devices  56.2 us (25%)
  local copies, waits for them, and re-layouts  25.8 us (11%)
  matrix products  10.3 us (4%)
  other arithmetic  3.16 us (1%)
    ppermute x31, waiting for transfers between devices, swapped(): return lax.ppermute(value, 'context', [(i, i ^ mask) for i in range(count)])  54.3 us
    ppermute x31, starting transfers between devices, swapped(): return lax.ppermute(value, 'context', [(i, i ^ mask) for i in range(count)])  50.7 us
    pallas_call x3, Pallas kernels, attention(): pl.pallas_call(attention_body, grid=(steps,), in_specs=[pl.BlockSpec(memo...  28.2 us
    unnamed x42, local copies, waits for them, and re-layouts  19.9 us
    pallas_call x1, Pallas kernels, finish_grad(): pl.pallas_call(body, in_specs=[pl.BlockSpec(memory_space=pltpu.SMEM), *(v...  14 us
    pallas_call x3, Pallas kernels, gradients(): pl.pallas_call(gradients_body, grid=(steps,), in_specs=[pl.BlockSpec((til...  11.9 us
    dot_general x3, matrix products, project(): jnp.dot(x, whole[:, :3 * cols], preferred_element_type=F32).astype(BF16)  7.92 us
    ppermute x4, starting transfers between devices, passed_along(): return lax.ppermute(value, axis, pairs)  6.72 us
  transfers between devices with their start and end apart: 35, of which 9 were waited for; matrix products, arithmetic and copies ran while one was open for 6% of the time, Pallas kernels for 30%

commit v1 on v0

--- a/solution.py
+++ b/solution.py
@@ -196,32 +196,34 @@
     return [4 * k + 2 * y + c for c in range(2) for y in range(2) for k in range(far)]
 
 
-def stacked(parts):
-    rows = [p.shape[0] for p in parts]
-
+def joined(parts, shape, sources, targets, grant=12):
     def body(*refs):
         out_ref, sem = refs[-2:]
         copies = [
-            pltpu.make_async_copy(
-                ref, out_ref.at[sum(rows[:i]) : sum(rows[: i + 1]), :], sem.at[i]
-            )
-            for i, ref in enumerate(refs[:-2])
+            pltpu.make_async_copy(ref.at[source], out_ref.at[target], sem.at[i])
+            for i, (ref, source, target) in enumerate(zip(refs[:-2], sources, targets))
         ]
         for copy in copies:
             copy.start()
         for copy in copies:
             copy.wait()
 
-    anywhere = pl.BlockSpec(memory_space=pl.ANY)
     return pl.pallas_call(
         body,
-        in_specs=[anywhere] * len(parts),
+        in_specs=[pl.BlockSpec(memory_space=pltpu.HBM)] * len(parts),
         out_specs=pl.BlockSpec(memory_space=pltpu.VMEM),
-        out_shape=jax.ShapeDtypeStruct((sum(rows), parts[0].shape[1]), parts[0].dtype),
+        out_shape=jax.ShapeDtypeStruct(shape, parts[0].dtype),
         scratch_shapes=[pltpu.SemaphoreType.DMA((len(parts),))],
-        compiler_params=pltpu.CompilerParams(vmem_limit_bytes=12 << 20),
+        compiler_params=pltpu.CompilerParams(vmem_limit_bytes=grant << 20),
         cost_estimate=hint(1.5),
     )(*parts)
+
+
+def stacked(parts):
+    ends = [sum(p.shape[0] for p in parts[: i + 1]) for i in range(len(parts))]
+    whole = [(slice(None), slice(None))] * len(parts)
+    targets = [(slice(end - p.shape[0], end), slice(None)) for end, p in zip(ends, parts)]
+    return joined(parts, (ends[-1], parts[0].shape[1]), whole, targets)
 
 
 def put_in_order(out_ref, flat_ref, turned_ref, value, here, order):
@@ -258,7 +260,7 @@
         ],
         scratch_shapes=[pltpu.VMEM((width, SPAN), BF16)],
         compiler_params=pltpu.CompilerParams(
-            dimension_semantics=("arbitrary",), vmem_limit_bytes=24 << 20
+            dimension_semantics=("arbitrary",), vmem_limit_bytes=60 << 20
         ),
         cost_estimate=hint(6.4),
     )(me, encoded, cotangent)
@@ -317,7 +319,7 @@
         send_ref[:, 3 * cols :] = outer
 
 
-def gradients(xt, ct, query_back, main, tail, returned, mixed):
+def gradients(xt, ct, query_back, main, tail, returned, mixed, us):
     width = xt.shape[0]
     rows, cols = mixed.shape
     tile = 256
@@ -345,7 +347,7 @@
         compiler_params=pltpu.CompilerParams(
             dimension_semantics=("arbitrary",), vmem_limit_bytes=24 << 20
         ),
-        cost_estimate=hint(4.0),
+        cost_estimate=hint(us),
     )(xt, ct, query_back, main, tail, returned, mixed)
 
 
@@ -408,7 +410,7 @@
             pltpu.SemaphoreType.DMA((groups, count)),
         ],
         compiler_params=pltpu.CompilerParams(vmem_limit_bytes=24 << 20),
-        cost_estimate=hint(7.0),
+        cost_estimate=hint(0.1),
     )(me, encoded, *attended, *weights)
 
 
@@ -512,8 +514,11 @@
     sources = (query_weight, key_weight, value_weight, out_weight)
 
     def block_of(i, sources):
-        part = slice(STARTS[i], STARTS[i] + WIDTHS[i])
-        return jnp.concatenate([w[:, part] for w in sources], axis=1)
+        cols = WIDTHS[i]
+        part = (slice(None), slice(STARTS[i], STARTS[i] + cols))
+        targets = [(slice(None), slice(k * cols, (k + 1) * cols)) for k in range(4)]
+        shape = (sources[0].shape[0], 4 * cols)
+        return joined(sources, shape, [part] * 4, targets, 12 if i else 60)
 
     raw, near, other, weights = ([None] * GROUPS for _ in range(4))
 
@@ -570,7 +575,7 @@
 
     held = got = own = parts = None
     for i in range(GROUPS):
-        projected, grad_attn = project(i, *((keeps[i - 1], *other[i + 1 : i + 2]) if i else ()))
+        projected, grad_attn = project(i, *((attended[i - 1], *other[i + 1 : i + 2]) if i else ()))
         if i:
             held, send = sum_chip(i - 1)
             held, send, projected = lax.optimization_barrier((held, send, projected))
@@ -591,7 +596,9 @@
             held, got, mixed = lax.optimization_barrier((held, got, mixed))
             own, away = split_far(held, got)
             parts = [swapped(part, 4 * k) for k, part in enumerate(away, 1)]
-        keep, send, back = gradients(xt, ct, query_back, main, tail, returned, mixed)
+        keep, send, back = gradients(
+            xt, ct, query_back, main, tail, returned, mixed, 4.0 if i + 1 < GROUPS else 0.1
+        )
         keeps.append(keep)
         sends.append(send)
         backs.append(back)

time: 229 us -> 222 us (0.969)
  local copies, waits for them, and re-layouts: 25.8 us -> 6.64 us
  Pallas kernels: 73.2 us -> 79.5 us
  starting transfers between devices: 57.4 us -> 61.5 us
  waiting for transfers between devices: 56.2 us -> 59.1 us
    unnamed x42 -> x36, local copies, waits for them, and re-layouts: 19.9 us -> 3.94 us
    ppermute x31, starting transfers between devices: 50.7 us -> 54.8 us  [swapped(): return lax.ppermute(value, 'context', [(i, i ^ mask) for i in range(count)])]
    pallas_call x1, Pallas kernels: 4.67 us -> 8.27 us  [prepare(): pl.pallas_call(body, grid=(frames // SPAN,), in_specs=[pl.BlockSpec(memor...]
    slice x20 -> x0, local copies, waits for them, and re-layouts: 3.24 us -> none  [block_of(): return jnp.concatenate([w[:, part] for w in sources], axis=1)]
    ppermute x31, waiting for transfers between devices: 54.3 us -> 57.2 us  [swapped(): return lax.ppermute(value, 'context', [(i, i ^ mask) for i in range(count)])]
    pallas_call x8 -> x11, Pallas kernels: 5.53 us -> 8.34 us  [joined(): pl.pallas_call(body, in_specs=[pl.BlockSpec(memory_space=pltpu.HBM)] * le...]
  transfers between devices with their start and end apart: 35 -> 35, of which waited for: 9 -> 10; matrix products, arithmetic and copies ran while one was open for 6% -> 6% of each run, Pallas kernels for 30% -> 33%
where the time goes in v1:
time: 222 us
  Pallas kernels  79.5 us (36%)
  starting transfers between devices  61.5 us (28%)
  waiting for transfers between devices  59.1 us (27%)
  matrix products  10.2 us (5%)
  local copies, waits for them, and re-layouts  6.64 us (3%)
  other arithmetic  2.95 us (1%)
    ppermute x31, waiting for transfers between devices, swapped(): return lax.ppermute(value, 'context', [(i, i ^ mask) for i in range(count)])  57.2 us
    ppermute x31, starting transfers between devices, swapped(): return lax.ppermute(value, 'context', [(i, i ^ mask) for i in range(count)])  54.8 us
    pallas_call x3, Pallas kernels, attention(): pl.pallas_call(attention_body, grid=(steps,), in_specs=[pl.BlockSpec(memo...  28.2 us
    pallas_call x1, Pallas kernels, finish_grad(): pl.pallas_call(body, in_specs=[pl.BlockSpec(memory_space=pltpu.SMEM), *(v...  14 us
    pallas_call x3, Pallas kernels, gradients(): pl.pallas_call(gradients_body, grid=(steps,), in_specs=[pl.BlockSpec((til...  11.8 us
    pallas_call x11, Pallas kernels, joined(): pl.pallas_call(body, in_specs=[pl.BlockSpec(memory_space=pltpu.HBM)] * le...  8.34 us
    pallas_call x1, Pallas kernels, prepare(): pl.pallas_call(body, grid=(frames // SPAN,), in_specs=[pl.BlockSpec(memor...  8.27 us
    dot_general x3, matrix products, project(): jnp.dot(x, whole[:, :3 * cols], preferred_element_type=F32).astype(BF16)  7.8 us
  transfers between devices with their start and end apart: 35, of which 10 were waited for; matrix products, arithmetic and copies ran while one was open for 6% of the time, Pallas kernels for 33%

profile of v1, /device:TPU:0, one launch (start us, length us, event | category | flops | bytes accessed | tf_op | source)
XLA Modules:
  0.0 221.7 jit_solution(3691204936204430042)
XLA Ops:
  0.6 1.6 shard_map.120.refs_0_
  2.2 5.1 %collective-permute-start.3 = (bf16[96,1024]{1,0:T(8,128)(2,1)}, bf16[96,1024]{1,0:T(8,128)(2,1)S(1)}, u32[]{:S(2)}, u32[]{:S(2)}) collective-permute-start(bf16[96,1024]{1,0:T(8,128)(2,1)} %shard_map.120.refs_0_), channel_id=1, source_target_pairs={{0,12},{1,13},{2,14},{3,15},{4,8},{5,9},{6,10},{7,11},{8,4},{9,5},... | collective-permute-start | bytes 589832 | tf_op jit(solution)/shard_map/ppermute | solution.py:41
  7.3 0.6 collective-permute-start.1
  8.0 2.1 slice.87
  10.0 2.2 collective-permute-start
  12.2 8.3 %shard_map.118 = (bf16[1024,1536]{1,0:T(8,128)(2,1)}, bf16[768,1536]{1,0:T(8,128)(2,1)}, bf16[1536,768]{1,0:T(8,128)(2,1)}, bf16[1536,768]{1,0:T(8,128)(2,1)}) custom-call(s32[1]{0:T(128)} %bitcast.me_ref, bf16[768,1536]{1,0:T(8,128)(2,1)} %enc_ref.3, bf16[768,1536]{1,0:T(8,128)(2,1)} %cot_ref.3), custom_call_target="tpu_custom_call" | custom-call | flops 2208000000 | bytes 1024 | tf_op jit(solution)/shard_map/pallas_call | solution.py:250
  20.5 3.7 %collective-permute-done.2.refs_2_ = bf16[96,1024]{1,0:T(8,128)(2,1)S(1)} collective-permute-done((bf16[96,1024]{1,0:T(8,128)(2,1)}, bf16[96,1024]{1,0:T(8,128)(2,1)S(1)}, u32[]{:S(2)}, u32[]{:S(2)}) %collective-permute-start.2) | collective-permute-done | bytes 196640 | tf_op jit(solution)/shard_map/ppermute | solution.py:41
  24.2 1.9 shard_map.121.refs_0_
  26.2 1.6 collective-permute-start.4
  27.9 3.7 %collective-permute-start.7 = (bf16[96,1024]{1,0:T(8,128)(2,1)S(1)}, bf16[96,1024]{1,0:T(8,128)(2,1)S(1)}, u32[]{:S(2)}, u32[]{:S(2)}) collective-permute-start(bf16[96,1024]{1,0:T(8,128)(2,1)S(1)} %shard_map.122.refs_0_), channel_id=1, source_target_pairs={{0,12},{1,13},{2,14},{3,15},{4,8},{5,9},{6,10},{7,11},{8,4},{9,5},... | collective-permute-start | bytes 589832 | tf_op jit(solution)/shard_map/ppermute | solution.py:41
  31.6 0.7 collective-permute-start.5
  32.3 5.3 %collective-permute-done.7.refs_3_ = bf16[96,1024]{1,0:T(8,128)(2,1)S(1)} collective-permute-done((bf16[96,1024]{1,0:T(8,128)(2,1)S(1)}, bf16[96,1024]{1,0:T(8,128)(2,1)S(1)}, u32[]{:S(2)}, u32[]{:S(2)}) %collective-permute-start.7) | collective-permute-done | bytes 196640 | tf_op jit(solution)/shard_map/ppermute | solution.py:41
  37.6 8.3 %collective-permute-done.6.refs_2_ = bf16[96,1024]{1,0:T(8,128)(2,1)S(1)} collective-permute-done((bf16[96,1024]{1,0:T(8,128)(2,1)S(1)}, bf16[96,1024]{1,0:T(8,128)(2,1)S(1)}, u32[]{:S(2)}, u32[]{:S(2)}) %collective-permute-start.6) | collective-permute-done | bytes 196640 | tf_op jit(solution)/shard_map/ppermute | solution.py:41
  45.9 1.0 shard_map.123.refs_0_
  47.0 0.9 copy-done.5
  48.6 2.1 shard_map.119
  50.9 3.1 %collective-permute-start.15 = (bf16[96,1024]{1,0:T(8,128)(2,1)S(1)}, bf16[96,1024]{1,0:T(8,128)(2,1)S(1)}, u32[]{:S(2)}, u32[]{:S(2)}) collective-permute-start(bf16[96,1024]{1,0:T(8,128)(2,1)S(1)} %shard_map.127.refs_0_), channel_id=1, source_target_pairs={{0,12},{1,13},{2,14},{3,15},{4,8},{5,9},{6,10},{7,11},{8,4},{9,5},... | collective-permute-start | bytes 589832 | tf_op jit(solution)/shard_map/ppermute | solution.py:41
  53.9 1.5 collective-permute-start.14
  55.9 3.2 %collective-permute-start.12 = (bf16[384,1024]{1,0:T(8,128)(2,1)S(1)}, bf16[384,1024]{1,0:T(8,128)(2,1)S(1)}, u32[]{:S(2)}, u32[]{:S(2)}) collective-permute-start(bf16[384,1024]{1,0:T(8,128)(2,1)S(1)} %copy-done.6), channel_id=1, source_target_pairs={{0,2},{1,3},{2,0},{3,1},{4,6},{5,7},{6,4},{7,5},{8,10},{9,11},{10,... | collective-permute-start | bytes 2359304 | tf_op jit(solution)/shard_map/ppermute | solution.py:41
  59.1 1.9 shard_map.124.refs_3_
  61.0 2.6 %fusion.12.q_ref.k_ref.v_ref = bf16[1024,768]{1,0:T(8,128)(2,1)S(1)} fusion(bf16[1024,1536]{1,0:T(8,128)(2,1)S(1)} %shard_map.119, bf16[1536,1024]{1,0:T(8,128)(2,1)S(1)} %shard_map.124.refs_3_), kind=kOutput, calls=%fused_computation.11 | convolution fusion | flops 2416705536 | bytes 7077888 | tf_op jit(solution)/shard_map/dot_general | solution.py:560
  63.6 0.8 fusion.15.g_ref
  64.4 9.4 %shard_map.125 = (bf16[768,256]{1,0:T(8,128)(2,1)S(1)}, bf16[768,256]{1,0:T(8,128)(2,1)S(1)}, bf16[2,512,256]{2,1,0:T(8,128)(2,1)S(1)}, f32[2,256,256]{2,1,0:T(8,128)S(1)}, bf16[2,256,256]{2,1,0:T(8,128)(2,1)S(1)}) custom-call(s32[2]{0:T(128)S(1)} %pad_add_fusion.pos_ref, bf16[1024,768]{1,0:T(8,128)(2,1)S(1)} %fusion.12.q_ref.k_ref.v_ref, ...), custom_call_target="tpu_custom_call" | custom-call | flops 3243000064 | bytes 1024 | tf_op jit(solution)/shard_map/pallas_call | solution.py:163
  73.8 1.1 shard_map.128.refs_0_
  74.9 1.3 collective-permute-done.12.refs_1_
  76.4 1.5 collective-permute-start.10
  77.9 2.8 %collective-permute-start.17 = (bf16[384,1024]{1,0:T(8,128)(2,1)S(1)}, bf16[384,1024]{1,0:T(8,128)(2,1)S(1)}, u32[]{:S(2)}, u32[]{:S(2)}) collective-permute-start(bf16[384,1024]{1,0:T(8,128)(2,1)S(1)} %shard_map.128.refs_0_), channel_id=1, source_target_pairs={{0,2},{1,3},{2,0},{3,1},{4,6},{5,7},{6,4},{7,5},{8,10},{9,11},{10,... | collective-permute-start | bytes 2359304 | tf_op jit(solution)/shard_map/ppermute | solution.py:41
  80.7 4.0 %shard_map.126 = (bf16[768,1024]{1,0:T(8,128)(2,1)S(1)}, bf16[768,1024]{1,0:T(8,128)(2,1)S(1)}, bf16[768,768]{1,0:T(8,128)(2,1)S(1)}) custom-call(bf16[1536,768]{1,0:T(8,128)(2,1)S(1)} %copy-done, bf16[1536,768]{1,0:T(8,128)(2,1)S(1)} %copy-done.1, bf16[768,256]{1,0:T(8,128)(2,1)S(1)} %get-tuple-element.106.query_ref, ...), custom_call_target="tpu_custom_call" | custom-call | flops 1380000000 | bytes 1024 | tf_op jit(solution)/shard_map/pallas_call | solution.py:329
  84.7 6.7 %collective-permute-start.11 = (bf16[768,1024]{1,0:T(8,128)(2,1)S(1)}, bf16[768,1024]{1,0:T(8,128)(2,1)S(1)}, u32[]{:S(2)}, u32[]{:S(2)}) collective-permute-start(bf16[768,1024]{1,0:T(8,128)(2,1)S(1)} %get-tuple-element.112), channel_id=1, source_target_pairs={{0,1},{1,0},{2,3},{3,2},{4,5},{5,4},{6,7},{7,6},{8,9},{9,8},{10,11... | collective-permute-start | bytes 4718600 | tf_op jit(solution)/shard_map/ppermute | solution.py:41
  91.7 9.7 %collective-permute-done.17.refs_1_ = bf16[384,1024]{1,0:T(8,128)(2,1)S(1)} collective-permute-done((bf16[384,1024]{1,0:T(8,128)(2,1)S(1)}, bf16[384,1024]{1,0:T(8,128)(2,1)S(1)}, u32[]{:S(2)}, u32[]{:S(2)}) %collective-permute-start.17) | collective-permute-done | bytes 786464 | tf_op jit(solution)/shard_map/ppermute | solution.py:41
  101.4 0.8 fusion.16.g_ref
  102.1 2.6 %fusion.6.q_ref.k_ref.v_ref = bf16[1024,768]{1,0:T(8,128)(2,1)S(1)} fusion(bf16[1024,1536]{1,0:T(8,128)(2,1)S(1)} %shard_map.119, bf16[1536,1024]{1,0:T(8,128)(2,1)S(1)} %shard_map.130.refs_4_), kind=kOutput, calls=%fused_computation.9 | convolution fusion | flops 2416705536 | bytes 7077888 | tf_op jit(solution)/shard_map/dot_general | solution.py:560
  104.8 0.6 convert_add_fusion.2
  105.5 1.5 copy-done.14
  107.0 1.7 collective-permute-start.18
  108.8 9.4 %shard_map.131 = (bf16[768,256]{1,0:T(8,128)(2,1)S(1)}, bf16[768,256]{1,0:T(8,128)(2,1)S(1)}, bf16[2,512,256]{2,1,0:T(8,128)(2,1)S(1)}, f32[2,256,256]{2,1,0:T(8,128)S(1)}, bf16[2,256,256]{2,1,0:T(8,128)(2,1)S(1)}) custom-call(s32[2]{0:T(128)S(1)} %pad_add_fusion.pos_ref, bf16[1024,768]{1,0:T(8,128)(2,1)S(1)} %fusion.6.q_ref.k_ref.v_ref, ...), custom_call_target="tpu_custom_call" | custom-call | flops 3243000064 | bytes 1024 | tf_op jit(solution)/shard_map/pallas_call | solution.py:163
  118.4 1.5 collective-permute-start.22
  119.9 8.0 %collective-permute-done.18 = bf16[384,1024]{1,0:T(8,128)(2,1)S(1)} collective-permute-done((bf16[384,1024]{1,0:T(8,128)(2,1)S(1)}, bf16[384,1024]{1,0:T(8,128)(2,1)S(1)}, u32[]{:S(2)}, u32[]{:S(2)}) %collective-permute-start.18) | collective-permute-done | bytes 786464 | tf_op jit(solution)/shard_map/ppermute | solution.py:41
  127.8 3.9 %shard_map.132 = (bf16[768,1024]{1,0:T(8,128)(2,1)S(1)}, bf16[768,1024]{1,0:T(8,128)(2,1)S(1)}, bf16[768,768]{1,0:T(8,128)(2,1)S(1)}) custom-call(bf16[1536,768]{1,0:T(8,128)(2,1)S(1)} %copy-done, bf16[1536,768]{1,0:T(8,128)(2,1)S(1)} %copy-done.1, bf16[768,256]{1,0:T(8,128)(2,1)S(1)} %get-tuple-element.131.query_ref, ...), custom_call_target="tpu_custom_call" | custom-call | flops 1380000000 | bytes 1024 | tf_op jit(solution)/shard_map/pallas_call | solution.py:329
  132.8 1.3 collective-permute-start.21
  134.0 1.6 collective-permute-start.20
  135.7 1.5 collective-permute-start.19
  137.5 2.6 %fusion.9.q_ref.k_ref.v_ref = bf16[1024,768]{1,0:T(8,128)(2,1)S(1)} fusion(bf16[1024,1536]{1,0:T(8,128)(2,1)S(1)} %shard_map.119, bf16[1536,1024]{1,0:T(8,128)(2,1)S(1)} %shard_map.134.refs_5_), kind=kOutput, calls=%fused_computation.10 | convolution fusion | flops 2416705536 | bytes 7077888 | tf_op jit(solution)/shard_map/dot_general | solution.py:560
  140.1 0.6 convert_add_fusion.1
  140.8 1.5 copy-done.15
  142.3 1.9 collective-permute-start.26
  144.3 0.8 fusion.17.g_ref
  145.1 8.0 %collective-permute-done.20.refs_2_ = bf16[96,1024]{1,0:T(8,128)(2,1)S(1)} collective-permute-done((bf16[96,1024]{1,0:T(8,128)(2,1)S(1)}, bf16[96,1024]{1,0:T(8,128)(2,1)S(1)}, u32[]{:S(2)}, u32[]{:S(2)}) %collective-permute-start.20) | collective-permute-done | bytes 196640 | tf_op jit(solution)/shard_map/ppermute | solution.py:41
  153.1 9.4 %shard_map.135 = (bf16[768,256]{1,0:T(8,128)(2,1)S(1)}, bf16[768,256]{1,0:T(8,128)(2,1)S(1)}, bf16[2,512,256]{2,1,0:T(8,128)(2,1)S(1)}, f32[2,256,256]{2,1,0:T(8,128)S(1)}, bf16[2,256,256]{2,1,0:T(8,128)(2,1)S(1)}) custom-call(s32[2]{0:T(128)S(1)} %pad_add_fusion.pos_ref, bf16[1024,768]{1,0:T(8,128)(2,1)S(1)} %fusion.9.q_ref.k_ref.v_ref, ...), custom_call_target="tpu_custom_call" | custom-call | flops 3243000064 | bytes 1024 | tf_op jit(solution)/shard_map/pallas_call | solution.py:163
  162.5 1.6 collective-permute-start.25
  164.1 1.9 collective-permute-done.25.returned_ref
  166.0 3.9 %shard_map.136 = (bf16[768,1024]{1,0:T(8,128)(2,1)S(1)}, bf16[768,1024]{1,0:T(8,128)(2,1)S(1)}, bf16[768,768]{1,0:T(8,128)(2,1)S(1)}) custom-call(bf16[1536,768]{1,0:T(8,128)(2,1)S(1)} %copy-done, bf16[1536,768]{1,0:T(8,128)(2,1)S(1)} %copy-done.1, bf16[768,256]{1,0:T(8,128)(2,1)S(1)} %get-tuple-element.142.query_ref, ...), custom_call_target="tpu_custom_call" | custom-call | flops 34500000 | bytes 1024 | tf_op jit(solution)/shard_map/pallas_call | solution.py:329
  169.9 5.1 %collective-permute-start.27 = (bf16[768,1024]{1,0:T(8,128)(2,1)S(1)}, bf16[768,1024]{1,0:T(8,128)(2,1)S(1)}, u32[]{:S(2)}, u32[]{:S(2)}) collective-permute-start(bf16[768,1024]{1,0:T(8,128)(2,1)S(1)} %get-tuple-element.151), channel_id=1, source_target_pairs={{0,1},{1,0},{2,3},{3,2},{4,5},{5,4},{6,7},{7,6},{8,9},{9,8},{10,11... | collective-permute-start | bytes 4718600 | tf_op jit(solution)/shard_map/ppermute | solution.py:41
  175.0 3.0 %collective-permute-done.27 = bf16[768,1024]{1,0:T(8,128)(2,1)S(1)} collective-permute-done((bf16[768,1024]{1,0:T(8,128)(2,1)S(1)}, bf16[768,1024]{1,0:T(8,128)(2,1)S(1)}, u32[]{:S(2)}, u32[]{:S(2)}) %collective-permute-start.27) | collective-permute-done | bytes 1572896 | tf_op jit(solution)/shard_map/ppermute | solution.py:41
  178.8 2.3 %collective-permute-start.28 = (bf16[384,1024]{1,0:T(8,128)(2,1)S(1)}, bf16[384,1024]{1,0:T(8,128)(2,1)S(1)}, u32[]{:S(2)}, u32[]{:S(2)}) collective-permute-start(bf16[384,1024]{1,0:T(8,128)(2,1)S(1)} %slice.153), channel_id=1, source_target_pairs={{0,2},{1,3},{2,0},{3,1},{4,6},{5,7},{6,4},{7,5},{8,10},{9,11},{10,... | collective-permute-start | bytes 2359304 | tf_op jit(solution)/shard_map/ppermute | solution.py:41
  181.6 1.5 collective-permute-start.31
  183.1 0.9 collective-permute-start.30
  184.0 2.1 collective-permute-start.29
  186.2 5.6 %shard_map.137 = bf16[768,1536]{1,0:T(8,128)(2,1)} custom-call(s32[1]{0:T(128)} %bitcast.me_ref, bf16[768,1536]{1,0:T(8,128)(2,1)S(1)} %copy-done.2, bf16[768,256]{1,0:T(8,128)(2,1)S(1)} %get-tuple-element.110.mixed_ref.refs_0_, bf16[768,256]{1,0:T(8,128)(2,1)S(1)} %get-tuple-element.135.mixed_ref.refs_1_, ...), custom_call_target="tpu_custom_call" | custom-call | flops 34500000 | bytes 1024 | tf_op jit(solution)/shard_map/pallas_call | solution.py:399
  191.8 9.8 %collective-permute-done.30.refs_6_ = bf16[96,1024]{1,0:T(8,128)(2,1)S(1)} collective-permute-done((bf16[96,1024]{1,0:T(8,128)(2,1)S(1)}, bf16[96,1024]{1,0:T(8,128)(2,1)S(1)}, u32[]{:S(2)}, u32[]{:S(2)}) %collective-permute-start.30) | collective-permute-done | bytes 196640 | tf_op jit(solution)/shard_map/ppermute | solution.py:41
  202.1 1.7 collective-permute-start.33
  203.8 2.6 %collective-permute-start.34 = (bf16[96,1024]{1,0:T(8,128)(2,1)S(1)}, bf16[96,1024]{1,0:T(8,128)(2,1)S(1)}, u32[]{:S(2)}, u32[]{:S(2)}) collective-permute-start(bf16[96,1024]{1,0:T(8,128)(2,1)S(1)} %get-tuple-element.161), channel_id=1, source_target_pairs={{0,12},{1,13},{2,14},{3,15},{4,8},{5,9},{6,10},{7,11},{8,4},{9,5},... | collective-permute-start | bytes 589832 | tf_op jit(solution)/shard_map/ppermute | solution.py:41
  206.5 14.0 %shard_map.138 = bf16[768,1536]{1,0:T(8,128)(2,1)} custom-call(s32[1]{0:T(128)} %bitcast.me_ref, bf16[768,1536]{1,0:T(8,128)(2,1)S(1)} %copy-done.2, bf16[768,1536]{1,0:T(8,128)(2,1)S(1)} %copy-done.4, bf16[768,768]{1,0:T(8,128)(2,1)S(1)} %get-tuple-element.163.refs_0_, bf16[768,768]{1,0:T(8,128)(2,1)S(1)} %get-tuple-element.164.refs_1_, ...), custom_call_target="tpu_custom_call" | custom-call | flops 4830000128 | bytes 1024 | tf_op jit(solution)/shard_map/pallas_call | solution.py:455
  220.6 1.2 shard_map.139
  (94 shorter events, 4.7 us)
Async XLA Ops:
  2.2 18.3 %collective-permute-start.3 = (bf16[96,1024]{1,0:T(8,128)(2,1)}, bf16[96,1024]{1,0:T(8,128)(2,1)S(1)}, u32[]{:S(2)}, u32[]{:S(2)}) collective-permute-start(bf16[96,1024]{1,0:T(8,128)(2,1)} %shard_map.120.refs_0_), channel_id=1, source_target_pairs={{0,12},{1,13},{2,14},{3,15},{4,8},{5,9},{6,10},{7,11},{8,4},{9,5},... | collective-permute-start | bytes 589832 | tf_op jit(solution)/shard_map/ppermute | solution.py:41
  7.3 16.9 %collective-permute-start.2 = (bf16[96,1024]{1,0:T(8,128)(2,1)}, bf16[96,1024]{1,0:T(8,128)(2,1)S(1)}, u32[]{:S(2)}, u32[]{:S(2)}) collective-permute-start(bf16[96,1024]{1,0:T(8,128)(2,1)} %shard_map.120.refs_0_), channel_id=1, source_target_pairs={{0,8},{1,9},{2,10},{3,11},{4,12},{5,13},{6,14},{7,15},{8,0},{9,1},... | collective-permute-start | bytes 589832 | tf_op jit(solution)/shard_map/ppermute | solution.py:41
  7.3 16.9 %collective-permute-start.1 = (bf16[96,1024]{1,0:T(8,128)(2,1)}, bf16[96,1024]{1,0:T(8,128)(2,1)S(1)}, u32[]{:S(2)}, u32[]{:S(2)}) collective-permute-start(bf16[96,1024]{1,0:T(8,128)(2,1)} %shard_map.120.refs_0_), channel_id=1, source_target_pairs={{0,4},{1,5},{2,6},{3,7},{4,0},{5,1},{6,2},{7,3},{8,12},{9,13},{10,... | collective-permute-start | bytes 589832 | tf_op jit(solution)/shard_map/ppermute | solution.py:41
  10.0 37.8 %collective-permute-start = (bf16[256,1536]{1,0:T(8,128)(2,1)}, bf16[256,1536]{1,0:T(8,128)(2,1)}, u32[]{:S(2)}, u32[]{:S(2)}) collective-permute-start(bf16[256,1536]{1,0:T(8,128)(2,1)} %slice.87), channel_id=1, source_target_pairs={{0,1},{1,2},{2,3},{3,4},{4,5},{5,6},{6,7},{7,8},{8,9},{9,10},{10,1... | collective-permute-start | bytes 2359304 | tf_op jit(solution)/shard_map/ppermute | solution.py:36
  12.2 12.0 %copy-start.7 = (bf16[96,1024]{1,0:T(8,128)(2,1)S(1)}, bf16[96,1024]{1,0:T(8,128)(2,1)}, u32[]{:S(2)}) copy-start(bf16[96,1024]{1,0:T(8,128)(2,1)} %shard_map.120.refs_0_) | copy-start | bytes 589828
  12.2 15.6 %copy-start.8 = (bf16[96,768]{1,0:T(8,128)(2,1)S(1)}, bf16[96,768]{1,0:T(8,128)(2,1)}, u32[]{:S(2)}) copy-start(bf16[96,768]{1,0:T(8,128)(2,1)} %refs_0_.3) | copy-start | bytes 442372
  12.2 15.6 %copy-start.9 = (bf16[96,768]{1,0:T(8,128)(2,1)S(1)}, bf16[96,768]{1,0:T(8,128)(2,1)}, u32[]{:S(2)}) copy-start(bf16[96,768]{1,0:T(8,128)(2,1)} %refs_1_.3) | copy-start | bytes 442372
  12.2 15.6 %copy-start.10 = (bf16[96,768]{1,0:T(8,128)(2,1)S(1)}, bf16[96,768]{1,0:T(8,128)(2,1)}, u32[]{:S(2)}) copy-start(bf16[96,768]{1,0:T(8,128)(2,1)} %refs_2_.3) | copy-start | bytes 442372
  12.2 15.6 %copy-start.12 = (bf16[96,768]{1,0:T(8,128)(2,1)S(1)}, bf16[96,768]{1,0:T(8,128)(2,1)}, u32[]{:S(2)}) copy-start(bf16[96,768]{1,0:T(8,128)(2,1)} %refs_3_.3) | copy-start | bytes 442372
  26.2 22.4 %copy-start.3 = (bf16[1024,1536]{1,0:T(8,128)(2,1)S(1)}, bf16[1024,1536]{1,0:T(8,128)(2,1)}, u32[]{:S(2)}) copy-start(bf16[1024,1536]{1,0:T(8,128)(2,1)} %get-tuple-element.95.x_ref) | copy-start | bytes 9437188
  26.2 21.7 %collective-permute-start.4 = (bf16[384,1024]{1,0:T(8,128)(2,1)}, bf16[384,1024]{1,0:T(8,128)(2,1)}, u32[]{:S(2)}, u32[]{:S(2)}) collective-permute-start(bf16[384,1024]{1,0:T(8,128)(2,1)} %shard_map.121.refs_0_), channel_id=1, source_target_pairs={{0,2},{1,3},{2,0},{3,1},{4,6},{5,7},{6,4},{7,5},{8,10},{9,11},{10,... | collective-permute-start | bytes 2359304 | tf_op jit(solution)/shard_map/ppermute | solution.py:41
  27.9 9.8 %collective-permute-start.7 = (bf16[96,1024]{1,0:T(8,128)(2,1)S(1)}, bf16[96,1024]{1,0:T(8,128)(2,1)S(1)}, u32[]{:S(2)}, u32[]{:S(2)}) collective-permute-start(bf16[96,1024]{1,0:T(8,128)(2,1)S(1)} %shard_map.122.refs_0_), channel_id=1, source_target_pairs={{0,12},{1,13},{2,14},{3,15},{4,8},{5,9},{6,10},{7,11},{8,4},{9,5},... | collective-permute-start | bytes 589832 | tf_op jit(solution)/shard_map/ppermute | solution.py:41
  31.6 14.3 %collective-permute-start.6 = (bf16[96,1024]{1,0:T(8,128)(2,1)S(1)}, bf16[96,1024]{1,0:T(8,128)(2,1)S(1)}, u32[]{:S(2)}, u32[]{:S(2)}) collective-permute-start(bf16[96,1024]{1,0:T(8,128)(2,1)S(1)} %shard_map.122.refs_0_), channel_id=1, source_target_pairs={{0,8},{1,9},{2,10},{3,11},{4,12},{5,13},{6,14},{7,15},{8,0},{9,1},... | collective-permute-start | bytes 589832 | tf_op jit(solution)/shard_map/ppermute | solution.py:41
  31.6 14.3 %collective-permute-start.5 = (bf16[96,1024]{1,0:T(8,128)(2,1)S(1)}, bf16[96,1024]{1,0:T(8,128)(2,1)S(1)}, u32[]{:S(2)}, u32[]{:S(2)}) collective-permute-start(bf16[96,1024]{1,0:T(8,128)(2,1)S(1)} %shard_map.122.refs_0_), channel_id=1, source_target_pairs={{0,4},{1,5},{2,6},{3,7},{4,0},{5,1},{6,2},{7,3},{8,12},{9,13},{10,... | collective-permute-start | bytes 589832 | tf_op jit(solution)/shard_map/ppermute | solution.py:41
  37.6 18.3 %collective-permute-start.8 = (bf16[384,1024]{1,0:T(8,128)(2,1)}, bf16[384,1024]{1,0:T(8,128)(2,1)}, u32[]{:S(2)}, u32[]{:S(2)}) collective-permute-start(bf16[384,1024]{1,0:T(8,128)(2,1)} %shard_map.121.refs_0_), channel_id=1, source_target_pairs={{0,1},{1,0},{2,3},{3,2},{4,5},{5,4},{6,7},{7,6},{8,9},{9,8},{10,11... | collective-permute-start | bytes 2359304 | tf_op jit(solution)/shard_map/ppermute | solution.py:41
  47.0 0.9 copy-start.5
  47.9 11.2 %collective-permute-start.9 = (bf16[384,1024]{1,0:T(8,128)(2,1)}, bf16[384,1024]{1,0:T(8,128)(2,1)}, u32[]{:S(2)}, u32[]{:S(2)}) collective-permute-start(bf16[384,1024]{1,0:T(8,128)(2,1)} %collective-permute-done.4.refs_1_), channel_id=1, source_target_pairs={{0,1},{1,0},{2,3},{3,2},{4,5},{5,4},{6,7},{7,6},{8,9},{9,8},{10,11... | collective-permute-start | bytes 2359304 | tf_op jit(solution)/shard_map/ppermute | solution.py:41
  48.6 2.2 copy-start.11
  48.6 2.2 copy-start.13
  48.6 7.3 %copy-start.6 = (bf16[384,1024]{1,0:T(8,128)(2,1)S(1)}, bf16[384,1024]{1,0:T(8,128)(2,1)}, u32[]{:S(2)}) copy-start(bf16[384,1024]{1,0:T(8,128)(2,1)} %copy-done.5) | copy-start | bytes 2359300
  50.9 22.9 %collective-permute-start.15 = (bf16[96,1024]{1,0:T(8,128)(2,1)S(1)}, bf16[96,1024]{1,0:T(8,128)(2,1)S(1)}, u32[]{:S(2)}, u32[]{:S(2)}) collective-permute-start(bf16[96,1024]{1,0:T(8,128)(2,1)S(1)} %shard_map.127.refs_0_), channel_id=1, source_target_pairs={{0,12},{1,13},{2,14},{3,15},{4,8},{5,9},{6,10},{7,11},{8,4},{9,5},... | collective-permute-start | bytes 589832 | tf_op jit(solution)/shard_map/ppermute | solution.py:41
  53.9 19.9 %collective-permute-start.14 = (bf16[96,1024]{1,0:T(8,128)(2,1)S(1)}, bf16[96,1024]{1,0:T(8,128)(2,1)S(1)}, u32[]{:S(2)}, u32[]{:S(2)}) collective-permute-start(bf16[96,1024]{1,0:T(8,128)(2,1)S(1)} %shard_map.127.refs_0_), channel_id=1, source_target_pairs={{0,8},{1,9},{2,10},{3,11},{4,12},{5,13},{6,14},{7,15},{8,0},{9,1},... | collective-permute-start | bytes 589832 | tf_op jit(solution)/shard_map/ppermute | solution.py:41
  55.4 18.4 %collective-permute-start.13 = (bf16[96,1024]{1,0:T(8,128)(2,1)S(1)}, bf16[96,1024]{1,0:T(8,128)(2,1)S(1)}, u32[]{:S(2)}, u32[]{:S(2)}) collective-permute-start(bf16[96,1024]{1,0:T(8,128)(2,1)S(1)} %shard_map.127.refs_0_), channel_id=1, source_target_pairs={{0,4},{1,5},{2,6},{3,7},{4,0},{5,1},{6,2},{7,3},{8,12},{9,13},{10,... | collective-permute-start | bytes 589832 | tf_op jit(solution)/shard_map/ppermute | solution.py:41
  55.9 20.3 %collective-permute-start.12 = (bf16[384,1024]{1,0:T(8,128)(2,1)S(1)}, bf16[384,1024]{1,0:T(8,128)(2,1)S(1)}, u32[]{:S(2)}, u32[]{:S(2)}) collective-permute-start(bf16[384,1024]{1,0:T(8,128)(2,1)S(1)} %copy-done.6), channel_id=1, source_target_pairs={{0,2},{1,3},{2,0},{3,1},{4,6},{5,7},{6,4},{7,5},{8,10},{9,11},{10,... | collective-permute-start | bytes 2359304 | tf_op jit(solution)/shard_map/ppermute | solution.py:41
  60.9 2.6 %copy-start.17 = (bf16[768,1536]{1,0:T(8,128)(2,1)S(1)}, bf16[768,1536]{1,0:T(8,128)(2,1)}, u32[]{:S(2)}) copy-start(bf16[768,1536]{1,0:T(8,128)(2,1)} %get-tuple-element.105) | copy-start | bytes 7077892
  73.8 6.9 %copy-start = (bf16[1536,768]{1,0:T(8,128)(2,1)S(1)}, bf16[1536,768]{1,0:T(8,128)(2,1)}, u32[]{:S(2)}) copy-start(bf16[1536,768]{1,0:T(8,128)(2,1)} %get-tuple-element.93.xt_ref) | copy-start | bytes 7077892
  73.8 6.9 %copy-start.1 = (bf16[1536,768]{1,0:T(8,128)(2,1)S(1)}, bf16[1536,768]{1,0:T(8,128)(2,1)}, u32[]{:S(2)}) copy-start(bf16[1536,768]{1,0:T(8,128)(2,1)} %get-tuple-element.94.ct_ref) | copy-start | bytes 7077892
  76.3 15.1 %collective-permute-start.16 = (bf16[768,1024]{1,0:T(8,128)(2,1)S(1)}, bf16[768,1024]{1,0:T(8,128)(2,1)S(1)}, u32[]{:S(2)}, u32[]{:S(2)}) collective-permute-start(bf16[768,1024]{1,0:T(8,128)(2,1)S(1)} %shard_map.129.refs_0_), channel_id=1, source_target_pairs={{0,1},{1,0},{2,3},{3,2},{4,5},{5,4},{6,7},{7,6},{8,9},{9,8},{10,11... | collective-permute-start | bytes 4718600 | tf_op jit(solution)/shard_map/ppermute | solution.py:41
  76.4 4.3 %collective-permute-start.10 = (bf16[2,256,256]{2,1,0:T(8,128)(2,1)S(1)}, bf16[2,256,256]{2,1,0:T(8,128)(2,1)S(1)}, u32[]{:S(2)}, u32[]{:S(2)}) collective-permute-start(bf16[2,256,256]{2,1,0:T(8,128)(2,1)S(1)} %get-tuple-element.109), channel_id=1, source_target_pairs={{1,0},{2,1},{3,2},{4,3},{5,4},{6,5},{7,6},{8,7},{9,8},{10,9},{11,1... | collective-permute-start | bytes 786440 | tf_op jit(solution)/shard_map/ppermute | solution.py:36
  77.9 23.4 %collective-permute-start.17 = (bf16[384,1024]{1,0:T(8,128)(2,1)S(1)}, bf16[384,1024]{1,0:T(8,128)(2,1)S(1)}, u32[]{:S(2)}, u32[]{:S(2)}) collective-permute-start(bf16[384,1024]{1,0:T(8,128)(2,1)S(1)} %shard_map.128.refs_0_), channel_id=1, source_target_pairs={{0,2},{1,3},{2,0},{3,1},{4,6},{5,7},{6,4},{7,5},{8,10},{9,11},{10,... | collective-permute-start | bytes 2359304 | tf_op jit(solution)/shard_map/ppermute | solution.py:41
  84.7 20.1 %collective-permute-start.11 = (bf16[768,1024]{1,0:T(8,128)(2,1)S(1)}, bf16[768,1024]{1,0:T(8,128)(2,1)S(1)}, u32[]{:S(2)}, u32[]{:S(2)}) collective-permute-start(bf16[768,1024]{1,0:T(8,128)(2,1)S(1)} %get-tuple-element.112), channel_id=1, source_target_pairs={{0,1},{1,0},{2,3},{3,2},{4,5},{5,4},{6,7},{7,6},{8,9},{9,8},{10,11... | collective-permute-start | bytes 4718600 | tf_op jit(solution)/shard_map/ppermute | solution.py:41
  105.4 1.6 copy-start.14
  107.0 20.8 %collective-permute-start.18 = (bf16[384,1024]{1,0:T(8,128)(2,1)S(1)}, bf16[384,1024]{1,0:T(8,128)(2,1)S(1)}, u32[]{:S(2)}, u32[]{:S(2)}) collective-permute-start(bf16[384,1024]{1,0:T(8,128)(2,1)S(1)} %slice.155), channel_id=1, source_target_pairs={{0,2},{1,3},{2,0},{3,1},{4,6},{5,7},{6,4},{7,5},{8,10},{9,11},{10,... | collective-permute-start | bytes 2359304 | tf_op jit(solution)/shard_map/ppermute | solution.py:41
  118.3 18.9 %collective-permute-start.24 = (bf16[768,1024]{1,0:T(8,128)(2,1)S(1)}, bf16[768,1024]{1,0:T(8,128)(2,1)S(1)}, u32[]{:S(2)}, u32[]{:S(2)}) collective-permute-start(bf16[768,1024]{1,0:T(8,128)(2,1)S(1)} %shard_map.133.refs_0_), channel_id=1, source_target_pairs={{0,1},{1,0},{2,3},{3,2},{4,5},{5,4},{6,7},{7,6},{8,9},{9,8},{10,11... | collective-permute-start | bytes 4718600 | tf_op jit(solution)/shard_map/ppermute | solution.py:41
  118.4 9.5 %collective-permute-start.22 = (bf16[2,256,256]{2,1,0:T(8,128)(2,1)S(1)}, bf16[2,256,256]{2,1,0:T(8,128)(2,1)S(1)}, u32[]{:S(2)}, u32[]{:S(2)}) collective-permute-start(bf16[2,256,256]{2,1,0:T(8,128)(2,1)S(1)} %get-tuple-element.134), channel_id=1, source_target_pairs={{1,0},{2,1},{3,2},{4,3},{5,4},{6,5},{7,6},{8,7},{9,8},{10,9},{11,1... | collective-permute-start | bytes 786440 | tf_op jit(solution)/shard_map/ppermute | solution.py:36
  127.8 4.6 %slice-start = ((f32[768,1024]{1,0:T(8,128)}), f32[384,1024]{1,0:T(8,128)S(1)}, s32[]{:S(2)}) async-start(f32[768,1024]{1,0:T(8,128)} %copy-done.14), calls=%async_computation | async-start | bytes 3145728 | tf_op jit(solution)/shard_map/slice | solution.py:569
  131.8 8.3 %collective-permute-start.23 = (bf16[768,1024]{1,0:T(8,128)(2,1)S(1)}, bf16[768,1024]{1,0:T(8,128)(2,1)S(1)}, u32[]{:S(2)}, u32[]{:S(2)}) collective-permute-start(bf16[768,1024]{1,0:T(8,128)(2,1)S(1)} %get-tuple-element.137), channel_id=1, source_target_pairs={{0,1},{1,0},{2,3},{3,2},{4,5},{5,4},{6,7},{7,6},{8,9},{9,8},{10,11... | collective-permute-start | bytes 4718600 | tf_op jit(solution)/shard_map/ppermute | solution.py:41
  132.8 12.3 %collective-permute-start.21 = (bf16[96,1024]{1,0:T(8,128)(2,1)S(1)}, bf16[96,1024]{1,0:T(8,128)(2,1)S(1)}, u32[]{:S(2)}, u32[]{:S(2)}) collective-permute-start(bf16[96,1024]{1,0:T(8,128)(2,1)S(1)} %get-tuple-element.192), channel_id=1, source_target_pairs={{0,12},{1,13},{2,14},{3,15},{4,8},{5,9},{6,10},{7,11},{8,4},{9,5},... | collective-permute-start | bytes 589832 | tf_op jit(solution)/shard_map/ppermute | solution.py:41
  134.0 19.1 %collective-permute-start.20 = (bf16[96,1024]{1,0:T(8,128)(2,1)S(1)}, bf16[96,1024]{1,0:T(8,128)(2,1)S(1)}, u32[]{:S(2)}, u32[]{:S(2)}) collective-permute-start(bf16[96,1024]{1,0:T(8,128)(2,1)S(1)} %get-tuple-element.193), channel_id=1, source_target_pairs={{0,8},{1,9},{2,10},{3,11},{4,12},{5,13},{6,14},{7,15},{8,0},{9,1},... | collective-permute-start | bytes 589832 | tf_op jit(solution)/shard_map/ppermute | solution.py:41
  135.7 17.4 %collective-permute-start.19 = (bf16[96,1024]{1,0:T(8,128)(2,1)S(1)}, bf16[96,1024]{1,0:T(8,128)(2,1)S(1)}, u32[]{:S(2)}, u32[]{:S(2)}) collective-permute-start(bf16[96,1024]{1,0:T(8,128)(2,1)S(1)} %get-tuple-element.194), channel_id=1, source_target_pairs={{0,4},{1,5},{2,6},{3,7},{4,0},{5,1},{6,2},{7,3},{8,12},{9,13},{10,... | collective-permute-start | bytes 589832 | tf_op jit(solution)/shard_map/ppermute | solution.py:41
  140.7 1.6 copy-start.15
  142.3 21.8 %collective-permute-start.26 = (bf16[384,1024]{1,0:T(8,128)(2,1)S(1)}, bf16[384,1024]{1,0:T(8,128)(2,1)S(1)}, u32[]{:S(2)}, u32[]{:S(2)}) collective-permute-start(bf16[384,1024]{1,0:T(8,128)(2,1)S(1)} %slice.154), channel_id=1, source_target_pairs={{0,2},{1,3},{2,0},{3,1},{4,6},{5,7},{6,4},{7,5},{8,10},{9,11},{10,... | collective-permute-start | bytes 2359304 | tf_op jit(solution)/shard_map/ppermute | solution.py:41
  162.5 3.4 %collective-permute-start.25 = (bf16[2,256,256]{2,1,0:T(8,128)(2,1)S(1)}, bf16[2,256,256]{2,1,0:T(8,128)(2,1)S(1)}, u32[]{:S(2)}, u32[]{:S(2)}) collective-permute-start(bf16[2,256,256]{2,1,0:T(8,128)(2,1)S(1)} %get-tuple-element.145), channel_id=1, source_target_pairs={{1,0},{2,1},{3,2},{4,3},{5,4},{6,5},{7,6},{8,7},{9,8},{10,9},{11,1... | collective-permute-start | bytes 786440 | tf_op jit(solution)/shard_map/ppermute | solution.py:36
  169.9 8.2 %collective-permute-start.27 = (bf16[768,1024]{1,0:T(8,128)(2,1)S(1)}, bf16[768,1024]{1,0:T(8,128)(2,1)S(1)}, u32[]{:S(2)}, u32[]{:S(2)}) collective-permute-start(bf16[768,1024]{1,0:T(8,128)(2,1)S(1)} %get-tuple-element.151), channel_id=1, source_target_pairs={{0,1},{1,0},{2,3},{3,2},{4,5},{5,4},{6,7},{7,6},{8,9},{9,8},{10,11... | collective-permute-start | bytes 4718600 | tf_op jit(solution)/shard_map/ppermute | solution.py:41
  178.7 2.9 %copy-start.16 = (f32[768,1024]{1,0:T(8,128)}, f32[768,1024]{1,0:T(8,128)S(1)}, u32[]{:S(2)}) copy-start(f32[768,1024]{1,0:T(8,128)S(1)} %convert_add_fusion) | copy-start | bytes 9437188
  178.7 2.5 %slice-start.1 = ((f32[768,1024]{1,0:T(8,128)}), f32[384,1024]{1,0:T(8,128)S(1)}, s32[]{:S(2)}) async-start(f32[768,1024]{1,0:T(8,128)} %copy-done.15), calls=%async_computation.1 | async-start | bytes 3145728 | tf_op jit(solution)/shard_map/slice | solution.py:569
  178.8 22.7 %collective-permute-start.28 = (bf16[384,1024]{1,0:T(8,128)(2,1)S(1)}, bf16[384,1024]{1,0:T(8,128)(2,1)S(1)}, u32[]{:S(2)}, u32[]{:S(2)}) collective-permute-start(bf16[384,1024]{1,0:T(8,128)(2,1)S(1)} %slice.153), channel_id=1, source_target_pairs={{0,2},{1,3},{2,0},{3,1},{4,6},{5,7},{6,4},{7,5},{8,10},{9,11},{10,... | collective-permute-start | bytes 2359304 | tf_op jit(solution)/shard_map/ppermute | solution.py:41
  181.6 4.6 %copy-start.2 = (bf16[768,1536]{1,0:T(8,128)(2,1)S(1)}, bf16[768,1536]{1,0:T(8,128)(2,1)}, u32[]{:S(2)}) copy-start(bf16[768,1536]{1,0:T(8,128)(2,1)} %enc_ref.3) | copy-start | bytes 7077892
  181.6 10.2 %collective-permute-start.31 = (bf16[96,1024]{1,0:T(8,128)(2,1)S(1)}, bf16[96,1024]{1,0:T(8,128)(2,1)S(1)}, u32[]{:S(2)}, u32[]{:S(2)}) collective-permute-start(bf16[96,1024]{1,0:T(8,128)(2,1)S(1)} %get-tuple-element.189), channel_id=1, source_target_pairs={{0,12},{1,13},{2,14},{3,15},{4,8},{5,9},{6,10},{7,11},{8,4},{9,5},... | collective-permute-start | bytes 589832 | tf_op jit(solution)/shard_map/ppermute | solution.py:41
  183.1 18.5 %collective-permute-start.30 = (bf16[96,1024]{1,0:T(8,128)(2,1)S(1)}, bf16[96,1024]{1,0:T(8,128)(2,1)S(1)}, u32[]{:S(2)}, u32[]{:S(2)}) collective-permute-start(bf16[96,1024]{1,0:T(8,128)(2,1)S(1)} %get-tuple-element.190), channel_id=1, source_target_pairs={{0,8},{1,9},{2,10},{3,11},{4,12},{5,13},{6,14},{7,15},{8,0},{9,1},... | collective-permute-start | bytes 589832 | tf_op jit(solution)/shard_map/ppermute | solution.py:41
  184.0 17.6 %collective-permute-start.29 = (bf16[96,1024]{1,0:T(8,128)(2,1)S(1)}, bf16[96,1024]{1,0:T(8,128)(2,1)S(1)}, u32[]{:S(2)}, u32[]{:S(2)}) collective-permute-start(bf16[96,1024]{1,0:T(8,128)(2,1)S(1)} %get-tuple-element.191), channel_id=1, source_target_pairs={{0,4},{1,5},{2,6},{3,7},{4,0},{5,1},{6,2},{7,3},{8,12},{9,13},{10,... | collective-permute-start | bytes 589832 | tf_op jit(solution)/shard_map/ppermute | solution.py:41
  186.2 15.4 %slice-start.2 = ((f32[768,1024]{1,0:T(8,128)}), f32[384,1024]{1,0:T(8,128)S(1)}, s32[]{:S(2)}) async-start(f32[768,1024]{1,0:T(8,128)} %copy-done.16), calls=%async_computation.2 | async-start | bytes 3145728 | tf_op jit(solution)/shard_map/slice | solution.py:569
  191.8 14.7 %copy-start.4 = (bf16[768,1536]{1,0:T(8,128)(2,1)S(1)}, bf16[768,1536]{1,0:T(8,128)(2,1)}, u32[]{:S(2)}) copy-start(bf16[768,1536]{1,0:T(8,128)(2,1)} %cot_ref.3) | copy-start | bytes 7077892
  202.0 18.5 %collective-permute-start.32 = (bf16[96,1024]{1,0:T(8,128)(2,1)S(1)}, bf16[96,1024]{1,0:T(8,128)(2,1)S(1)}, u32[]{:S(2)}, u32[]{:S(2)}) collective-permute-start(bf16[96,1024]{1,0:T(8,128)(2,1)S(1)} %get-tuple-element.159), channel_id=1, source_target_pairs={{0,4},{1,5},{2,6},{3,7},{4,0},{5,1},{6,2},{7,3},{8,12},{9,13},{10,... | collective-permute-start | bytes 589832 | tf_op jit(solution)/shard_map/ppermute | solution.py:41
  202.1 18.4 %collective-permute-start.33 = (bf16[96,1024]{1,0:T(8,128)(2,1)S(1)}, bf16[96,1024]{1,0:T(8,128)(2,1)S(1)}, u32[]{:S(2)}, u32[]{:S(2)}) collective-permute-start(bf16[96,1024]{1,0:T(8,128)(2,1)S(1)} %get-tuple-element.160), channel_id=1, source_target_pairs={{0,8},{1,9},{2,10},{3,11},{4,12},{5,13},{6,14},{7,15},{8,0},{9,1},... | collective-permute-start | bytes 589832 | tf_op jit(solution)/shard_map/ppermute | solution.py:41
  203.8 16.7 %collective-permute-start.34 = (bf16[96,1024]{1,0:T(8,128)(2,1)S(1)}, bf16[96,1024]{1,0:T(8,128)(2,1)S(1)}, u32[]{:S(2)}, u32[]{:S(2)}) collective-permute-start(bf16[96,1024]{1,0:T(8,128)(2,1)S(1)} %get-tuple-element.161), channel_id=1, source_target_pairs={{0,12},{1,13},{2,14},{3,15},{4,8},{5,9},{6,10},{7,11},{8,4},{9,5},... | collective-permute-start | bytes 589832 | tf_op jit(solution)/shard_map/ppermute | solution.py:41

commit v2 on v1

--- a/solution.py
+++ b/solution.py
@@ -564,9 +564,10 @@
     attended, backs, keeps, sends, sums = [], [], [], [], []
 
     def sum_chip(i):
-        total = keeps[i].astype(F32) + swapped(sends[i], 1).astype(F32)
-        half = total.shape[0] // 2
-        return total[:half], total[half:].astype(BF16)
+        got = swapped(sends[i], 1)
+        half = got.shape[0] // 2
+        held = keeps[i][:half].astype(F32) + got[:half].astype(F32)
+        return held, (keeps[i][half:].astype(F32) + got[half:].astype(F32)).astype(BF16)
 
     def split_far(held, got):
         total = held + got.astype(F32)

time: 222 us -> 218 us (0.982)
  local copies, waits for them, and re-layouts: 6.64 us -> 3.21 us
    unnamed x36 -> x30, local copies, waits for them, and re-layouts: 3.94 us -> 0.95 us
where the time goes in v2:
time: 218 us
  Pallas kernels  79.4 us (36%)
  starting transfers between devices  61.6 us (28%)
  waiting for transfers between devices  58.6 us (27%)
  matrix products  10.1 us (5%)
  local copies, waits for them, and re-layouts  3.21 us (1%)
  other arithmetic  2.94 us (1%)
    ppermute x31, waiting for transfers between devices, swapped(): return lax.ppermute(value, 'context', [(i, i ^ mask) for i in range(count)])  56.8 us
    ppermute x31, starting transfers between devices, swapped(): return lax.ppermute(value, 'context', [(i, i ^ mask) for i in range(count)])  54.9 us
    pallas_call x3, Pallas kernels, attention(): pl.pallas_call(attention_body, grid=(steps,), in_specs=[pl.BlockSpec(memo...  28.2 us
    pallas_call x1, Pallas kernels, finish_grad(): pl.pallas_call(body, in_specs=[pl.BlockSpec(memory_space=pltpu.SMEM), *(v...  14 us
    pallas_call x3, Pallas kernels, gradients(): pl.pallas_call(gradients_body, grid=(steps,), in_specs=[pl.BlockSpec((til...  11.8 us
    pallas_call x11, Pallas kernels, joined(): pl.pallas_call(body, in_specs=[pl.BlockSpec(memory_space=pltpu.HBM)] * le...  8.34 us
    pallas_call x1, Pallas kernels, prepare(): pl.pallas_call(body, grid=(frames // SPAN,), in_specs=[pl.BlockSpec(memor...  8.21 us
    dot_general x3, matrix products, project(): jnp.dot(x, whole[:, :3 * cols], preferred_element_type=F32).astype(BF16)  7.8 us
  transfers between devices with their start and end apart: 35, of which 10 were waited for; matrix products, arithmetic and copies ran while one was open for 6% of the time, Pallas kernels for 33%

profile of v2, /device:TPU:0, one launch (start us, length us, event | category | flops | bytes accessed | tf_op | source)
XLA Modules:
  0.0 217.8 jit_solution(16666311980051942954)
XLA Ops:
  0.6 1.6 shard_map.120.refs_0_
  2.2 5.1 %collective-permute-start.3 = (bf16[96,1024]{1,0:T(8,128)(2,1)}, bf16[96,1024]{1,0:T(8,128)(2,1)S(1)}, u32[]{:S(2)}, u32[]{:S(2)}) collective-permute-start(bf16[96,1024]{1,0:T(8,128)(2,1)} %shard_map.120.refs_0_), channel_id=1, source_target_pairs={{0,12},{1,13},{2,14},{3,15},{4,8},{5,9},{6,10},{7,11},{8,4},{9,5},... | collective-permute-start | bytes 589832 | tf_op jit(solution)/shard_map/ppermute | solution.py:41
  7.3 0.6 collective-permute-start.1
  8.0 2.1 slice.102
  10.0 2.2 %collective-permute-start = (bf16[256,1536]{1,0:T(8,128)(2,1)}, bf16[256,1536]{1,0:T(8,128)(2,1)}, u32[]{:S(2)}, u32[]{:S(2)}) collective-permute-start(bf16[256,1536]{1,0:T(8,128)(2,1)} %slice.102), channel_id=1, source_target_pairs={{0,1},{1,2},{2,3},{3,4},{4,5},{5,6},{6,7},{7,8},{8,9},{9,10},{10,1... | collective-permute-start | bytes 2359304 | tf_op jit(solution)/shard_map/ppermute | solution.py:36
  12.2 8.2 %shard_map.118 = (bf16[1024,1536]{1,0:T(8,128)(2,1)}, bf16[768,1536]{1,0:T(8,128)(2,1)}, bf16[1536,768]{1,0:T(8,128)(2,1)}, bf16[1536,768]{1,0:T(8,128)(2,1)}) custom-call(s32[1]{0:T(128)} %bitcast.me_ref, bf16[768,1536]{1,0:T(8,128)(2,1)} %enc_ref.3, bf16[768,1536]{1,0:T(8,128)(2,1)} %cot_ref.3), custom_call_target="tpu_custom_call" | custom-call | flops 2208000000 | bytes 1024 | tf_op jit(solution)/shard_map/pallas_call | solution.py:250
  20.5 3.7 %collective-permute-done.2.refs_2_ = bf16[96,1024]{1,0:T(8,128)(2,1)S(1)} collective-permute-done((bf16[96,1024]{1,0:T(8,128)(2,1)}, bf16[96,1024]{1,0:T(8,128)(2,1)S(1)}, u32[]{:S(2)}, u32[]{:S(2)}) %collective-permute-start.2) | collective-permute-done | bytes 196640 | tf_op jit(solution)/shard_map/ppermute | solution.py:41
  24.2 1.9 shard_map.121.refs_0_
  26.2 1.6 collective-permute-start.4
  27.9 3.7 %collective-permute-start.7 = (bf16[96,1024]{1,0:T(8,128)(2,1)S(1)}, bf16[96,1024]{1,0:T(8,128)(2,1)S(1)}, u32[]{:S(2)}, u32[]{:S(2)}) collective-permute-start(bf16[96,1024]{1,0:T(8,128)(2,1)S(1)} %shard_map.122.refs_0_), channel_id=1, source_target_pairs={{0,12},{1,13},{2,14},{3,15},{4,8},{5,9},{6,10},{7,11},{8,4},{9,5},... | collective-permute-start | bytes 589832 | tf_op jit(solution)/shard_map/ppermute | solution.py:41
  31.6 0.7 collective-permute-start.5
  32.3 5.3 %collective-permute-done.7.refs_3_ = bf16[96,1024]{1,0:T(8,128)(2,1)S(1)} collective-permute-done((bf16[96,1024]{1,0:T(8,128)(2,1)S(1)}, bf16[96,1024]{1,0:T(8,128)(2,1)S(1)}, u32[]{:S(2)}, u32[]{:S(2)}) %collective-permute-start.7) | collective-permute-done | bytes 196640 | tf_op jit(solution)/shard_map/ppermute | solution.py:41
  37.6 8.3 %collective-permute-done.6.refs_2_ = bf16[96,1024]{1,0:T(8,128)(2,1)S(1)} collective-permute-done((bf16[96,1024]{1,0:T(8,128)(2,1)S(1)}, bf16[96,1024]{1,0:T(8,128)(2,1)S(1)}, u32[]{:S(2)}, u32[]{:S(2)}) %collective-permute-start.6) | collective-permute-done | bytes 196640 | tf_op jit(solution)/shard_map/ppermute | solution.py:41
  45.9 1.0 shard_map.123.refs_0_
  47.0 0.9 copy-done.5
  48.6 2.1 shard_map.119
  50.8 3.0 %collective-permute-start.15 = (bf16[96,1024]{1,0:T(8,128)(2,1)S(1)}, bf16[96,1024]{1,0:T(8,128)(2,1)S(1)}, u32[]{:S(2)}, u32[]{:S(2)}) collective-permute-start(bf16[96,1024]{1,0:T(8,128)(2,1)S(1)} %shard_map.127.refs_0_), channel_id=1, source_target_pairs={{0,12},{1,13},{2,14},{3,15},{4,8},{5,9},{6,10},{7,11},{8,4},{9,5},... | collective-permute-start | bytes 589832 | tf_op jit(solution)/shard_map/ppermute | solution.py:41
  53.9 1.5 collective-permute-start.14
  55.4 0.5 collective-permute-start.13
  55.9 3.2 %collective-permute-start.12 = (bf16[384,1024]{1,0:T(8,128)(2,1)S(1)}, bf16[384,1024]{1,0:T(8,128)(2,1)S(1)}, u32[]{:S(2)}, u32[]{:S(2)}) collective-permute-start(bf16[384,1024]{1,0:T(8,128)(2,1)S(1)} %copy-done.6), channel_id=1, source_target_pairs={{0,2},{1,3},{2,0},{3,1},{4,6},{5,7},{6,4},{7,5},{8,10},{9,11},{10,... | collective-permute-start | bytes 2359304 | tf_op jit(solution)/shard_map/ppermute | solution.py:41
  59.0 1.9 shard_map.124.refs_3_
  60.9 2.6 %fusion.12.q_ref.k_ref.v_ref = bf16[1024,768]{1,0:T(8,128)(2,1)S(1)} fusion(bf16[1024,1536]{1,0:T(8,128)(2,1)S(1)} %shard_map.119, bf16[1536,1024]{1,0:T(8,128)(2,1)S(1)} %shard_map.124.refs_3_), kind=kOutput, calls=%fused_computation.8 | convolution fusion | flops 2416705536 | bytes 7077888 | tf_op jit(solution)/shard_map/dot_general | solution.py:560
  63.5 0.8 fusion.15.g_ref
  64.3 9.4 %shard_map.125 = (bf16[768,256]{1,0:T(8,128)(2,1)S(1)}, bf16[768,256]{1,0:T(8,128)(2,1)S(1)}, bf16[2,512,256]{2,1,0:T(8,128)(2,1)S(1)}, f32[2,256,256]{2,1,0:T(8,128)S(1)}, bf16[2,256,256]{2,1,0:T(8,128)(2,1)S(1)}) custom-call(s32[2]{0:T(128)S(1)} %pad_add_fusion.pos_ref, bf16[1024,768]{1,0:T(8,128)(2,1)S(1)} %fusion.12.q_ref.k_ref.v_ref, ...), custom_call_target="tpu_custom_call" | custom-call | flops 3243000064 | bytes 1024 | tf_op jit(solution)/shard_map/pallas_call | solution.py:163
  73.8 1.1 shard_map.128.refs_0_
  74.9 1.3 collective-permute-done.12.refs_1_
  76.4 1.5 collective-permute-start.10
  77.9 2.8 %collective-permute-start.17 = (bf16[384,1024]{1,0:T(8,128)(2,1)S(1)}, bf16[384,1024]{1,0:T(8,128)(2,1)S(1)}, u32[]{:S(2)}, u32[]{:S(2)}) collective-permute-start(bf16[384,1024]{1,0:T(8,128)(2,1)S(1)} %shard_map.128.refs_0_), channel_id=1, source_target_pairs={{0,2},{1,3},{2,0},{3,1},{4,6},{5,7},{6,4},{7,5},{8,10},{9,11},{10,... | collective-permute-start | bytes 2359304 | tf_op jit(solution)/shard_map/ppermute | solution.py:41
  80.7 4.0 %shard_map.126 = (bf16[768,1024]{1,0:T(8,128)(2,1)S(1)}, bf16[768,1024]{1,0:T(8,128)(2,1)S(1)}, bf16[768,768]{1,0:T(8,128)(2,1)S(1)}) custom-call(bf16[1536,768]{1,0:T(8,128)(2,1)S(1)} %copy-done, bf16[1536,768]{1,0:T(8,128)(2,1)S(1)} %copy-done.1, bf16[768,256]{1,0:T(8,128)(2,1)S(1)} %get-tuple-element.106.query_ref, ...), custom_call_target="tpu_custom_call" | custom-call | flops 1380000000 | bytes 1024 | tf_op jit(solution)/shard_map/pallas_call | solution.py:329
  84.6 6.7 %collective-permute-start.11 = (bf16[768,1024]{1,0:T(8,128)(2,1)S(1)}, bf16[768,1024]{1,0:T(8,128)(2,1)S(1)}, u32[]{:S(2)}, u32[]{:S(2)}) collective-permute-start(bf16[768,1024]{1,0:T(8,128)(2,1)S(1)} %get-tuple-element.112), channel_id=1, source_target_pairs={{0,1},{1,0},{2,3},{3,2},{4,5},{5,4},{6,7},{7,6},{8,9},{9,8},{10,11... | collective-permute-start | bytes 4718600 | tf_op jit(solution)/shard_map/ppermute | solution.py:41
  91.6 9.7 %collective-permute-done.17.refs_1_ = bf16[384,1024]{1,0:T(8,128)(2,1)S(1)} collective-permute-done((bf16[384,1024]{1,0:T(8,128)(2,1)S(1)}, bf16[384,1024]{1,0:T(8,128)(2,1)S(1)}, u32[]{:S(2)}, u32[]{:S(2)}) %collective-permute-start.17) | collective-permute-done | bytes 786464 | tf_op jit(solution)/shard_map/ppermute | solution.py:41
  101.3 0.8 fusion.16.g_ref
  102.1 2.6 %fusion.6.q_ref.k_ref.v_ref = bf16[1024,768]{1,0:T(8,128)(2,1)S(1)} fusion(bf16[1024,1536]{1,0:T(8,128)(2,1)S(1)} %shard_map.119, bf16[1536,1024]{1,0:T(8,128)(2,1)S(1)} %shard_map.130.refs_4_), kind=kOutput, calls=%fused_computation.6 | convolution fusion | flops 2416705536 | bytes 7077888 | tf_op jit(solution)/shard_map/dot_general | solution.py:560
  104.7 0.6 add_convert_fusion.2
  105.3 1.8 collective-permute-start.18
  107.1 9.4 %shard_map.131 = (bf16[768,256]{1,0:T(8,128)(2,1)S(1)}, bf16[768,256]{1,0:T(8,128)(2,1)S(1)}, bf16[2,512,256]{2,1,0:T(8,128)(2,1)S(1)}, f32[2,256,256]{2,1,0:T(8,128)S(1)}, bf16[2,256,256]{2,1,0:T(8,128)(2,1)S(1)}) custom-call(s32[2]{0:T(128)S(1)} %pad_add_fusion.pos_ref, bf16[1024,768]{1,0:T(8,128)(2,1)S(1)} %fusion.6.q_ref.k_ref.v_ref, ...), custom_call_target="tpu_custom_call" | custom-call | flops 3243000064 | bytes 1024 | tf_op jit(solution)/shard_map/pallas_call | solution.py:163
  116.7 1.5 collective-permute-start.22
  118.3 8.0 %collective-permute-done.18 = bf16[384,1024]{1,0:T(8,128)(2,1)S(1)} collective-permute-done((bf16[384,1024]{1,0:T(8,128)(2,1)S(1)}, bf16[384,1024]{1,0:T(8,128)(2,1)S(1)}, u32[]{:S(2)}, u32[]{:S(2)}) %collective-permute-start.18) | collective-permute-done | bytes 786464 | tf_op jit(solution)/shard_map/ppermute | solution.py:41
  126.2 3.9 %shard_map.132 = (bf16[768,1024]{1,0:T(8,128)(2,1)S(1)}, bf16[768,1024]{1,0:T(8,128)(2,1)S(1)}, bf16[768,768]{1,0:T(8,128)(2,1)S(1)}) custom-call(bf16[1536,768]{1,0:T(8,128)(2,1)S(1)} %copy-done, bf16[1536,768]{1,0:T(8,128)(2,1)S(1)} %copy-done.1, bf16[768,256]{1,0:T(8,128)(2,1)S(1)} %get-tuple-element.131.query_ref, ...), custom_call_target="tpu_custom_call" | custom-call | flops 1380000000 | bytes 1024 | tf_op jit(solution)/shard_map/pallas_call | solution.py:329
  130.2 0.6 collective-permute-start.23
  131.2 1.3 collective-permute-start.21
  132.4 1.6 collective-permute-start.20
  134.1 1.5 collective-permute-start.19
  135.9 2.6 %fusion.9.q_ref.k_ref.v_ref = bf16[1024,768]{1,0:T(8,128)(2,1)S(1)} fusion(bf16[1024,1536]{1,0:T(8,128)(2,1)S(1)} %shard_map.119, bf16[1536,1024]{1,0:T(8,128)(2,1)S(1)} %shard_map.134.refs_5_), kind=kOutput, calls=%fused_computation.7 | convolution fusion | flops 2416705536 | bytes 7077888 | tf_op jit(solution)/shard_map/dot_general | solution.py:560
  138.5 0.6 add_convert_fusion.1
  139.1 2.0 collective-permute-start.26
  141.1 0.8 fusion.17.g_ref
  141.9 9.6 %collective-permute-done.20.refs_2_ = bf16[96,1024]{1,0:T(8,128)(2,1)S(1)} collective-permute-done((bf16[96,1024]{1,0:T(8,128)(2,1)S(1)}, bf16[96,1024]{1,0:T(8,128)(2,1)S(1)}, u32[]{:S(2)}, u32[]{:S(2)}) %collective-permute-start.20) | collective-permute-done | bytes 196640 | tf_op jit(solution)/shard_map/ppermute | solution.py:41
  151.5 9.4 %shard_map.135 = (bf16[768,256]{1,0:T(8,128)(2,1)S(1)}, bf16[768,256]{1,0:T(8,128)(2,1)S(1)}, bf16[2,512,256]{2,1,0:T(8,128)(2,1)S(1)}, f32[2,256,256]{2,1,0:T(8,128)S(1)}, bf16[2,256,256]{2,1,0:T(8,128)(2,1)S(1)}) custom-call(s32[2]{0:T(128)S(1)} %pad_add_fusion.pos_ref, bf16[1024,768]{1,0:T(8,128)(2,1)S(1)} %fusion.9.q_ref.k_ref.v_ref, ...), custom_call_target="tpu_custom_call" | custom-call | flops 3243000064 | bytes 1024 | tf_op jit(solution)/shard_map/pallas_call | solution.py:163
  160.9 1.6 collective-permute-start.25
  162.5 1.9 collective-permute-done.25.returned_ref
  164.3 3.9 %shard_map.136 = (bf16[768,1024]{1,0:T(8,128)(2,1)S(1)}, bf16[768,1024]{1,0:T(8,128)(2,1)S(1)}, bf16[768,768]{1,0:T(8,128)(2,1)S(1)}) custom-call(bf16[1536,768]{1,0:T(8,128)(2,1)S(1)} %copy-done, bf16[1536,768]{1,0:T(8,128)(2,1)S(1)} %copy-done.1, bf16[768,256]{1,0:T(8,128)(2,1)S(1)} %get-tuple-element.142.query_ref, ...), custom_call_target="tpu_custom_call" | custom-call | flops 34500000 | bytes 1024 | tf_op jit(solution)/shard_map/pallas_call | solution.py:329
  168.3 5.1 %collective-permute-start.27 = (bf16[768,1024]{1,0:T(8,128)(2,1)S(1)}, bf16[768,1024]{1,0:T(8,128)(2,1)S(1)}, u32[]{:S(2)}, u32[]{:S(2)}) collective-permute-start(bf16[768,1024]{1,0:T(8,128)(2,1)S(1)} %get-tuple-element.151), channel_id=1, source_target_pairs={{0,1},{1,0},{2,3},{3,2},{4,5},{5,4},{6,7},{7,6},{8,9},{9,8},{10,11... | collective-permute-start | bytes 4718600 | tf_op jit(solution)/shard_map/ppermute | solution.py:41
  173.4 3.0 %collective-permute-done.27 = bf16[768,1024]{1,0:T(8,128)(2,1)S(1)} collective-permute-done((bf16[768,1024]{1,0:T(8,128)(2,1)S(1)}, bf16[768,1024]{1,0:T(8,128)(2,1)S(1)}, u32[]{:S(2)}, u32[]{:S(2)}) %collective-permute-start.27) | collective-permute-done | bytes 1572896 | tf_op jit(solution)/shard_map/ppermute | solution.py:41
  176.4 0.6 add_convert_fusion
  177.1 2.3 %collective-permute-start.28 = (bf16[384,1024]{1,0:T(8,128)(2,1)S(1)}, bf16[384,1024]{1,0:T(8,128)(2,1)S(1)}, u32[]{:S(2)}, u32[]{:S(2)}) collective-permute-start(bf16[384,1024]{1,0:T(8,128)(2,1)S(1)} %get-tuple-element.152), channel_id=1, source_target_pairs={{0,2},{1,3},{2,0},{3,1},{4,6},{5,7},{6,4},{7,5},{8,10},{9,11},{10,... | collective-permute-start | bytes 2359304 | tf_op jit(solution)/shard_map/ppermute | solution.py:41
  179.4 0.4 fusion.23
  180.2 4.1 %collective-permute-start.29 = (bf16[96,1024]{1,0:T(8,128)(2,1)S(1)}, bf16[96,1024]{1,0:T(8,128)(2,1)S(1)}, u32[]{:S(2)}, u32[]{:S(2)}) collective-permute-start(bf16[96,1024]{1,0:T(8,128)(2,1)S(1)} %get-tuple-element.197), channel_id=1, source_target_pairs={{0,4},{1,5},{2,6},{3,7},{4,0},{5,1},{6,2},{7,3},{8,12},{9,13},{10,... | collective-permute-start | bytes 589832 | tf_op jit(solution)/shard_map/ppermute | solution.py:41
  184.4 5.6 %shard_map.137 = bf16[768,1536]{1,0:T(8,128)(2,1)} custom-call(s32[1]{0:T(128)} %bitcast.me_ref, bf16[768,1536]{1,0:T(8,128)(2,1)S(1)} %copy-done.2, bf16[768,256]{1,0:T(8,128)(2,1)S(1)} %get-tuple-element.110.mixed_ref.refs_0_, bf16[768,256]{1,0:T(8,128)(2,1)S(1)} %get-tuple-element.135.mixed_ref.refs_1_, ...), custom_call_target="tpu_custom_call" | custom-call | flops 34500000 | bytes 1024 | tf_op jit(solution)/shard_map/pallas_call | solution.py:399
  190.0 7.7 %collective-permute-done.30.refs_6_ = bf16[96,1024]{1,0:T(8,128)(2,1)S(1)} collective-permute-done((bf16[96,1024]{1,0:T(8,128)(2,1)S(1)}, bf16[96,1024]{1,0:T(8,128)(2,1)S(1)}, u32[]{:S(2)}, u32[]{:S(2)}) %collective-permute-start.30) | collective-permute-done | bytes 196640 | tf_op jit(solution)/shard_map/ppermute | solution.py:41
  198.2 2.7 %collective-permute-start.33 = (bf16[96,1024]{1,0:T(8,128)(2,1)S(1)}, bf16[96,1024]{1,0:T(8,128)(2,1)S(1)}, u32[]{:S(2)}, u32[]{:S(2)}) collective-permute-start(bf16[96,1024]{1,0:T(8,128)(2,1)S(1)} %get-tuple-element.160), channel_id=1, source_target_pairs={{0,8},{1,9},{2,10},{3,11},{4,12},{5,13},{6,14},{7,15},{8,0},{9,1},... | collective-permute-start | bytes 589832 | tf_op jit(solution)/shard_map/ppermute | solution.py:41
  200.9 1.7 collective-permute-start.34
  202.5 14.0 %shard_map.138 = bf16[768,1536]{1,0:T(8,128)(2,1)} custom-call(s32[1]{0:T(128)} %bitcast.me_ref, bf16[768,1536]{1,0:T(8,128)(2,1)S(1)} %copy-done.2, bf16[768,1536]{1,0:T(8,128)(2,1)S(1)} %copy-done.4, bf16[768,768]{1,0:T(8,128)(2,1)S(1)} %get-tuple-element.163.refs_0_, bf16[768,768]{1,0:T(8,128)(2,1)S(1)} %get-tuple-element.164.refs_1_, ...), custom_call_target="tpu_custom_call" | custom-call | flops 4830000128 | bytes 1024 | tf_op jit(solution)/shard_map/pallas_call | solution.py:455
  216.6 1.2 shard_map.139
  (79 shorter events, 2.4 us)
Async XLA Ops:
  2.2 18.3 %collective-permute-start.3 = (bf16[96,1024]{1,0:T(8,128)(2,1)}, bf16[96,1024]{1,0:T(8,128)(2,1)S(1)}, u32[]{:S(2)}, u32[]{:S(2)}) collective-permute-start(bf16[96,1024]{1,0:T(8,128)(2,1)} %shard_map.120.refs_0_), channel_id=1, source_target_pairs={{0,12},{1,13},{2,14},{3,15},{4,8},{5,9},{6,10},{7,11},{8,4},{9,5},... | collective-permute-start | bytes 589832 | tf_op jit(solution)/shard_map/ppermute | solution.py:41
  7.3 16.9 %collective-permute-start.2 = (bf16[96,1024]{1,0:T(8,128)(2,1)}, bf16[96,1024]{1,0:T(8,128)(2,1)S(1)}, u32[]{:S(2)}, u32[]{:S(2)}) collective-permute-start(bf16[96,1024]{1,0:T(8,128)(2,1)} %shard_map.120.refs_0_), channel_id=1, source_target_pairs={{0,8},{1,9},{2,10},{3,11},{4,12},{5,13},{6,14},{7,15},{8,0},{9,1},... | collective-permute-start | bytes 589832 | tf_op jit(solution)/shard_map/ppermute | solution.py:41
  7.3 16.9 %collective-permute-start.1 = (bf16[96,1024]{1,0:T(8,128)(2,1)}, bf16[96,1024]{1,0:T(8,128)(2,1)S(1)}, u32[]{:S(2)}, u32[]{:S(2)}) collective-permute-start(bf16[96,1024]{1,0:T(8,128)(2,1)} %shard_map.120.refs_0_), channel_id=1, source_target_pairs={{0,4},{1,5},{2,6},{3,7},{4,0},{5,1},{6,2},{7,3},{8,12},{9,13},{10,... | collective-permute-start | bytes 589832 | tf_op jit(solution)/shard_map/ppermute | solution.py:41
  10.0 37.8 %collective-permute-start = (bf16[256,1536]{1,0:T(8,128)(2,1)}, bf16[256,1536]{1,0:T(8,128)(2,1)}, u32[]{:S(2)}, u32[]{:S(2)}) collective-permute-start(bf16[256,1536]{1,0:T(8,128)(2,1)} %slice.102), channel_id=1, source_target_pairs={{0,1},{1,2},{2,3},{3,4},{4,5},{5,6},{6,7},{7,8},{8,9},{9,10},{10,1... | collective-permute-start | bytes 2359304 | tf_op jit(solution)/shard_map/ppermute | solution.py:36
  12.2 12.0 %copy-start.7 = (bf16[96,1024]{1,0:T(8,128)(2,1)S(1)}, bf16[96,1024]{1,0:T(8,128)(2,1)}, u32[]{:S(2)}) copy-start(bf16[96,1024]{1,0:T(8,128)(2,1)} %shard_map.120.refs_0_) | copy-start | bytes 589828
  20.5 7.3 %copy-start.8 = (bf16[96,768]{1,0:T(8,128)(2,1)S(1)}, bf16[96,768]{1,0:T(8,128)(2,1)}, u32[]{:S(2)}) copy-start(bf16[96,768]{1,0:T(8,128)(2,1)} %refs_0_.3) | copy-start | bytes 442372
  20.5 7.3 %copy-start.9 = (bf16[96,768]{1,0:T(8,128)(2,1)S(1)}, bf16[96,768]{1,0:T(8,128)(2,1)}, u32[]{:S(2)}) copy-start(bf16[96,768]{1,0:T(8,128)(2,1)} %refs_1_.3) | copy-start | bytes 442372
  20.5 7.3 %copy-start.10 = (bf16[96,768]{1,0:T(8,128)(2,1)S(1)}, bf16[96,768]{1,0:T(8,128)(2,1)}, u32[]{:S(2)}) copy-start(bf16[96,768]{1,0:T(8,128)(2,1)} %refs_2_.3) | copy-start | bytes 442372
  20.5 7.3 %copy-start.12 = (bf16[96,768]{1,0:T(8,128)(2,1)S(1)}, bf16[96,768]{1,0:T(8,128)(2,1)}, u32[]{:S(2)}) copy-start(bf16[96,768]{1,0:T(8,128)(2,1)} %refs_3_.3) | copy-start | bytes 442372
  26.2 22.4 %copy-start.3 = (bf16[1024,1536]{1,0:T(8,128)(2,1)S(1)}, bf16[1024,1536]{1,0:T(8,128)(2,1)}, u32[]{:S(2)}) copy-start(bf16[1024,1536]{1,0:T(8,128)(2,1)} %get-tuple-element.95.x_ref) | copy-start | bytes 9437188
  26.2 21.7 %collective-permute-start.4 = (bf16[384,1024]{1,0:T(8,128)(2,1)}, bf16[384,1024]{1,0:T(8,128)(2,1)}, u32[]{:S(2)}, u32[]{:S(2)}) collective-permute-start(bf16[384,1024]{1,0:T(8,128)(2,1)} %shard_map.121.refs_0_), channel_id=1, source_target_pairs={{0,2},{1,3},{2,0},{3,1},{4,6},{5,7},{6,4},{7,5},{8,10},{9,11},{10,... | collective-permute-start | bytes 2359304 | tf_op jit(solution)/shard_map/ppermute | solution.py:41
  27.9 9.8 %collective-permute-start.7 = (bf16[96,1024]{1,0:T(8,128)(2,1)S(1)}, bf16[96,1024]{1,0:T(8,128)(2,1)S(1)}, u32[]{:S(2)}, u32[]{:S(2)}) collective-permute-start(bf16[96,1024]{1,0:T(8,128)(2,1)S(1)} %shard_map.122.refs_0_), channel_id=1, source_target_pairs={{0,12},{1,13},{2,14},{3,15},{4,8},{5,9},{6,10},{7,11},{8,4},{9,5},... | collective-permute-start | bytes 589832 | tf_op jit(solution)/shard_map/ppermute | solution.py:41
  31.6 14.3 %collective-permute-start.6 = (bf16[96,1024]{1,0:T(8,128)(2,1)S(1)}, bf16[96,1024]{1,0:T(8,128)(2,1)S(1)}, u32[]{:S(2)}, u32[]{:S(2)}) collective-permute-start(bf16[96,1024]{1,0:T(8,128)(2,1)S(1)} %shard_map.122.refs_0_), channel_id=1, source_target_pairs={{0,8},{1,9},{2,10},{3,11},{4,12},{5,13},{6,14},{7,15},{8,0},{9,1},... | collective-permute-start | bytes 589832 | tf_op jit(solution)/shard_map/ppermute | solution.py:41
  31.6 14.3 %collective-permute-start.5 = (bf16[96,1024]{1,0:T(8,128)(2,1)S(1)}, bf16[96,1024]{1,0:T(8,128)(2,1)S(1)}, u32[]{:S(2)}, u32[]{:S(2)}) collective-permute-start(bf16[96,1024]{1,0:T(8,128)(2,1)S(1)} %shard_map.122.refs_0_), channel_id=1, source_target_pairs={{0,4},{1,5},{2,6},{3,7},{4,0},{5,1},{6,2},{7,3},{8,12},{9,13},{10,... | collective-permute-start | bytes 589832 | tf_op jit(solution)/shard_map/ppermute | solution.py:41
  37.6 18.2 %collective-permute-start.8 = (bf16[384,1024]{1,0:T(8,128)(2,1)}, bf16[384,1024]{1,0:T(8,128)(2,1)}, u32[]{:S(2)}, u32[]{:S(2)}) collective-permute-start(bf16[384,1024]{1,0:T(8,128)(2,1)} %shard_map.121.refs_0_), channel_id=1, source_target_pairs={{0,1},{1,0},{2,3},{3,2},{4,5},{5,4},{6,7},{7,6},{8,9},{9,8},{10,11... | collective-permute-start | bytes 2359304 | tf_op jit(solution)/shard_map/ppermute | solution.py:41
  47.0 0.9 copy-start.5
  47.9 11.1 %collective-permute-start.9 = (bf16[384,1024]{1,0:T(8,128)(2,1)}, bf16[384,1024]{1,0:T(8,128)(2,1)}, u32[]{:S(2)}, u32[]{:S(2)}) collective-permute-start(bf16[384,1024]{1,0:T(8,128)(2,1)} %collective-permute-done.4.refs_1_), channel_id=1, source_target_pairs={{0,1},{1,0},{2,3},{3,2},{4,5},{5,4},{6,7},{7,6},{8,9},{9,8},{10,11... | collective-permute-start | bytes 2359304 | tf_op jit(solution)/shard_map/ppermute | solution.py:41
  48.6 2.1 copy-start.11
  48.6 2.1 copy-start.13
  50.7 5.1 %copy-start.6 = (bf16[384,1024]{1,0:T(8,128)(2,1)S(1)}, bf16[384,1024]{1,0:T(8,128)(2,1)}, u32[]{:S(2)}) copy-start(bf16[384,1024]{1,0:T(8,128)(2,1)} %copy-done.5) | copy-start | bytes 2359300
  50.8 22.9 %collective-permute-start.15 = (bf16[96,1024]{1,0:T(8,128)(2,1)S(1)}, bf16[96,1024]{1,0:T(8,128)(2,1)S(1)}, u32[]{:S(2)}, u32[]{:S(2)}) collective-permute-start(bf16[96,1024]{1,0:T(8,128)(2,1)S(1)} %shard_map.127.refs_0_), channel_id=1, source_target_pairs={{0,12},{1,13},{2,14},{3,15},{4,8},{5,9},{6,10},{7,11},{8,4},{9,5},... | collective-permute-start | bytes 589832 | tf_op jit(solution)/shard_map/ppermute | solution.py:41
  53.9 19.9 %collective-permute-start.14 = (bf16[96,1024]{1,0:T(8,128)(2,1)S(1)}, bf16[96,1024]{1,0:T(8,128)(2,1)S(1)}, u32[]{:S(2)}, u32[]{:S(2)}) collective-permute-start(bf16[96,1024]{1,0:T(8,128)(2,1)S(1)} %shard_map.127.refs_0_), channel_id=1, source_target_pairs={{0,8},{1,9},{2,10},{3,11},{4,12},{5,13},{6,14},{7,15},{8,0},{9,1},... | collective-permute-start | bytes 589832 | tf_op jit(solution)/shard_map/ppermute | solution.py:41
  55.4 18.4 %collective-permute-start.13 = (bf16[96,1024]{1,0:T(8,128)(2,1)S(1)}, bf16[96,1024]{1,0:T(8,128)(2,1)S(1)}, u32[]{:S(2)}, u32[]{:S(2)}) collective-permute-start(bf16[96,1024]{1,0:T(8,128)(2,1)S(1)} %shard_map.127.refs_0_), channel_id=1, source_target_pairs={{0,4},{1,5},{2,6},{3,7},{4,0},{5,1},{6,2},{7,3},{8,12},{9,13},{10,... | collective-permute-start | bytes 589832 | tf_op jit(solution)/shard_map/ppermute | solution.py:41
  55.9 20.3 %collective-permute-start.12 = (bf16[384,1024]{1,0:T(8,128)(2,1)S(1)}, bf16[384,1024]{1,0:T(8,128)(2,1)S(1)}, u32[]{:S(2)}, u32[]{:S(2)}) collective-permute-start(bf16[384,1024]{1,0:T(8,128)(2,1)S(1)} %copy-done.6), channel_id=1, source_target_pairs={{0,2},{1,3},{2,0},{3,1},{4,6},{5,7},{6,4},{7,5},{8,10},{9,11},{10,... | collective-permute-start | bytes 2359304 | tf_op jit(solution)/shard_map/ppermute | solution.py:41
  60.9 2.6 %copy-start.14 = (bf16[768,1536]{1,0:T(8,128)(2,1)S(1)}, bf16[768,1536]{1,0:T(8,128)(2,1)}, u32[]{:S(2)}) copy-start(bf16[768,1536]{1,0:T(8,128)(2,1)} %get-tuple-element.105) | copy-start | bytes 7077892
  73.8 6.9 %copy-start.1 = (bf16[1536,768]{1,0:T(8,128)(2,1)S(1)}, bf16[1536,768]{1,0:T(8,128)(2,1)}, u32[]{:S(2)}) copy-start(bf16[1536,768]{1,0:T(8,128)(2,1)} %get-tuple-element.94.ct_ref) | copy-start | bytes 7077892
  74.9 5.8 %copy-start = (bf16[1536,768]{1,0:T(8,128)(2,1)S(1)}, bf16[1536,768]{1,0:T(8,128)(2,1)}, u32[]{:S(2)}) copy-start(bf16[1536,768]{1,0:T(8,128)(2,1)} %get-tuple-element.93.xt_ref) | copy-start | bytes 7077892
  76.3 15.1 %collective-permute-start.16 = (bf16[768,1024]{1,0:T(8,128)(2,1)S(1)}, bf16[768,1024]{1,0:T(8,128)(2,1)S(1)}, u32[]{:S(2)}, u32[]{:S(2)}) collective-permute-start(bf16[768,1024]{1,0:T(8,128)(2,1)S(1)} %shard_map.129.refs_0_), channel_id=1, source_target_pairs={{0,1},{1,0},{2,3},{3,2},{4,5},{5,4},{6,7},{7,6},{8,9},{9,8},{10,11... | collective-permute-start | bytes 4718600 | tf_op jit(solution)/shard_map/ppermute | solution.py:41
  76.4 4.3 %collective-permute-start.10 = (bf16[2,256,256]{2,1,0:T(8,128)(2,1)S(1)}, bf16[2,256,256]{2,1,0:T(8,128)(2,1)S(1)}, u32[]{:S(2)}, u32[]{:S(2)}) collective-permute-start(bf16[2,256,256]{2,1,0:T(8,128)(2,1)S(1)} %get-tuple-element.109), channel_id=1, source_target_pairs={{1,0},{2,1},{3,2},{4,3},{5,4},{6,5},{7,6},{8,7},{9,8},{10,9},{11,1... | collective-permute-start | bytes 786440 | tf_op jit(solution)/shard_map/ppermute | solution.py:36
  77.9 23.4 %collective-permute-start.17 = (bf16[384,1024]{1,0:T(8,128)(2,1)S(1)}, bf16[384,1024]{1,0:T(8,128)(2,1)S(1)}, u32[]{:S(2)}, u32[]{:S(2)}) collective-permute-start(bf16[384,1024]{1,0:T(8,128)(2,1)S(1)} %shard_map.128.refs_0_), channel_id=1, source_target_pairs={{0,2},{1,3},{2,0},{3,1},{4,6},{5,7},{6,4},{7,5},{8,10},{9,11},{10,... | collective-permute-start | bytes 2359304 | tf_op jit(solution)/shard_map/ppermute | solution.py:41
  84.6 20.1 %collective-permute-start.11 = (bf16[768,1024]{1,0:T(8,128)(2,1)S(1)}, bf16[768,1024]{1,0:T(8,128)(2,1)S(1)}, u32[]{:S(2)}, u32[]{:S(2)}) collective-permute-start(bf16[768,1024]{1,0:T(8,128)(2,1)S(1)} %get-tuple-element.112), channel_id=1, source_target_pairs={{0,1},{1,0},{2,3},{3,2},{4,5},{5,4},{6,7},{7,6},{8,9},{9,8},{10,11... | collective-permute-start | bytes 4718600 | tf_op jit(solution)/shard_map/ppermute | solution.py:41
  105.3 20.9 %collective-permute-start.18 = (bf16[384,1024]{1,0:T(8,128)(2,1)S(1)}, bf16[384,1024]{1,0:T(8,128)(2,1)S(1)}, u32[]{:S(2)}, u32[]{:S(2)}) collective-permute-start(bf16[384,1024]{1,0:T(8,128)(2,1)S(1)} %get-tuple-element.126), channel_id=1, source_target_pairs={{0,2},{1,3},{2,0},{3,1},{4,6},{5,7},{6,4},{7,5},{8,10},{9,11},{10,... | collective-permute-start | bytes 2359304 | tf_op jit(solution)/shard_map/ppermute | solution.py:41
  116.7 19.0 %collective-permute-start.24 = (bf16[768,1024]{1,0:T(8,128)(2,1)S(1)}, bf16[768,1024]{1,0:T(8,128)(2,1)S(1)}, u32[]{:S(2)}, u32[]{:S(2)}) collective-permute-start(bf16[768,1024]{1,0:T(8,128)(2,1)S(1)} %shard_map.133.refs_0_), channel_id=1, source_target_pairs={{0,1},{1,0},{2,3},{3,2},{4,5},{5,4},{6,7},{7,6},{8,9},{9,8},{10,11... | collective-permute-start | bytes 4718600 | tf_op jit(solution)/shard_map/ppermute | solution.py:41
  116.7 9.5 %collective-permute-start.22 = (bf16[2,256,256]{2,1,0:T(8,128)(2,1)S(1)}, bf16[2,256,256]{2,1,0:T(8,128)(2,1)S(1)}, u32[]{:S(2)}, u32[]{:S(2)}) collective-permute-start(bf16[2,256,256]{2,1,0:T(8,128)(2,1)S(1)} %get-tuple-element.134), channel_id=1, source_target_pairs={{1,0},{2,1},{3,2},{4,3},{5,4},{6,5},{7,6},{8,7},{9,8},{10,9},{11,1... | collective-permute-start | bytes 786440 | tf_op jit(solution)/shard_map/ppermute | solution.py:36
  130.2 8.3 %collective-permute-start.23 = (bf16[768,1024]{1,0:T(8,128)(2,1)S(1)}, bf16[768,1024]{1,0:T(8,128)(2,1)S(1)}, u32[]{:S(2)}, u32[]{:S(2)}) collective-permute-start(bf16[768,1024]{1,0:T(8,128)(2,1)S(1)} %get-tuple-element.137), channel_id=1, source_target_pairs={{0,1},{1,0},{2,3},{3,2},{4,5},{5,4},{6,7},{7,6},{8,9},{9,8},{10,11... | collective-permute-start | bytes 4718600 | tf_op jit(solution)/shard_map/ppermute | solution.py:41
  131.2 10.7 %collective-permute-start.21 = (bf16[96,1024]{1,0:T(8,128)(2,1)S(1)}, bf16[96,1024]{1,0:T(8,128)(2,1)S(1)}, u32[]{:S(2)}, u32[]{:S(2)}) collective-permute-start(bf16[96,1024]{1,0:T(8,128)(2,1)S(1)} %get-tuple-element.198), channel_id=1, source_target_pairs={{0,12},{1,13},{2,14},{3,15},{4,8},{5,9},{6,10},{7,11},{8,4},{9,5},... | collective-permute-start | bytes 589832 | tf_op jit(solution)/shard_map/ppermute | solution.py:41
  132.4 19.1 %collective-permute-start.20 = (bf16[96,1024]{1,0:T(8,128)(2,1)S(1)}, bf16[96,1024]{1,0:T(8,128)(2,1)S(1)}, u32[]{:S(2)}, u32[]{:S(2)}) collective-permute-start(bf16[96,1024]{1,0:T(8,128)(2,1)S(1)} %get-tuple-element.199), channel_id=1, source_target_pairs={{0,8},{1,9},{2,10},{3,11},{4,12},{5,13},{6,14},{7,15},{8,0},{9,1},... | collective-permute-start | bytes 589832 | tf_op jit(solution)/shard_map/ppermute | solution.py:41
  134.1 17.4 %collective-permute-start.19 = (bf16[96,1024]{1,0:T(8,128)(2,1)S(1)}, bf16[96,1024]{1,0:T(8,128)(2,1)S(1)}, u32[]{:S(2)}, u32[]{:S(2)}) collective-permute-start(bf16[96,1024]{1,0:T(8,128)(2,1)S(1)} %get-tuple-element.200), channel_id=1, source_target_pairs={{0,4},{1,5},{2,6},{3,7},{4,0},{5,1},{6,2},{7,3},{8,12},{9,13},{10,... | collective-permute-start | bytes 589832 | tf_op jit(solution)/shard_map/ppermute | solution.py:41
  139.1 23.4 %collective-permute-start.26 = (bf16[384,1024]{1,0:T(8,128)(2,1)S(1)}, bf16[384,1024]{1,0:T(8,128)(2,1)S(1)}, u32[]{:S(2)}, u32[]{:S(2)}) collective-permute-start(bf16[384,1024]{1,0:T(8,128)(2,1)S(1)} %get-tuple-element.147), channel_id=1, source_target_pairs={{0,2},{1,3},{2,0},{3,1},{4,6},{5,7},{6,4},{7,5},{8,10},{9,11},{10,... | collective-permute-start | bytes 2359304 | tf_op jit(solution)/shard_map/ppermute | solution.py:41
  160.9 3.4 %collective-permute-start.25 = (bf16[2,256,256]{2,1,0:T(8,128)(2,1)S(1)}, bf16[2,256,256]{2,1,0:T(8,128)(2,1)S(1)}, u32[]{:S(2)}, u32[]{:S(2)}) collective-permute-start(bf16[2,256,256]{2,1,0:T(8,128)(2,1)S(1)} %get-tuple-element.145), channel_id=1, source_target_pairs={{1,0},{2,1},{3,2},{4,3},{5,4},{6,5},{7,6},{8,7},{9,8},{10,9},{11,1... | collective-permute-start | bytes 786440 | tf_op jit(solution)/shard_map/ppermute | solution.py:36
  168.3 8.2 %collective-permute-start.27 = (bf16[768,1024]{1,0:T(8,128)(2,1)S(1)}, bf16[768,1024]{1,0:T(8,128)(2,1)S(1)}, u32[]{:S(2)}, u32[]{:S(2)}) collective-permute-start(bf16[768,1024]{1,0:T(8,128)(2,1)S(1)} %get-tuple-element.151), channel_id=1, source_target_pairs={{0,1},{1,0},{2,3},{3,2},{4,5},{5,4},{6,7},{7,6},{8,9},{9,8},{10,11... | collective-permute-start | bytes 4718600 | tf_op jit(solution)/shard_map/ppermute | solution.py:41
  177.1 20.6 %collective-permute-start.28 = (bf16[384,1024]{1,0:T(8,128)(2,1)S(1)}, bf16[384,1024]{1,0:T(8,128)(2,1)S(1)}, u32[]{:S(2)}, u32[]{:S(2)}) collective-permute-start(bf16[384,1024]{1,0:T(8,128)(2,1)S(1)} %get-tuple-element.152), channel_id=1, source_target_pairs={{0,2},{1,3},{2,0},{3,1},{4,6},{5,7},{6,4},{7,5},{8,10},{9,11},{10,... | collective-permute-start | bytes 2359304 | tf_op jit(solution)/shard_map/ppermute | solution.py:41
  179.8 4.6 %copy-start.2 = (bf16[768,1536]{1,0:T(8,128)(2,1)S(1)}, bf16[768,1536]{1,0:T(8,128)(2,1)}, u32[]{:S(2)}) copy-start(bf16[768,1536]{1,0:T(8,128)(2,1)} %enc_ref.3) | copy-start | bytes 7077892
  179.8 10.1 %collective-permute-start.31 = (bf16[96,1024]{1,0:T(8,128)(2,1)S(1)}, bf16[96,1024]{1,0:T(8,128)(2,1)S(1)}, u32[]{:S(2)}, u32[]{:S(2)}) collective-permute-start(bf16[96,1024]{1,0:T(8,128)(2,1)S(1)} %get-tuple-element.195), channel_id=1, source_target_pairs={{0,12},{1,13},{2,14},{3,15},{4,8},{5,9},{6,10},{7,11},{8,4},{9,5},... | collective-permute-start | bytes 589832 | tf_op jit(solution)/shard_map/ppermute | solution.py:41
  179.9 17.8 %collective-permute-start.30 = (bf16[96,1024]{1,0:T(8,128)(2,1)S(1)}, bf16[96,1024]{1,0:T(8,128)(2,1)S(1)}, u32[]{:S(2)}, u32[]{:S(2)}) collective-permute-start(bf16[96,1024]{1,0:T(8,128)(2,1)S(1)} %get-tuple-element.196), channel_id=1, source_target_pairs={{0,8},{1,9},{2,10},{3,11},{4,12},{5,13},{6,14},{7,15},{8,0},{9,1},... | collective-permute-start | bytes 589832 | tf_op jit(solution)/shard_map/ppermute | solution.py:41
  180.2 17.5 %collective-permute-start.29 = (bf16[96,1024]{1,0:T(8,128)(2,1)S(1)}, bf16[96,1024]{1,0:T(8,128)(2,1)S(1)}, u32[]{:S(2)}, u32[]{:S(2)}) collective-permute-start(bf16[96,1024]{1,0:T(8,128)(2,1)S(1)} %get-tuple-element.197), channel_id=1, source_target_pairs={{0,4},{1,5},{2,6},{3,7},{4,0},{5,1},{6,2},{7,3},{8,12},{9,13},{10,... | collective-permute-start | bytes 589832 | tf_op jit(solution)/shard_map/ppermute | solution.py:41
  197.7 4.8 %copy-start.4 = (bf16[768,1536]{1,0:T(8,128)(2,1)S(1)}, bf16[768,1536]{1,0:T(8,128)(2,1)}, u32[]{:S(2)}) copy-start(bf16[768,1536]{1,0:T(8,128)(2,1)} %cot_ref.3) | copy-start | bytes 7077892
  198.1 18.5 %collective-permute-start.32 = (bf16[96,1024]{1,0:T(8,128)(2,1)S(1)}, bf16[96,1024]{1,0:T(8,128)(2,1)S(1)}, u32[]{:S(2)}, u32[]{:S(2)}) collective-permute-start(bf16[96,1024]{1,0:T(8,128)(2,1)S(1)} %get-tuple-element.159), channel_id=1, source_target_pairs={{0,4},{1,5},{2,6},{3,7},{4,0},{5,1},{6,2},{7,3},{8,12},{9,13},{10,... | collective-permute-start | bytes 589832 | tf_op jit(solution)/shard_map/ppermute | solution.py:41
  198.2 18.4 %collective-permute-start.33 = (bf16[96,1024]{1,0:T(8,128)(2,1)S(1)}, bf16[96,1024]{1,0:T(8,128)(2,1)S(1)}, u32[]{:S(2)}, u32[]{:S(2)}) collective-permute-start(bf16[96,1024]{1,0:T(8,128)(2,1)S(1)} %get-tuple-element.160), channel_id=1, source_target_pairs={{0,8},{1,9},{2,10},{3,11},{4,12},{5,13},{6,14},{7,15},{8,0},{9,1},... | collective-permute-start | bytes 589832 | tf_op jit(solution)/shard_map/ppermute | solution.py:41
  200.9 15.7 %collective-permute-start.34 = (bf16[96,1024]{1,0:T(8,128)(2,1)S(1)}, bf16[96,1024]{1,0:T(8,128)(2,1)S(1)}, u32[]{:S(2)}, u32[]{:S(2)}) collective-permute-start(bf16[96,1024]{1,0:T(8,128)(2,1)S(1)} %get-tuple-element.161), channel_id=1, source_target_pairs={{0,12},{1,13},{2,14},{3,15},{4,8},{5,9},{6,10},{7,11},{8,4},{9,5},... | collective-permute-start | bytes 589832 | tf_op jit(solution)/shard_map/ppermute | solution.py:41

commit v3 on v2

--- a/solution.py
+++ b/solution.py
@@ -322,7 +322,7 @@
 def gradients(xt, ct, query_back, main, tail, returned, mixed, us):
     width = xt.shape[0]
     rows, cols = mixed.shape
-    tile = 256
+    tile = 384
     steps = width // tile
     whole = lambda a: pl.BlockSpec(a.shape, lambda i: (0,) * a.ndim)
     sd = jax.ShapeDtypeStruct

time: 218 us -> 217 us (level)
  no operation moved by 1% of the time
where the time goes in v3:
time: 217 us
  Pallas kernels  78.3 us (36%)
  starting transfers between devices  61.6 us (28%)
  waiting for transfers between devices  59 us (27%)
  matrix products  10.2 us (5%)
  local copies, waits for them, and re-layouts  3.21 us (1%)
  other arithmetic  2.94 us (1%)
    ppermute x31, waiting for transfers between devices, swapped(): return lax.ppermute(value, 'context', [(i, i ^ mask) for i in range(count)])  57.1 us
    ppermute x31, starting transfers between devices, swapped(): return lax.ppermute(value, 'context', [(i, i ^ mask) for i in range(count)])  54.9 us
    pallas_call x3, Pallas kernels, attention(): pl.pallas_call(attention_body, grid=(steps,), in_specs=[pl.BlockSpec(memo...  28.2 us
    pallas_call x1, Pallas kernels, finish_grad(): pl.pallas_call(body, in_specs=[pl.BlockSpec(memory_space=pltpu.SMEM), *(v...  14 us
    pallas_call x3, Pallas kernels, gradients(): pl.pallas_call(gradients_body, grid=(steps,), in_specs=[pl.BlockSpec((til...  10.7 us
    pallas_call x11, Pallas kernels, joined(): pl.pallas_call(body, in_specs=[pl.BlockSpec(memory_space=pltpu.HBM)] * le...  8.34 us
    pallas_call x1, Pallas kernels, prepare(): pl.pallas_call(body, grid=(frames // SPAN,), in_specs=[pl.BlockSpec(memor...  8.21 us
    dot_general x3, matrix products, project(): jnp.dot(x, whole[:, :3 * cols], preferred_element_type=F32).astype(BF16)  7.8 us
  transfers between devices with their start and end apart: 35, of which 10 were waited for; matrix products, arithmetic and copies ran while one was open for 6% of the time, Pallas kernels for 33%

profile of v3, /device:TPU:0, one launch (start us, length us, event | category | flops | bytes accessed | tf_op | source)
XLA Modules:
  0.0 217.1 jit_solution(11174429098023306120)
XLA Ops:
  0.6 1.6 shard_map.120.refs_0_
  2.2 5.1 %collective-permute-start.3 = (bf16[96,1024]{1,0:T(8,128)(2,1)}, bf16[96,1024]{1,0:T(8,128)(2,1)S(1)}, u32[]{:S(2)}, u32[]{:S(2)}) collective-permute-start(bf16[96,1024]{1,0:T(8,128)(2,1)} %shard_map.120.refs_0_), channel_id=1, source_target_pairs={{0,12},{1,13},{2,14},{3,15},{4,8},{5,9},{6,10},{7,11},{8,4},{9,5},... | collective-permute-start | bytes 589832 | tf_op jit(solution)/shard_map/ppermute | solution.py:41
  7.3 0.6 collective-permute-start.1
  8.0 2.1 slice.102
  10.0 2.2 %collective-permute-start = (bf16[256,1536]{1,0:T(8,128)(2,1)}, bf16[256,1536]{1,0:T(8,128)(2,1)}, u32[]{:S(2)}, u32[]{:S(2)}) collective-permute-start(bf16[256,1536]{1,0:T(8,128)(2,1)} %slice.102), channel_id=1, source_target_pairs={{0,1},{1,2},{2,3},{3,4},{4,5},{5,6},{6,7},{7,8},{8,9},{9,10},{10,1... | collective-permute-start | bytes 2359304 | tf_op jit(solution)/shard_map/ppermute | solution.py:36
  12.2 8.2 %shard_map.118 = (bf16[1024,1536]{1,0:T(8,128)(2,1)}, bf16[768,1536]{1,0:T(8,128)(2,1)}, bf16[1536,768]{1,0:T(8,128)(2,1)}, bf16[1536,768]{1,0:T(8,128)(2,1)}) custom-call(s32[1]{0:T(128)} %bitcast.me_ref, bf16[768,1536]{1,0:T(8,128)(2,1)} %enc_ref.3, bf16[768,1536]{1,0:T(8,128)(2,1)} %cot_ref.3), custom_call_target="tpu_custom_call" | custom-call | flops 2208000000 | bytes 1024 | tf_op jit(solution)/shard_map/pallas_call | solution.py:250
  20.5 3.7 %collective-permute-done.2.refs_2_ = bf16[96,1024]{1,0:T(8,128)(2,1)S(1)} collective-permute-done((bf16[96,1024]{1,0:T(8,128)(2,1)}, bf16[96,1024]{1,0:T(8,128)(2,1)S(1)}, u32[]{:S(2)}, u32[]{:S(2)}) %collective-permute-start.2) | collective-permute-done | bytes 196640 | tf_op jit(solution)/shard_map/ppermute | solution.py:41
  24.2 1.9 shard_map.121.refs_0_
  26.2 1.6 collective-permute-start.4
  27.9 3.7 %collective-permute-start.7 = (bf16[96,1024]{1,0:T(8,128)(2,1)S(1)}, bf16[96,1024]{1,0:T(8,128)(2,1)S(1)}, u32[]{:S(2)}, u32[]{:S(2)}) collective-permute-start(bf16[96,1024]{1,0:T(8,128)(2,1)S(1)} %shard_map.122.refs_0_), channel_id=1, source_target_pairs={{0,12},{1,13},{2,14},{3,15},{4,8},{5,9},{6,10},{7,11},{8,4},{9,5},... | collective-permute-start | bytes 589832 | tf_op jit(solution)/shard_map/ppermute | solution.py:41
  31.6 0.7 collective-permute-start.5
  32.3 5.3 %collective-permute-done.7.refs_3_ = bf16[96,1024]{1,0:T(8,128)(2,1)S(1)} collective-permute-done((bf16[96,1024]{1,0:T(8,128)(2,1)S(1)}, bf16[96,1024]{1,0:T(8,128)(2,1)S(1)}, u32[]{:S(2)}, u32[]{:S(2)}) %collective-permute-start.7) | collective-permute-done | bytes 196640 | tf_op jit(solution)/shard_map/ppermute | solution.py:41
  37.6 8.3 %collective-permute-done.6.refs_2_ = bf16[96,1024]{1,0:T(8,128)(2,1)S(1)} collective-permute-done((bf16[96,1024]{1,0:T(8,128)(2,1)S(1)}, bf16[96,1024]{1,0:T(8,128)(2,1)S(1)}, u32[]{:S(2)}, u32[]{:S(2)}) %collective-permute-start.6) | collective-permute-done | bytes 196640 | tf_op jit(solution)/shard_map/ppermute | solution.py:41
  45.9 1.0 shard_map.123.refs_0_
  47.0 0.9 copy-done.5
  48.6 2.1 shard_map.119
  50.8 3.0 %collective-permute-start.15 = (bf16[96,1024]{1,0:T(8,128)(2,1)S(1)}, bf16[96,1024]{1,0:T(8,128)(2,1)S(1)}, u32[]{:S(2)}, u32[]{:S(2)}) collective-permute-start(bf16[96,1024]{1,0:T(8,128)(2,1)S(1)} %shard_map.127.refs_0_), channel_id=1, source_target_pairs={{0,12},{1,13},{2,14},{3,15},{4,8},{5,9},{6,10},{7,11},{8,4},{9,5},... | collective-permute-start | bytes 589832 | tf_op jit(solution)/shard_map/ppermute | solution.py:41
  53.9 1.5 collective-permute-start.14
  55.4 0.5 collective-permute-start.13
  55.9 3.2 %collective-permute-start.12 = (bf16[384,1024]{1,0:T(8,128)(2,1)S(1)}, bf16[384,1024]{1,0:T(8,128)(2,1)S(1)}, u32[]{:S(2)}, u32[]{:S(2)}) collective-permute-start(bf16[384,1024]{1,0:T(8,128)(2,1)S(1)} %copy-done.6), channel_id=1, source_target_pairs={{0,2},{1,3},{2,0},{3,1},{4,6},{5,7},{6,4},{7,5},{8,10},{9,11},{10,... | collective-permute-start | bytes 2359304 | tf_op jit(solution)/shard_map/ppermute | solution.py:41
  59.0 1.9 shard_map.124.refs_3_
  60.9 2.6 %fusion.12.q_ref.k_ref.v_ref = bf16[1024,768]{1,0:T(8,128)(2,1)S(1)} fusion(bf16[1024,1536]{1,0:T(8,128)(2,1)S(1)} %shard_map.119, bf16[1536,1024]{1,0:T(8,128)(2,1)S(1)} %shard_map.124.refs_3_), kind=kOutput, calls=%fused_computation.8 | convolution fusion | flops 2416705536 | bytes 7077888 | tf_op jit(solution)/shard_map/dot_general | solution.py:560
  63.5 0.8 fusion.15.g_ref
  64.3 9.4 %shard_map.125 = (bf16[768,256]{1,0:T(8,128)(2,1)S(1)}, bf16[768,256]{1,0:T(8,128)(2,1)S(1)}, bf16[2,512,256]{2,1,0:T(8,128)(2,1)S(1)}, f32[2,256,256]{2,1,0:T(8,128)S(1)}, bf16[2,256,256]{2,1,0:T(8,128)(2,1)S(1)}) custom-call(s32[2]{0:T(128)S(1)} %pad_add_fusion.pos_ref, bf16[1024,768]{1,0:T(8,128)(2,1)S(1)} %fusion.12.q_ref.k_ref.v_ref, ...), custom_call_target="tpu_custom_call" | custom-call | flops 3243000064 | bytes 1024 | tf_op jit(solution)/shard_map/pallas_call | solution.py:163
  73.8 1.1 shard_map.128.refs_0_
  74.9 1.3 collective-permute-done.12.refs_1_
  76.4 1.5 collective-permute-start.10
  77.9 2.8 %collective-permute-start.17 = (bf16[384,1024]{1,0:T(8,128)(2,1)S(1)}, bf16[384,1024]{1,0:T(8,128)(2,1)S(1)}, u32[]{:S(2)}, u32[]{:S(2)}) collective-permute-start(bf16[384,1024]{1,0:T(8,128)(2,1)S(1)} %shard_map.128.refs_0_), channel_id=1, source_target_pairs={{0,2},{1,3},{2,0},{3,1},{4,6},{5,7},{6,4},{7,5},{8,10},{9,11},{10,... | collective-permute-start | bytes 2359304 | tf_op jit(solution)/shard_map/ppermute | solution.py:41
  80.7 3.6 %shard_map.126 = (bf16[768,1024]{1,0:T(8,128)(2,1)S(1)}, bf16[768,1024]{1,0:T(8,128)(2,1)S(1)}, bf16[768,768]{1,0:T(8,128)(2,1)S(1)}) custom-call(bf16[1536,768]{1,0:T(8,128)(2,1)S(1)} %copy-done, bf16[1536,768]{1,0:T(8,128)(2,1)S(1)} %copy-done.1, bf16[768,256]{1,0:T(8,128)(2,1)S(1)} %get-tuple-element.106.query_ref, ...), custom_call_target="tpu_custom_call" | custom-call | flops 1380000000 | bytes 1024 | tf_op jit(solution)/shard_map/pallas_call | solution.py:329
  84.3 6.7 %collective-permute-start.11 = (bf16[768,1024]{1,0:T(8,128)(2,1)S(1)}, bf16[768,1024]{1,0:T(8,128)(2,1)S(1)}, u32[]{:S(2)}, u32[]{:S(2)}) collective-permute-start(bf16[768,1024]{1,0:T(8,128)(2,1)S(1)} %get-tuple-element.112), channel_id=1, source_target_pairs={{0,1},{1,0},{2,3},{3,2},{4,5},{5,4},{6,7},{7,6},{8,9},{9,8},{10,11... | collective-permute-start | bytes 4718600 | tf_op jit(solution)/shard_map/ppermute | solution.py:41
  91.3 10.1 %collective-permute-done.17.refs_1_ = bf16[384,1024]{1,0:T(8,128)(2,1)S(1)} collective-permute-done((bf16[384,1024]{1,0:T(8,128)(2,1)S(1)}, bf16[384,1024]{1,0:T(8,128)(2,1)S(1)}, u32[]{:S(2)}, u32[]{:S(2)}) %collective-permute-start.17) | collective-permute-done | bytes 786464 | tf_op jit(solution)/shard_map/ppermute | solution.py:41
  101.3 0.8 fusion.16.g_ref
  102.1 2.6 %fusion.6.q_ref.k_ref.v_ref = bf16[1024,768]{1,0:T(8,128)(2,1)S(1)} fusion(bf16[1024,1536]{1,0:T(8,128)(2,1)S(1)} %shard_map.119, bf16[1536,1024]{1,0:T(8,128)(2,1)S(1)} %shard_map.130.refs_4_), kind=kOutput, calls=%fused_computation.6 | convolution fusion | flops 2416705536 | bytes 7077888 | tf_op jit(solution)/shard_map/dot_general | solution.py:560
  104.7 0.6 add_convert_fusion.2
  105.3 1.8 collective-permute-start.18
  107.1 9.4 %shard_map.131 = (bf16[768,256]{1,0:T(8,128)(2,1)S(1)}, bf16[768,256]{1,0:T(8,128)(2,1)S(1)}, bf16[2,512,256]{2,1,0:T(8,128)(2,1)S(1)}, f32[2,256,256]{2,1,0:T(8,128)S(1)}, bf16[2,256,256]{2,1,0:T(8,128)(2,1)S(1)}) custom-call(s32[2]{0:T(128)S(1)} %pad_add_fusion.pos_ref, bf16[1024,768]{1,0:T(8,128)(2,1)S(1)} %fusion.6.q_ref.k_ref.v_ref, ...), custom_call_target="tpu_custom_call" | custom-call | flops 3243000064 | bytes 1024 | tf_op jit(solution)/shard_map/pallas_call | solution.py:163
  116.7 1.5 collective-permute-start.22
  118.3 8.0 %collective-permute-done.18 = bf16[384,1024]{1,0:T(8,128)(2,1)S(1)} collective-permute-done((bf16[384,1024]{1,0:T(8,128)(2,1)S(1)}, bf16[384,1024]{1,0:T(8,128)(2,1)S(1)}, u32[]{:S(2)}, u32[]{:S(2)}) %collective-permute-start.18) | collective-permute-done | bytes 786464 | tf_op jit(solution)/shard_map/ppermute | solution.py:41
  126.2 3.6 %shard_map.132 = (bf16[768,1024]{1,0:T(8,128)(2,1)S(1)}, bf16[768,1024]{1,0:T(8,128)(2,1)S(1)}, bf16[768,768]{1,0:T(8,128)(2,1)S(1)}) custom-call(bf16[1536,768]{1,0:T(8,128)(2,1)S(1)} %copy-done, bf16[1536,768]{1,0:T(8,128)(2,1)S(1)} %copy-done.1, bf16[768,256]{1,0:T(8,128)(2,1)S(1)} %get-tuple-element.131.query_ref, ...), custom_call_target="tpu_custom_call" | custom-call | flops 1380000000 | bytes 1024 | tf_op jit(solution)/shard_map/pallas_call | solution.py:329
  129.8 0.6 collective-permute-start.23
  130.8 1.3 collective-permute-start.21
  132.1 1.6 collective-permute-start.20
  133.7 1.5 collective-permute-start.19
  135.5 2.6 %fusion.9.q_ref.k_ref.v_ref = bf16[1024,768]{1,0:T(8,128)(2,1)S(1)} fusion(bf16[1024,1536]{1,0:T(8,128)(2,1)S(1)} %shard_map.119, bf16[1536,1024]{1,0:T(8,128)(2,1)S(1)} %shard_map.134.refs_5_), kind=kOutput, calls=%fused_computation.7 | convolution fusion | flops 2416705536 | bytes 7077888 | tf_op jit(solution)/shard_map/dot_general | solution.py:560
  138.1 0.6 add_convert_fusion.1
  138.7 2.0 collective-permute-start.26
  140.7 0.8 fusion.17.g_ref
  141.5 9.6 %collective-permute-done.20.refs_2_ = bf16[96,1024]{1,0:T(8,128)(2,1)S(1)} collective-permute-done((bf16[96,1024]{1,0:T(8,128)(2,1)S(1)}, bf16[96,1024]{1,0:T(8,128)(2,1)S(1)}, u32[]{:S(2)}, u32[]{:S(2)}) %collective-permute-start.20) | collective-permute-done | bytes 196640 | tf_op jit(solution)/shard_map/ppermute | solution.py:41
  151.1 9.4 %shard_map.135 = (bf16[768,256]{1,0:T(8,128)(2,1)S(1)}, bf16[768,256]{1,0:T(8,128)(2,1)S(1)}, bf16[2,512,256]{2,1,0:T(8,128)(2,1)S(1)}, f32[2,256,256]{2,1,0:T(8,128)S(1)}, bf16[2,256,256]{2,1,0:T(8,128)(2,1)S(1)}) custom-call(s32[2]{0:T(128)S(1)} %pad_add_fusion.pos_ref, bf16[1024,768]{1,0:T(8,128)(2,1)S(1)} %fusion.9.q_ref.k_ref.v_ref, ...), custom_call_target="tpu_custom_call" | custom-call | flops 3243000064 | bytes 1024 | tf_op jit(solution)/shard_map/pallas_call | solution.py:163
  160.5 1.6 collective-permute-start.25
  162.1 1.9 collective-permute-done.25.returned_ref
  164.0 3.6 %shard_map.136 = (bf16[768,1024]{1,0:T(8,128)(2,1)S(1)}, bf16[768,1024]{1,0:T(8,128)(2,1)S(1)}, bf16[768,768]{1,0:T(8,128)(2,1)S(1)}) custom-call(bf16[1536,768]{1,0:T(8,128)(2,1)S(1)} %copy-done, bf16[1536,768]{1,0:T(8,128)(2,1)S(1)} %copy-done.1, bf16[768,256]{1,0:T(8,128)(2,1)S(1)} %get-tuple-element.142.query_ref, ...), custom_call_target="tpu_custom_call" | custom-call | flops 34500000 | bytes 1024 | tf_op jit(solution)/shard_map/pallas_call | solution.py:329
  167.5 5.1 %collective-permute-start.27 = (bf16[768,1024]{1,0:T(8,128)(2,1)S(1)}, bf16[768,1024]{1,0:T(8,128)(2,1)S(1)}, u32[]{:S(2)}, u32[]{:S(2)}) collective-permute-start(bf16[768,1024]{1,0:T(8,128)(2,1)S(1)} %get-tuple-element.151), channel_id=1, source_target_pairs={{0,1},{1,0},{2,3},{3,2},{4,5},{5,4},{6,7},{7,6},{8,9},{9,8},{10,11... | collective-permute-start | bytes 4718600 | tf_op jit(solution)/shard_map/ppermute | solution.py:41
  172.7 3.0 %collective-permute-done.27 = bf16[768,1024]{1,0:T(8,128)(2,1)S(1)} collective-permute-done((bf16[768,1024]{1,0:T(8,128)(2,1)S(1)}, bf16[768,1024]{1,0:T(8,128)(2,1)S(1)}, u32[]{:S(2)}, u32[]{:S(2)}) %collective-permute-start.27) | collective-permute-done | bytes 1572896 | tf_op jit(solution)/shard_map/ppermute | solution.py:41
  175.7 0.6 add_convert_fusion
  176.3 2.3 %collective-permute-start.28 = (bf16[384,1024]{1,0:T(8,128)(2,1)S(1)}, bf16[384,1024]{1,0:T(8,128)(2,1)S(1)}, u32[]{:S(2)}, u32[]{:S(2)}) collective-permute-start(bf16[384,1024]{1,0:T(8,128)(2,1)S(1)} %get-tuple-element.152), channel_id=1, source_target_pairs={{0,2},{1,3},{2,0},{3,1},{4,6},{5,7},{6,4},{7,5},{8,10},{9,11},{10,... | collective-permute-start | bytes 2359304 | tf_op jit(solution)/shard_map/ppermute | solution.py:41
  178.6 0.4 fusion.23
  179.4 4.1 %collective-permute-start.29 = (bf16[96,1024]{1,0:T(8,128)(2,1)S(1)}, bf16[96,1024]{1,0:T(8,128)(2,1)S(1)}, u32[]{:S(2)}, u32[]{:S(2)}) collective-permute-start(bf16[96,1024]{1,0:T(8,128)(2,1)S(1)} %get-tuple-element.197), channel_id=1, source_target_pairs={{0,4},{1,5},{2,6},{3,7},{4,0},{5,1},{6,2},{7,3},{8,12},{9,13},{10,... | collective-permute-start | bytes 589832 | tf_op jit(solution)/shard_map/ppermute | solution.py:41
  183.6 5.6 %shard_map.137 = bf16[768,1536]{1,0:T(8,128)(2,1)} custom-call(s32[1]{0:T(128)} %bitcast.me_ref, bf16[768,1536]{1,0:T(8,128)(2,1)S(1)} %copy-done.2, bf16[768,256]{1,0:T(8,128)(2,1)S(1)} %get-tuple-element.110.mixed_ref.refs_0_, bf16[768,256]{1,0:T(8,128)(2,1)S(1)} %get-tuple-element.135.mixed_ref.refs_1_, ...), custom_call_target="tpu_custom_call" | custom-call | flops 34500000 | bytes 1024 | tf_op jit(solution)/shard_map/pallas_call | solution.py:399
  189.3 7.7 %collective-permute-done.30.refs_6_ = bf16[96,1024]{1,0:T(8,128)(2,1)S(1)} collective-permute-done((bf16[96,1024]{1,0:T(8,128)(2,1)S(1)}, bf16[96,1024]{1,0:T(8,128)(2,1)S(1)}, u32[]{:S(2)}, u32[]{:S(2)}) %collective-permute-start.30) | collective-permute-done | bytes 196640 | tf_op jit(solution)/shard_map/ppermute | solution.py:41
  197.4 2.7 %collective-permute-start.33 = (bf16[96,1024]{1,0:T(8,128)(2,1)S(1)}, bf16[96,1024]{1,0:T(8,128)(2,1)S(1)}, u32[]{:S(2)}, u32[]{:S(2)}) collective-permute-start(bf16[96,1024]{1,0:T(8,128)(2,1)S(1)} %get-tuple-element.160), channel_id=1, source_target_pairs={{0,8},{1,9},{2,10},{3,11},{4,12},{5,13},{6,14},{7,15},{8,0},{9,1},... | collective-permute-start | bytes 589832 | tf_op jit(solution)/shard_map/ppermute | solution.py:41
  200.2 1.6 collective-permute-start.34
  201.8 14.0 %shard_map.138 = bf16[768,1536]{1,0:T(8,128)(2,1)} custom-call(s32[1]{0:T(128)} %bitcast.me_ref, bf16[768,1536]{1,0:T(8,128)(2,1)S(1)} %copy-done.2, bf16[768,1536]{1,0:T(8,128)(2,1)S(1)} %copy-done.4, bf16[768,768]{1,0:T(8,128)(2,1)S(1)} %get-tuple-element.163.refs_0_, bf16[768,768]{1,0:T(8,128)(2,1)S(1)} %get-tuple-element.164.refs_1_, ...), custom_call_target="tpu_custom_call" | custom-call | flops 4830000128 | bytes 1024 | tf_op jit(solution)/shard_map/pallas_call | solution.py:455
  215.9 1.2 shard_map.139
  (79 shorter events, 2.4 us)
Async XLA Ops:
  2.2 18.3 %collective-permute-start.3 = (bf16[96,1024]{1,0:T(8,128)(2,1)}, bf16[96,1024]{1,0:T(8,128)(2,1)S(1)}, u32[]{:S(2)}, u32[]{:S(2)}) collective-permute-start(bf16[96,1024]{1,0:T(8,128)(2,1)} %shard_map.120.refs_0_), channel_id=1, source_target_pairs={{0,12},{1,13},{2,14},{3,15},{4,8},{5,9},{6,10},{7,11},{8,4},{9,5},... | collective-permute-start | bytes 589832 | tf_op jit(solution)/shard_map/ppermute | solution.py:41
  7.3 16.9 %collective-permute-start.2 = (bf16[96,1024]{1,0:T(8,128)(2,1)}, bf16[96,1024]{1,0:T(8,128)(2,1)S(1)}, u32[]{:S(2)}, u32[]{:S(2)}) collective-permute-start(bf16[96,1024]{1,0:T(8,128)(2,1)} %shard_map.120.refs_0_), channel_id=1, source_target_pairs={{0,8},{1,9},{2,10},{3,11},{4,12},{5,13},{6,14},{7,15},{8,0},{9,1},... | collective-permute-start | bytes 589832 | tf_op jit(solution)/shard_map/ppermute | solution.py:41
  7.3 16.9 %collective-permute-start.1 = (bf16[96,1024]{1,0:T(8,128)(2,1)}, bf16[96,1024]{1,0:T(8,128)(2,1)S(1)}, u32[]{:S(2)}, u32[]{:S(2)}) collective-permute-start(bf16[96,1024]{1,0:T(8,128)(2,1)} %shard_map.120.refs_0_), channel_id=1, source_target_pairs={{0,4},{1,5},{2,6},{3,7},{4,0},{5,1},{6,2},{7,3},{8,12},{9,13},{10,... | collective-permute-start | bytes 589832 | tf_op jit(solution)/shard_map/ppermute | solution.py:41
  10.0 37.8 %collective-permute-start = (bf16[256,1536]{1,0:T(8,128)(2,1)}, bf16[256,1536]{1,0:T(8,128)(2,1)}, u32[]{:S(2)}, u32[]{:S(2)}) collective-permute-start(bf16[256,1536]{1,0:T(8,128)(2,1)} %slice.102), channel_id=1, source_target_pairs={{0,1},{1,2},{2,3},{3,4},{4,5},{5,6},{6,7},{7,8},{8,9},{9,10},{10,1... | collective-permute-start | bytes 2359304 | tf_op jit(solution)/shard_map/ppermute | solution.py:36
  12.2 12.0 %copy-start.7 = (bf16[96,1024]{1,0:T(8,128)(2,1)S(1)}, bf16[96,1024]{1,0:T(8,128)(2,1)}, u32[]{:S(2)}) copy-start(bf16[96,1024]{1,0:T(8,128)(2,1)} %shard_map.120.refs_0_) | copy-start | bytes 589828
  20.5 7.3 %copy-start.8 = (bf16[96,768]{1,0:T(8,128)(2,1)S(1)}, bf16[96,768]{1,0:T(8,128)(2,1)}, u32[]{:S(2)}) copy-start(bf16[96,768]{1,0:T(8,128)(2,1)} %refs_0_.3) | copy-start | bytes 442372
  20.5 7.3 %copy-start.9 = (bf16[96,768]{1,0:T(8,128)(2,1)S(1)}, bf16[96,768]{1,0:T(8,128)(2,1)}, u32[]{:S(2)}) copy-start(bf16[96,768]{1,0:T(8,128)(2,1)} %refs_1_.3) | copy-start | bytes 442372
  20.5 7.3 %copy-start.10 = (bf16[96,768]{1,0:T(8,128)(2,1)S(1)}, bf16[96,768]{1,0:T(8,128)(2,1)}, u32[]{:S(2)}) copy-start(bf16[96,768]{1,0:T(8,128)(2,1)} %refs_2_.3) | copy-start | bytes 442372
  20.5 7.3 %copy-start.12 = (bf16[96,768]{1,0:T(8,128)(2,1)S(1)}, bf16[96,768]{1,0:T(8,128)(2,1)}, u32[]{:S(2)}) copy-start(bf16[96,768]{1,0:T(8,128)(2,1)} %refs_3_.3) | copy-start | bytes 442372
  26.2 22.4 %copy-start.3 = (bf16[1024,1536]{1,0:T(8,128)(2,1)S(1)}, bf16[1024,1536]{1,0:T(8,128)(2,1)}, u32[]{:S(2)}) copy-start(bf16[1024,1536]{1,0:T(8,128)(2,1)} %get-tuple-element.95.x_ref) | copy-start | bytes 9437188
  26.2 21.7 %collective-permute-start.4 = (bf16[384,1024]{1,0:T(8,128)(2,1)}, bf16[384,1024]{1,0:T(8,128)(2,1)}, u32[]{:S(2)}, u32[]{:S(2)}) collective-permute-start(bf16[384,1024]{1,0:T(8,128)(2,1)} %shard_map.121.refs_0_), channel_id=1, source_target_pairs={{0,2},{1,3},{2,0},{3,1},{4,6},{5,7},{6,4},{7,5},{8,10},{9,11},{10,... | collective-permute-start | bytes 2359304 | tf_op jit(solution)/shard_map/ppermute | solution.py:41
  27.9 9.8 %collective-permute-start.7 = (bf16[96,1024]{1,0:T(8,128)(2,1)S(1)}, bf16[96,1024]{1,0:T(8,128)(2,1)S(1)}, u32[]{:S(2)}, u32[]{:S(2)}) collective-permute-start(bf16[96,1024]{1,0:T(8,128)(2,1)S(1)} %shard_map.122.refs_0_), channel_id=1, source_target_pairs={{0,12},{1,13},{2,14},{3,15},{4,8},{5,9},{6,10},{7,11},{8,4},{9,5},... | collective-permute-start | bytes 589832 | tf_op jit(solution)/shard_map/ppermute | solution.py:41
  31.6 14.3 %collective-permute-start.6 = (bf16[96,1024]{1,0:T(8,128)(2,1)S(1)}, bf16[96,1024]{1,0:T(8,128)(2,1)S(1)}, u32[]{:S(2)}, u32[]{:S(2)}) collective-permute-start(bf16[96,1024]{1,0:T(8,128)(2,1)S(1)} %shard_map.122.refs_0_), channel_id=1, source_target_pairs={{0,8},{1,9},{2,10},{3,11},{4,12},{5,13},{6,14},{7,15},{8,0},{9,1},... | collective-permute-start | bytes 589832 | tf_op jit(solution)/shard_map/ppermute | solution.py:41
  31.6 14.3 %collective-permute-start.5 = (bf16[96,1024]{1,0:T(8,128)(2,1)S(1)}, bf16[96,1024]{1,0:T(8,128)(2,1)S(1)}, u32[]{:S(2)}, u32[]{:S(2)}) collective-permute-start(bf16[96,1024]{1,0:T(8,128)(2,1)S(1)} %shard_map.122.refs_0_), channel_id=1, source_target_pairs={{0,4},{1,5},{2,6},{3,7},{4,0},{5,1},{6,2},{7,3},{8,12},{9,13},{10,... | collective-permute-start | bytes 589832 | tf_op jit(solution)/shard_map/ppermute | solution.py:41
  37.6 18.2 %collective-permute-start.8 = (bf16[384,1024]{1,0:T(8,128)(2,1)}, bf16[384,1024]{1,0:T(8,128)(2,1)}, u32[]{:S(2)}, u32[]{:S(2)}) collective-permute-start(bf16[384,1024]{1,0:T(8,128)(2,1)} %shard_map.121.refs_0_), channel_id=1, source_target_pairs={{0,1},{1,0},{2,3},{3,2},{4,5},{5,4},{6,7},{7,6},{8,9},{9,8},{10,11... | collective-permute-start | bytes 2359304 | tf_op jit(solution)/shard_map/ppermute | solution.py:41
  47.0 0.9 copy-start.5
  47.9 11.1 %collective-permute-start.9 = (bf16[384,1024]{1,0:T(8,128)(2,1)}, bf16[384,1024]{1,0:T(8,128)(2,1)}, u32[]{:S(2)}, u32[]{:S(2)}) collective-permute-start(bf16[384,1024]{1,0:T(8,128)(2,1)} %collective-permute-done.4.refs_1_), channel_id=1, source_target_pairs={{0,1},{1,0},{2,3},{3,2},{4,5},{5,4},{6,7},{7,6},{8,9},{9,8},{10,11... | collective-permute-start | bytes 2359304 | tf_op jit(solution)/shard_map/ppermute | solution.py:41
  48.6 2.1 copy-start.11
  48.6 2.1 copy-start.13
  50.7 5.1 %copy-start.6 = (bf16[384,1024]{1,0:T(8,128)(2,1)S(1)}, bf16[384,1024]{1,0:T(8,128)(2,1)}, u32[]{:S(2)}) copy-start(bf16[384,1024]{1,0:T(8,128)(2,1)} %copy-done.5) | copy-start | bytes 2359300
  50.8 22.9 %collective-permute-start.15 = (bf16[96,1024]{1,0:T(8,128)(2,1)S(1)}, bf16[96,1024]{1,0:T(8,128)(2,1)S(1)}, u32[]{:S(2)}, u32[]{:S(2)}) collective-permute-start(bf16[96,1024]{1,0:T(8,128)(2,1)S(1)} %shard_map.127.refs_0_), channel_id=1, source_target_pairs={{0,12},{1,13},{2,14},{3,15},{4,8},{5,9},{6,10},{7,11},{8,4},{9,5},... | collective-permute-start | bytes 589832 | tf_op jit(solution)/shard_map/ppermute | solution.py:41
  53.9 19.9 %collective-permute-start.14 = (bf16[96,1024]{1,0:T(8,128)(2,1)S(1)}, bf16[96,1024]{1,0:T(8,128)(2,1)S(1)}, u32[]{:S(2)}, u32[]{:S(2)}) collective-permute-start(bf16[96,1024]{1,0:T(8,128)(2,1)S(1)} %shard_map.127.refs_0_), channel_id=1, source_target_pairs={{0,8},{1,9},{2,10},{3,11},{4,12},{5,13},{6,14},{7,15},{8,0},{9,1},... | collective-permute-start | bytes 589832 | tf_op jit(solution)/shard_map/ppermute | solution.py:41
  55.4 18.4 %collective-permute-start.13 = (bf16[96,1024]{1,0:T(8,128)(2,1)S(1)}, bf16[96,1024]{1,0:T(8,128)(2,1)S(1)}, u32[]{:S(2)}, u32[]{:S(2)}) collective-permute-start(bf16[96,1024]{1,0:T(8,128)(2,1)S(1)} %shard_map.127.refs_0_), channel_id=1, source_target_pairs={{0,4},{1,5},{2,6},{3,7},{4,0},{5,1},{6,2},{7,3},{8,12},{9,13},{10,... | collective-permute-start | bytes 589832 | tf_op jit(solution)/shard_map/ppermute | solution.py:41
  55.9 20.3 %collective-permute-start.12 = (bf16[384,1024]{1,0:T(8,128)(2,1)S(1)}, bf16[384,1024]{1,0:T(8,128)(2,1)S(1)}, u32[]{:S(2)}, u32[]{:S(2)}) collective-permute-start(bf16[384,1024]{1,0:T(8,128)(2,1)S(1)} %copy-done.6), channel_id=1, source_target_pairs={{0,2},{1,3},{2,0},{3,1},{4,6},{5,7},{6,4},{7,5},{8,10},{9,11},{10,... | collective-permute-start | bytes 2359304 | tf_op jit(solution)/shard_map/ppermute | solution.py:41
  60.9 2.6 %copy-start.14 = (bf16[768,1536]{1,0:T(8,128)(2,1)S(1)}, bf16[768,1536]{1,0:T(8,128)(2,1)}, u32[]{:S(2)}) copy-start(bf16[768,1536]{1,0:T(8,128)(2,1)} %get-tuple-element.105) | copy-start | bytes 7077892
  73.8 6.9 %copy-start.1 = (bf16[1536,768]{1,0:T(8,128)(2,1)S(1)}, bf16[1536,768]{1,0:T(8,128)(2,1)}, u32[]{:S(2)}) copy-start(bf16[1536,768]{1,0:T(8,128)(2,1)} %get-tuple-element.94.ct_ref) | copy-start | bytes 7077892
  74.9 5.8 %copy-start = (bf16[1536,768]{1,0:T(8,128)(2,1)S(1)}, bf16[1536,768]{1,0:T(8,128)(2,1)}, u32[]{:S(2)}) copy-start(bf16[1536,768]{1,0:T(8,128)(2,1)} %get-tuple-element.93.xt_ref) | copy-start | bytes 7077892
  76.3 14.7 %collective-permute-start.16 = (bf16[768,1024]{1,0:T(8,128)(2,1)S(1)}, bf16[768,1024]{1,0:T(8,128)(2,1)S(1)}, u32[]{:S(2)}, u32[]{:S(2)}) collective-permute-start(bf16[768,1024]{1,0:T(8,128)(2,1)S(1)} %shard_map.129.refs_0_), channel_id=1, source_target_pairs={{0,1},{1,0},{2,3},{3,2},{4,5},{5,4},{6,7},{7,6},{8,9},{9,8},{10,11... | collective-permute-start | bytes 4718600 | tf_op jit(solution)/shard_map/ppermute | solution.py:41
  76.4 4.3 %collective-permute-start.10 = (bf16[2,256,256]{2,1,0:T(8,128)(2,1)S(1)}, bf16[2,256,256]{2,1,0:T(8,128)(2,1)S(1)}, u32[]{:S(2)}, u32[]{:S(2)}) collective-permute-start(bf16[2,256,256]{2,1,0:T(8,128)(2,1)S(1)} %get-tuple-element.109), channel_id=1, source_target_pairs={{1,0},{2,1},{3,2},{4,3},{5,4},{6,5},{7,6},{8,7},{9,8},{10,9},{11,1... | collective-permute-start | bytes 786440 | tf_op jit(solution)/shard_map/ppermute | solution.py:36
  77.9 23.4 %collective-permute-start.17 = (bf16[384,1024]{1,0:T(8,128)(2,1)S(1)}, bf16[384,1024]{1,0:T(8,128)(2,1)S(1)}, u32[]{:S(2)}, u32[]{:S(2)}) collective-permute-start(bf16[384,1024]{1,0:T(8,128)(2,1)S(1)} %shard_map.128.refs_0_), channel_id=1, source_target_pairs={{0,2},{1,3},{2,0},{3,1},{4,6},{5,7},{6,4},{7,5},{8,10},{9,11},{10,... | collective-permute-start | bytes 2359304 | tf_op jit(solution)/shard_map/ppermute | solution.py:41
  84.3 20.4 %collective-permute-start.11 = (bf16[768,1024]{1,0:T(8,128)(2,1)S(1)}, bf16[768,1024]{1,0:T(8,128)(2,1)S(1)}, u32[]{:S(2)}, u32[]{:S(2)}) collective-permute-start(bf16[768,1024]{1,0:T(8,128)(2,1)S(1)} %get-tuple-element.112), channel_id=1, source_target_pairs={{0,1},{1,0},{2,3},{3,2},{4,5},{5,4},{6,7},{7,6},{8,9},{9,8},{10,11... | collective-permute-start | bytes 4718600 | tf_op jit(solution)/shard_map/ppermute | solution.py:41
  105.3 20.9 %collective-permute-start.18 = (bf16[384,1024]{1,0:T(8,128)(2,1)S(1)}, bf16[384,1024]{1,0:T(8,128)(2,1)S(1)}, u32[]{:S(2)}, u32[]{:S(2)}) collective-permute-start(bf16[384,1024]{1,0:T(8,128)(2,1)S(1)} %get-tuple-element.126), channel_id=1, source_target_pairs={{0,2},{1,3},{2,0},{3,1},{4,6},{5,7},{6,4},{7,5},{8,10},{9,11},{10,... | collective-permute-start | bytes 2359304 | tf_op jit(solution)/shard_map/ppermute | solution.py:41
  116.7 18.6 %collective-permute-start.24 = (bf16[768,1024]{1,0:T(8,128)(2,1)S(1)}, bf16[768,1024]{1,0:T(8,128)(2,1)S(1)}, u32[]{:S(2)}, u32[]{:S(2)}) collective-permute-start(bf16[768,1024]{1,0:T(8,128)(2,1)S(1)} %shard_map.133.refs_0_), channel_id=1, source_target_pairs={{0,1},{1,0},{2,3},{3,2},{4,5},{5,4},{6,7},{7,6},{8,9},{9,8},{10,11... | collective-permute-start | bytes 4718600 | tf_op jit(solution)/shard_map/ppermute | solution.py:41
  116.7 9.5 %collective-permute-start.22 = (bf16[2,256,256]{2,1,0:T(8,128)(2,1)S(1)}, bf16[2,256,256]{2,1,0:T(8,128)(2,1)S(1)}, u32[]{:S(2)}, u32[]{:S(2)}) collective-permute-start(bf16[2,256,256]{2,1,0:T(8,128)(2,1)S(1)} %get-tuple-element.134), channel_id=1, source_target_pairs={{1,0},{2,1},{3,2},{4,3},{5,4},{6,5},{7,6},{8,7},{9,8},{10,9},{11,1... | collective-permute-start | bytes 786440 | tf_op jit(solution)/shard_map/ppermute | solution.py:36
  129.8 8.3 %collective-permute-start.23 = (bf16[768,1024]{1,0:T(8,128)(2,1)S(1)}, bf16[768,1024]{1,0:T(8,128)(2,1)S(1)}, u32[]{:S(2)}, u32[]{:S(2)}) collective-permute-start(bf16[768,1024]{1,0:T(8,128)(2,1)S(1)} %get-tuple-element.137), channel_id=1, source_target_pairs={{0,1},{1,0},{2,3},{3,2},{4,5},{5,4},{6,7},{7,6},{8,9},{9,8},{10,11... | collective-permute-start | bytes 4718600 | tf_op jit(solution)/shard_map/ppermute | solution.py:41
  130.8 10.7 %collective-permute-start.21 = (bf16[96,1024]{1,0:T(8,128)(2,1)S(1)}, bf16[96,1024]{1,0:T(8,128)(2,1)S(1)}, u32[]{:S(2)}, u32[]{:S(2)}) collective-permute-start(bf16[96,1024]{1,0:T(8,128)(2,1)S(1)} %get-tuple-element.198), channel_id=1, source_target_pairs={{0,12},{1,13},{2,14},{3,15},{4,8},{5,9},{6,10},{7,11},{8,4},{9,5},... | collective-permute-start | bytes 589832 | tf_op jit(solution)/shard_map/ppermute | solution.py:41
  132.1 19.1 %collective-permute-start.20 = (bf16[96,1024]{1,0:T(8,128)(2,1)S(1)}, bf16[96,1024]{1,0:T(8,128)(2,1)S(1)}, u32[]{:S(2)}, u32[]{:S(2)}) collective-permute-start(bf16[96,1024]{1,0:T(8,128)(2,1)S(1)} %get-tuple-element.199), channel_id=1, source_target_pairs={{0,8},{1,9},{2,10},{3,11},{4,12},{5,13},{6,14},{7,15},{8,0},{9,1},... | collective-permute-start | bytes 589832 | tf_op jit(solution)/shard_map/ppermute | solution.py:41
  133.7 17.4 %collective-permute-start.19 = (bf16[96,1024]{1,0:T(8,128)(2,1)S(1)}, bf16[96,1024]{1,0:T(8,128)(2,1)S(1)}, u32[]{:S(2)}, u32[]{:S(2)}) collective-permute-start(bf16[96,1024]{1,0:T(8,128)(2,1)S(1)} %get-tuple-element.200), channel_id=1, source_target_pairs={{0,4},{1,5},{2,6},{3,7},{4,0},{5,1},{6,2},{7,3},{8,12},{9,13},{10,... | collective-permute-start | bytes 589832 | tf_op jit(solution)/shard_map/ppermute | solution.py:41
  138.7 23.4 %collective-permute-start.26 = (bf16[384,1024]{1,0:T(8,128)(2,1)S(1)}, bf16[384,1024]{1,0:T(8,128)(2,1)S(1)}, u32[]{:S(2)}, u32[]{:S(2)}) collective-permute-start(bf16[384,1024]{1,0:T(8,128)(2,1)S(1)} %get-tuple-element.147), channel_id=1, source_target_pairs={{0,2},{1,3},{2,0},{3,1},{4,6},{5,7},{6,4},{7,5},{8,10},{9,11},{10,... | collective-permute-start | bytes 2359304 | tf_op jit(solution)/shard_map/ppermute | solution.py:41
  160.5 3.4 %collective-permute-start.25 = (bf16[2,256,256]{2,1,0:T(8,128)(2,1)S(1)}, bf16[2,256,256]{2,1,0:T(8,128)(2,1)S(1)}, u32[]{:S(2)}, u32[]{:S(2)}) collective-permute-start(bf16[2,256,256]{2,1,0:T(8,128)(2,1)S(1)} %get-tuple-element.145), channel_id=1, source_target_pairs={{1,0},{2,1},{3,2},{4,3},{5,4},{6,5},{7,6},{8,7},{9,8},{10,9},{11,1... | collective-permute-start | bytes 786440 | tf_op jit(solution)/shard_map/ppermute | solution.py:36
  167.5 8.2 %collective-permute-start.27 = (bf16[768,1024]{1,0:T(8,128)(2,1)S(1)}, bf16[768,1024]{1,0:T(8,128)(2,1)S(1)}, u32[]{:S(2)}, u32[]{:S(2)}) collective-permute-start(bf16[768,1024]{1,0:T(8,128)(2,1)S(1)} %get-tuple-element.151), channel_id=1, source_target_pairs={{0,1},{1,0},{2,3},{3,2},{4,5},{5,4},{6,7},{7,6},{8,9},{9,8},{10,11... | collective-permute-start | bytes 4718600 | tf_op jit(solution)/shard_map/ppermute | solution.py:41
  176.3 20.6 %collective-permute-start.28 = (bf16[384,1024]{1,0:T(8,128)(2,1)S(1)}, bf16[384,1024]{1,0:T(8,128)(2,1)S(1)}, u32[]{:S(2)}, u32[]{:S(2)}) collective-permute-start(bf16[384,1024]{1,0:T(8,128)(2,1)S(1)} %get-tuple-element.152), channel_id=1, source_target_pairs={{0,2},{1,3},{2,0},{3,1},{4,6},{5,7},{6,4},{7,5},{8,10},{9,11},{10,... | collective-permute-start | bytes 2359304 | tf_op jit(solution)/shard_map/ppermute | solution.py:41
  179.0 4.6 %copy-start.2 = (bf16[768,1536]{1,0:T(8,128)(2,1)S(1)}, bf16[768,1536]{1,0:T(8,128)(2,1)}, u32[]{:S(2)}) copy-start(bf16[768,1536]{1,0:T(8,128)(2,1)} %enc_ref.3) | copy-start | bytes 7077892
  179.1 10.1 %collective-permute-start.31 = (bf16[96,1024]{1,0:T(8,128)(2,1)S(1)}, bf16[96,1024]{1,0:T(8,128)(2,1)S(1)}, u32[]{:S(2)}, u32[]{:S(2)}) collective-permute-start(bf16[96,1024]{1,0:T(8,128)(2,1)S(1)} %get-tuple-element.195), channel_id=1, source_target_pairs={{0,12},{1,13},{2,14},{3,15},{4,8},{5,9},{6,10},{7,11},{8,4},{9,5},... | collective-permute-start | bytes 589832 | tf_op jit(solution)/shard_map/ppermute | solution.py:41
  179.2 17.8 %collective-permute-start.30 = (bf16[96,1024]{1,0:T(8,128)(2,1)S(1)}, bf16[96,1024]{1,0:T(8,128)(2,1)S(1)}, u32[]{:S(2)}, u32[]{:S(2)}) collective-permute-start(bf16[96,1024]{1,0:T(8,128)(2,1)S(1)} %get-tuple-element.196), channel_id=1, source_target_pairs={{0,8},{1,9},{2,10},{3,11},{4,12},{5,13},{6,14},{7,15},{8,0},{9,1},... | collective-permute-start | bytes 589832 | tf_op jit(solution)/shard_map/ppermute | solution.py:41
  179.4 17.5 %collective-permute-start.29 = (bf16[96,1024]{1,0:T(8,128)(2,1)S(1)}, bf16[96,1024]{1,0:T(8,128)(2,1)S(1)}, u32[]{:S(2)}, u32[]{:S(2)}) collective-permute-start(bf16[96,1024]{1,0:T(8,128)(2,1)S(1)} %get-tuple-element.197), channel_id=1, source_target_pairs={{0,4},{1,5},{2,6},{3,7},{4,0},{5,1},{6,2},{7,3},{8,12},{9,13},{10,... | collective-permute-start | bytes 589832 | tf_op jit(solution)/shard_map/ppermute | solution.py:41
  197.0 4.8 %copy-start.4 = (bf16[768,1536]{1,0:T(8,128)(2,1)S(1)}, bf16[768,1536]{1,0:T(8,128)(2,1)}, u32[]{:S(2)}) copy-start(bf16[768,1536]{1,0:T(8,128)(2,1)} %cot_ref.3) | copy-start | bytes 7077892
  197.4 18.5 %collective-permute-start.32 = (bf16[96,1024]{1,0:T(8,128)(2,1)S(1)}, bf16[96,1024]{1,0:T(8,128)(2,1)S(1)}, u32[]{:S(2)}, u32[]{:S(2)}) collective-permute-start(bf16[96,1024]{1,0:T(8,128)(2,1)S(1)} %get-tuple-element.159), channel_id=1, source_target_pairs={{0,4},{1,5},{2,6},{3,7},{4,0},{5,1},{6,2},{7,3},{8,12},{9,13},{10,... | collective-permute-start | bytes 589832 | tf_op jit(solution)/shard_map/ppermute | solution.py:41
  197.4 18.4 %collective-permute-start.33 = (bf16[96,1024]{1,0:T(8,128)(2,1)S(1)}, bf16[96,1024]{1,0:T(8,128)(2,1)S(1)}, u32[]{:S(2)}, u32[]{:S(2)}) collective-permute-start(bf16[96,1024]{1,0:T(8,128)(2,1)S(1)} %get-tuple-element.160), channel_id=1, source_target_pairs={{0,8},{1,9},{2,10},{3,11},{4,12},{5,13},{6,14},{7,15},{8,0},{9,1},... | collective-permute-start | bytes 589832 | tf_op jit(solution)/shard_map/ppermute | solution.py:41
  200.2 15.7 %collective-permute-start.34 = (bf16[96,1024]{1,0:T(8,128)(2,1)S(1)}, bf16[96,1024]{1,0:T(8,128)(2,1)S(1)}, u32[]{:S(2)}, u32[]{:S(2)}) collective-permute-start(bf16[96,1024]{1,0:T(8,128)(2,1)S(1)} %get-tuple-element.161), channel_id=1, source_target_pairs={{0,12},{1,13},{2,14},{3,15},{4,8},{5,9},{6,10},{7,11},{8,4},{9,5},... | collective-permute-start | bytes 589832 | tf_op jit(solution)/shard_map/ppermute | solution.py:41
